TPU v7x, 32 devices: a whole 2x2x4 slice. The times are simulated.
32 devices in a mesh: dp: 4 (over y, x), fsdp: 8 (over z, core).
Axes of the slice: x: 2, y: 2, z: 4, core: 2. Of those that a mesh axis runs over, the one named last changes fastest.
Arguments:
- step_count: int32 [1], replicated, may hold values from 2 to 20
- token_ids: int32 [2, 32, 512], replicated, may hold values from 0 to 50303
- segment_ids: int32 [2, 32, 512], P(None, ('dp', 'fsdp')), may hold values from 0 to 3, never falling along the last dimension, each value on 1 to 256 neighbouring positions
- loss_positions: int32 [2, 32, 32], P(None, ('dp', 'fsdp')), may hold values from 0 to 511
- label_ids: int32 [2, 32, 32], replicated, may hold values from 0 to 50303
- label_mask: int32 [2, 32, 32], replicated, may hold values 0 or 1
- embed_in: float32 [768, 50304], P(('dp', 'fsdp')), may hold values from -6 to 6
- embed_in_first: float32 [768, 50304], P(('dp', 'fsdp')), may hold values from -8.940697e-08 to 8.940697e-08
- embed_in_second: float32 [768, 50304], P(('dp', 'fsdp')), may hold values from 4.741832e-16 to 3.9120115e-15
- embed_out: float32 [50304, 768], P(('dp', 'fsdp')), may hold values from -0.4375 to 0.4375
- embed_out_first: float32 [50304, 768], P(('dp', 'fsdp')), may hold values from -7.1525574e-07 to 7.1525574e-07
- embed_out_second: float32 [50304, 768], P(('dp', 'fsdp')), may hold values from 3.0821906e-14 to 2.4894618e-13
- proj_in: float32 [768, 2304], P(('dp', 'fsdp')), may hold values from -0.21875 to 0.21875
- proj_in_first: float32 [768, 2304], P(('dp', 'fsdp')), may hold values from -7.1525574e-07 to 7.1525574e-07
- proj_in_second: float32 [768, 2304], P(('dp', 'fsdp')), may hold values from 3.0821906e-14 to 2.4894618e-13
- proj_up: float32 [768, 3072], P(('dp', 'fsdp')), may hold values from -0.21875 to 0.21875
- proj_up_first: float32 [768, 3072], P(('dp', 'fsdp')), may hold values from -7.1525574e-07 to 7.1525574e-07
- proj_up_second: float32 [768, 3072], P(('dp', 'fsdp')), may hold values from 3.0821906e-14 to 2.4894618e-13
- proj_mix: float32 [3840, 768], P(('dp', 'fsdp')), may hold values from -0.21875 to 0.21875
- proj_mix_first: float32 [3840, 768], P(('dp', 'fsdp')), may hold values from -7.1525574e-07 to 7.1525574e-07
- proj_mix_second: float32 [3840, 768], P(('dp', 'fsdp')), may hold values from 3.0821906e-14 to 2.4894618e-13
- vector_params: float32 [10752], P(('dp', 'fsdp')), may hold values from -1.5 to 1.5, as said below
- vector_first: float32 [10752], P(('dp', 'fsdp')), may hold values from -2.861023e-06 to 2.861023e-06
- vector_second: float32 [10752], P(('dp', 'fsdp')), may hold values from 4.9789236e-13 to 4.030557e-12
- basis_in: bfloat16 [768, 768], replicated, may hold values from -0.21875 to 0.21875
- basis_out: bfloat16 [3072, 3072], replicated, may hold values from -0.109375 to 0.109375
Outputs:
- new_embed_in: float32 [768, 50304], P(('dp', 'fsdp'))
- next_embed_in_first: float32 [768, 50304], P(('dp', 'fsdp'))
- next_embed_in_second: float32 [768, 50304], P(('dp', 'fsdp'))
- new_embed_out: float32 [50304, 768], P(('dp', 'fsdp'))
- next_embed_out_first: float32 [50304, 768], P(('dp', 'fsdp'))
- next_embed_out_second: float32 [50304, 768], P(('dp', 'fsdp'))
- new_proj_in: float32 [768, 2304], P(('dp', 'fsdp'))
- next_proj_in_first: float32 [768, 2304], P(('dp', 'fsdp'))
- next_proj_in_second: float32 [768, 2304], P(('dp', 'fsdp'))
- new_proj_up: float32 [768, 3072], P(('dp', 'fsdp'))
- next_proj_up_first: float32 [768, 3072], P(('dp', 'fsdp'))
- next_proj_up_second: float32 [768, 3072], P(('dp', 'fsdp'))
- new_proj_mix: float32 [3840, 768], P(('dp', 'fsdp'))
- next_proj_mix_first: float32 [3840, 768], P(('dp', 'fsdp'))
- next_proj_mix_second: float32 [3840, 768], P(('dp', 'fsdp'))
- new_vector_params: float32 [10752], P(('dp', 'fsdp'))
- next_vector_first: float32 [10752], P(('dp', 'fsdp'))
- next_vector_second: float32 [10752], P(('dp', 'fsdp'))
- loss_value: float32 [], replicated
- grad_norm: float32 [], replicated
- eigen_scales: float32 [768, 3072], P(('dp', 'fsdp'))
Inputs may be any that keep to these rules, and one draw needn't show every extreme that they name: `segment_ids`: within a row the ids never fall; a document has at most 256 positions. `vector_params`: the first 8448 entries are biases, the last 2304 are gains between 0.7 and 1.3.
All inputs are finite; a program needn't handle non-finite values.
Results may differ from a plain program's by a relative error of at most 0.0055.
The roundings to bfloat16 on the way count: a program that leaves them out, or rounds other values in their place, can miss the bound.
Values may be sent and summed in bfloat16 or wider, within the bound.
No kernel may reach another device: no remote copies, remote signals or barrier semaphores. Data moves between devices by JAX's collectives and lax.ppermute only.
A program may use at most 384 MiB of HBM per device.

v0:
```python
import math

import jax
import jax.numpy as jnp
from jax import lax
from jax.sharding import PartitionSpec as P

HEADS = 12
ROT = 16
DOCS = 4


half_type = jnp.bfloat16
full_type = jnp.float32
clip_limit = 0.01
decay_first = 0.9
decay_second = 0.95
adam_epsilon = 1e-08
weight_decay = 0.01
step_rates = (1.0, 0.07, 0.04, 0.04, 0.04, 0.3)
block_limit = 512


def merged(value, axis, join):
    pieces = jax.tree.map(lambda part: lax.all_gather(part, axis), value)
    head = jax.tree.map(lambda part: part[0], pieces)
    tail = jax.tree.map(lambda part: part[1:], pieces)
    total, _ = lax.scan(lambda total, piece: (join(total, piece), None), head, tail)
    return total


def split_vector(vector, width, hidden):
    lengths = (3 * width, hidden, width, width, width, width, width, width, width)
    pieces = []
    offset = 0
    for length in lengths:
        pieces.append(vector[offset : offset + length])
        offset = offset + length
    return pieces


def rotary_tables(row_length):
    halfway = ROT // 2
    inverse = 10000.0 ** (-2.0 * jnp.arange(halfway, dtype=full_type) / ROT)
    angles = jnp.arange(row_length, dtype=full_type)[:, None] * inverse[None, :]
    return (jnp.concatenate([jnp.cos(angles)] * 2, 1), jnp.concatenate([jnp.sin(angles)] * 2, 1))


def turn(values_in, cosine_table, sine_table, forward):
    halfway = ROT // 2
    rotated = values_in[..., :ROT]
    lower_half = rotated[..., :halfway]
    upper_half = rotated[..., halfway:]
    if forward:
        swapped = jnp.concatenate([-upper_half, lower_half], -1)
    else:
        swapped = jnp.concatenate([upper_half, -lower_half], -1)
    moved = rotated * cosine_table[:, None, :] + swapped * sine_table[:, None, :]
    return jnp.concatenate([moved, values_in[..., ROT:]], -1)


def normalize(inputs):
    centred = inputs - jnp.mean(inputs, 1, keepdims=True)
    inv_std = lax.rsqrt(jnp.mean(centred * centred, 1, keepdims=True) + 1e-05)
    return (centred * inv_std, inv_std)


def norm_back(grad_out, normed, inv_std):
    return inv_std * (
        grad_out
        - jnp.mean(grad_out, 1, keepdims=True)
        - normed * jnp.mean(grad_out * normed, 1, keepdims=True)
    )


def gelu_slope(inputs):
    return 0.5 * (1.0 + lax.erf(inputs * (1.0 / math.sqrt(2.0)))) + inputs * jnp.exp(
        -0.5 * inputs * inputs
    ) * (1.0 / math.sqrt(2.0 * math.pi))


def block_scores(queries, keys_all, segments, offset, block_rows):
    places = jnp.arange(keys_all.shape[0])
    query_places = offset + jnp.arange(block_rows)
    allowed = (places[None, :] <= query_places[:, None]) & (segments[None, :] == segments[:, None])
    score_scale = 1.0 / math.sqrt(queries.shape[2])
    scores = (
        jnp.einsum("qhd,khd->hqk", queries, keys_all, preferred_element_type=full_type)
        * score_scale
    )
    return (jnp.where(allowed[None], scores, -1e30), queries)


def attention_forward(queries, keys_all, values_all, segments):
    row_length, head_count, head_width = queries.shape
    block_rows = min(row_length, block_limit)

    def one_block(block_id):
        scores, unused = block_scores(
            queries, keys_all, segments, block_id * block_rows, block_rows
        )
        row_peak = jnp.max(scores, 2, keepdims=True)
        logsum = row_peak + jnp.log(jnp.sum(jnp.exp(scores - row_peak), 2, keepdims=True))
        weights_soft = jnp.exp(scores - logsum).astype(half_type)
        context = jnp.einsum(
            "hqk,khd->qhd", weights_soft, values_all, preferred_element_type=full_type
        )
        return (context, logsum[:, :, 0])

    context, logsum = lax.map(one_block, jnp.arange(row_length // block_rows))
    return (
        context.reshape(row_length, head_count * head_width),
        jnp.transpose(logsum, (1, 0, 2)).reshape(head_count, row_length),
    )


def attention_backward(queries, keys_all, values_all, segments, logsum, grad_context):
    row_length, head_count, head_width = queries.shape
    block_rows = min(row_length, block_limit)
    score_scale = 1.0 / math.sqrt(head_width)

    def one_block(carry, block_id):
        grad_keys, grad_values = carry
        offset = block_id * block_rows
        scores, query_block = block_scores(queries, keys_all, segments, offset, block_rows)
        weights_soft = jnp.exp(scores - logsum[:, :, None])
        grad_values = grad_values + jnp.einsum(
            "hqk,qhd->khd",
            weights_soft.astype(half_type),
            grad_context,
            preferred_element_type=full_type,
        )
        grad_weights = jnp.einsum(
            "qhd,khd->hqk", grad_context, values_all, preferred_element_type=full_type
        )
        grad_scores = (
            weights_soft * (grad_weights - jnp.sum(weights_soft * grad_weights, 2, keepdims=True))
        ).astype(half_type)
        grad_query = (
            jnp.einsum("hqk,khd->qhd", grad_scores, keys_all, preferred_element_type=full_type)
            * score_scale
        )
        grad_keys = (
            grad_keys
            + jnp.einsum("hqk,qhd->khd", grad_scores, query_block, preferred_element_type=full_type)
            * score_scale
        )
        return ((grad_keys, grad_values), grad_query)

    empty_grad = jnp.zeros((row_length, head_count, head_width), full_type)
    (grad_keys, grad_values), grad_queries = lax.scan(
        one_block, (empty_grad, empty_grad), jnp.arange(row_length // block_rows)
    )
    return (grad_queries.reshape(row_length, head_count, head_width), grad_keys, grad_values)


def layer_forward(embedded, segments, picks, weights_half, vector):
    proj_in, proj_up, proj_mix = weights_half
    row_length, width = embedded.shape
    hidden = proj_up.shape[1]
    (
        bias_in,
        bias_up,
        bias_mix,
        shift_first,
        shift_second,
        shift_last,
        gain_first,
        gain_second,
        gain_last,
    ) = split_vector(vector, width, hidden)
    normed, inv_std = normalize(embedded)
    first_in = (normed * gain_first + shift_first).astype(half_type)
    second_in = (normed * gain_second + shift_second).astype(half_type)
    mixed = (jnp.dot(first_in, proj_in, preferred_element_type=full_type) + bias_in).reshape(
        row_length, 3, HEADS, width // HEADS
    )
    cosine_table, sine_table = rotary_tables(row_length)
    queries = turn(mixed[:, 0], cosine_table, sine_table, True).astype(half_type)
    keys_all = turn(mixed[:, 1], cosine_table, sine_table, True).astype(half_type)
    values_all = mixed[:, 2].astype(half_type)
    context, logsum = attention_forward(queries, keys_all, values_all, segments)
    hidden_pre = jnp.dot(second_in, proj_up, preferred_element_type=full_type) + bias_up
    joined = jnp.concatenate(
        [context.astype(half_type), jax.nn.gelu(hidden_pre, approximate=False).astype(half_type)], 1
    )
    residual = embedded + jnp.dot(joined, proj_mix, preferred_element_type=full_type) + bias_mix
    normed_last, inv_last = normalize(residual)
    final = normed_last * gain_last + shift_last
    picked = jnp.take(final, picks, axis=0).astype(half_type)
    saved = (
        normed,
        inv_std,
        first_in,
        second_in,
        queries,
        keys_all,
        values_all,
        logsum,
        hidden_pre,
        joined,
        normed_last,
        inv_last,
    )
    return (picked, saved)


def layer_backward(grad_picked, picks, segments, weights_half, vector, saved):
    proj_in, proj_up, proj_mix = weights_half
    (
        normed,
        inv_std,
        first_in,
        second_in,
        queries,
        keys_all,
        values_all,
        logsum,
        hidden_pre,
        joined,
        normed_last,
        inv_last,
    ) = saved
    row_length, width = normed.shape
    hidden = proj_up.shape[1]
    pieces = split_vector(vector, width, hidden)
    gain_first, gain_second, gain_last = (pieces[6], pieces[7], pieces[8])
    grad_final = jnp.zeros((row_length, width), full_type).at[picks].add(grad_picked)
    grad_residual = norm_back(grad_final * gain_last, normed_last, inv_last)
    grad_branch = grad_residual.astype(half_type)
    grad_mix = jnp.einsum("sa,sb->ab", joined, grad_branch, preferred_element_type=full_type)
    grad_joined = jnp.einsum("sb,ab->sa", grad_branch, proj_mix, preferred_element_type=full_type)
    grad_context = (
        grad_joined[:, :width].astype(half_type).reshape(row_length, HEADS, width // HEADS)
    )
    grad_hidden = (grad_joined[:, width:] * gelu_slope(hidden_pre)).astype(half_type)
    grad_up = jnp.einsum("sa,sb->ab", second_in, grad_hidden, preferred_element_type=full_type)
    grad_second = jnp.einsum("sb,ab->sa", grad_hidden, proj_up, preferred_element_type=full_type)
    grad_queries, grad_keys, grad_values = attention_backward(
        queries, keys_all, values_all, segments, logsum, grad_context
    )
    cosine_table, sine_table = rotary_tables(row_length)
    grad_mixed = jnp.stack(
        [
            turn(grad_queries, cosine_table, sine_table, False),
            turn(grad_keys, cosine_table, sine_table, False),
            grad_values,
        ],
        1,
    )
    grad_mixed = grad_mixed.reshape(row_length, 3 * width).astype(half_type)
    grad_in = jnp.einsum("sa,sb->ab", first_in, grad_mixed, preferred_element_type=full_type)
    grad_first = jnp.einsum("sb,ab->sa", grad_mixed, proj_in, preferred_element_type=full_type)
    grad_embedded = grad_residual + norm_back(
        grad_first * gain_first + grad_second * gain_second, normed, inv_std
    )
    vector_grad = jnp.concatenate(
        [
            jnp.sum(grad_mixed.astype(full_type), 0),
            jnp.sum(grad_hidden.astype(full_type), 0),
            jnp.sum(grad_residual, 0),
            jnp.sum(grad_first, 0),
            jnp.sum(grad_second, 0),
            jnp.sum(grad_final, 0),
            jnp.sum(grad_first * normed, 0),
            jnp.sum(grad_second * normed, 0),
            jnp.sum(grad_final * normed_last, 0),
        ]
    )
    return (grad_embedded.astype(half_type), (grad_in, grad_up, grad_mix, vector_grad), grad_hidden)


def doc_scales(second_in, grad_hidden, segments, basis_in, basis_out, total):
    rot_in = jnp.dot(second_in, basis_in, preferred_element_type=full_type).astype(half_type)
    rot_out = jnp.dot(grad_hidden, basis_out, preferred_element_type=full_type).astype(half_type)
    docs = segments[None, :] == jnp.arange(DOCS)[:, None]
    masked = jnp.where(docs[:, :, None], rot_in[None], jnp.zeros((), half_type))
    blocks = (
        jnp.einsum("nsa,sb->nab", masked, rot_out, preferred_element_type=full_type) * total
    ).astype(half_type)
    arrived = lax.all_to_all(
        blocks, ("dp", "fsdp"), split_axis=1, concat_axis=0, tiled=True
    ).astype(full_type)
    return jnp.sum(arrived * arrived, 0)


def combine_partial(earlier, later):
    max_first, sum_first, label_first = earlier
    max_second, sum_second, label_second = later
    max_both = jnp.maximum(max_first, max_second)
    sum_both = sum_first * jnp.exp(max_first - max_both) + sum_second * jnp.exp(
        max_second - max_both
    )
    return (max_both, sum_both, label_first + label_second)


def head_step(micro_labels, micro_mask, picked, table_group, total):
    vocab_rows = table_group.shape[0]
    gathered = lax.all_gather(picked, ("dp", "fsdp"), axis=0, tiled=True)
    vocab_ids = lax.axis_index(("dp", "fsdp")) * vocab_rows + jnp.arange(vocab_rows)
    labels_flat = micro_labels.reshape(-1)
    mask_flat = micro_mask.reshape(-1).astype(full_type)
    logits = jnp.einsum("rd,vd->rv", gathered, table_group, preferred_element_type=full_type)
    matches = labels_flat[:, None] == vocab_ids[None, :]
    label_part = jnp.sum(jnp.where(matches, logits, 0.0), 1)
    local_max = jnp.max(logits, 1)
    local_sum = jnp.sum(jnp.exp(logits - local_max[:, None]), 1)
    maximum, exp_sums, label_logit = merged(
        (local_max, local_sum, label_part), ("dp", "fsdp"), combine_partial
    )
    logsum = maximum + jnp.log(exp_sums)
    loss_part = jnp.sum(mask_flat * (logsum - label_logit)) / total
    grad_logits = (
        (jnp.exp(logits - logsum[:, None]) - matches.astype(full_type))
        * (mask_flat / total)[:, None]
    ).astype(half_type)
    grad_table = jnp.einsum("rv,rd->vd", grad_logits, gathered, preferred_element_type=full_type)
    grad_picked = lax.psum_scatter(
        jnp.dot(grad_logits, table_group, preferred_element_type=full_type),
        ("dp", "fsdp"),
        scatter_dimension=0,
        tiled=True,
    )
    return (loss_part, grad_table, grad_picked)


def fetch_weights(shards):
    halves = tuple((shard_part.astype(half_type) for shard_part in shards))
    gathered = (
        lax.all_gather(halves[0], ("dp", "fsdp"), axis=0, tiled=True),
        lax.all_gather(halves[1], ("dp", "fsdp"), axis=0, tiled=True),
        lax.all_gather(halves[2], ("dp", "fsdp"), axis=0, tiled=True),
        lax.all_gather(halves[3], ("dp", "fsdp"), axis=0, tiled=True),
    )
    return ((gathered[0], gathered[1], gathered[2]), gathered[3].astype(full_type))


def reduce_grads(full_grads):
    return (
        lax.psum_scatter(full_grads[0], ("dp", "fsdp"), scatter_dimension=0, tiled=True),
        lax.psum_scatter(full_grads[1], ("dp", "fsdp"), scatter_dimension=0, tiled=True),
        lax.psum_scatter(full_grads[2], ("dp", "fsdp"), scatter_dimension=0, tiled=True),
        lax.psum_scatter(full_grads[3], ("dp", "fsdp"), scatter_dimension=0, tiled=True),
    )


def lookup(table_half, ids_all):
    batch_count = ids_all.shape[0]
    row_length = ids_all.shape[2]
    flat_ids = jnp.transpose(ids_all, (1, 0, 2)).reshape(-1)
    columns = jnp.take(table_half, flat_ids, axis=1)
    arrived = lax.all_to_all(columns, ("dp", "fsdp"), split_axis=1, concat_axis=0, tiled=True)
    return (arrived.T.reshape(batch_count, row_length, -1).astype(full_type), flat_ids)


def embed_back(grad_half, flat_ids, vocab):
    batch_count, row_length, width = grad_half.shape
    sending = grad_half.reshape(batch_count * row_length, width).T
    arrived = lax.all_to_all(sending, ("dp", "fsdp"), split_axis=0, concat_axis=1, tiled=True)
    return (
        jnp.zeros((arrived.shape[0], vocab), full_type)
        .at[:, flat_ids]
        .add(arrived.astype(full_type))
    )


def adam_update(weight, gradient, moment_one, moment_two, rate, step_value):
    next_one = decay_first * moment_one + (1.0 - decay_first) * gradient
    next_two = decay_second * moment_two + (1.0 - decay_second) * gradient * gradient
    fix_one = 1.0 - decay_first**step_value
    fix_two = 1.0 - decay_second**step_value
    update = next_one / fix_one / (jnp.sqrt(next_two / fix_two) + adam_epsilon)
    return [weight - rate * (update + weight_decay * weight), next_one, next_two]


def per_device(
    step_count,
    token_ids,
    segment_ids,
    loss_positions,
    label_ids,
    label_mask,
    embed_in,
    embed_in_first,
    embed_in_second,
    embed_out,
    embed_out_first,
    embed_out_second,
    proj_in,
    proj_in_first,
    proj_in_second,
    proj_up,
    proj_up_first,
    proj_up_second,
    proj_mix,
    proj_mix_first,
    proj_mix_second,
    vector_params,
    vector_first,
    vector_second,
    basis_in,
    basis_out,
):
    micro_count = token_ids.shape[0]
    total = jnp.maximum(jnp.sum(label_mask.astype(full_type)), 1.0)
    table_in = embed_in.astype(half_type)
    table_out = embed_out.astype(half_type)
    shards = (proj_in, proj_up, proj_mix, vector_params)
    vocab = embed_in.shape[1]
    loss_value = jnp.zeros((), full_type)
    scale_sum = jnp.zeros((embed_in.shape[0], proj_up.shape[1]), full_type)
    grad_out_table = jnp.zeros(table_out.shape, full_type)
    grad_in_table = jnp.zeros(embed_in.shape, full_type)
    layer_sums = tuple((jnp.zeros(shard_part.shape, full_type) for shard_part in shards))
    for micro_id in range(micro_count):
        weights_half, vector = fetch_weights(shards)
        embedded, flat_ids = lookup(table_in, token_ids[micro_id : micro_id + 1])
        run_embedded = embedded[0]
        segments = segment_ids[micro_id, 0]
        picks = loss_positions[micro_id, 0]
        picked, saved = layer_forward(run_embedded, segments, picks, weights_half, vector)
        loss_part, grad_table, grad_picked = head_step(
            label_ids[micro_id], label_mask[micro_id], picked, table_out, total
        )
        grad_embedded, layer_grads, grad_hidden = layer_backward(
            grad_picked, picks, segments, weights_half, vector, saved
        )
        scale_part = doc_scales(saved[3], grad_hidden, segments, basis_in, basis_out, total)
        loss_part, grad_table, layer_grads, grad_embedded, scale_part = (
            loss_part,
            grad_table,
            layer_grads,
            grad_embedded,
            scale_part,
        )
        loss_value = loss_value + loss_part
        grad_out_table = grad_out_table + grad_table
        scale_sum = scale_sum + scale_part
        grad_in_table = grad_in_table + embed_back(grad_embedded[None], flat_ids, vocab)
        reduced = reduce_grads(layer_grads)
        layer_sums = tuple(
            (held_sum + fresh_sum for held_sum, fresh_sum in zip(layer_sums, reduced))
        )
    eigen_scales = scale_sum / float(micro_count * lax.axis_size(("dp", "fsdp")) * DOCS)
    grads = (grad_in_table, grad_out_table) + tuple(layer_sums)
    squares = sum((jnp.sum(gradient * gradient) for gradient in grads))
    grad_norm = jnp.sqrt(lax.psum(squares, ("dp", "fsdp")))
    factor = jnp.minimum(1.0, clip_limit / (grad_norm + 1e-06))
    step_value = step_count[0].astype(full_type)
    weights = (embed_in, embed_out, proj_in, proj_up, proj_mix, vector_params)
    firsts = (
        embed_in_first,
        embed_out_first,
        proj_in_first,
        proj_up_first,
        proj_mix_first,
        vector_first,
    )
    seconds = (
        embed_in_second,
        embed_out_second,
        proj_in_second,
        proj_up_second,
        proj_mix_second,
        vector_second,
    )
    results = []
    for weight, gradient, moment_one, moment_two, rate in zip(
        weights, grads, firsts, seconds, step_rates
    ):
        results.extend(
            adam_update(weight, gradient * factor, moment_one, moment_two, rate, step_value)
        )
    return tuple(results) + (loss_value, grad_norm, eigen_scales)


def solution(mesh):
    in_specs = (
        P(),
        P(),
        P(None, ("dp", "fsdp"), None),
        P(None, ("dp", "fsdp"), None),
        P(),
        P(),
        P(("dp", "fsdp"), None),
        P(("dp", "fsdp"), None),
        P(("dp", "fsdp"), None),
        P(("dp", "fsdp"), None),
        P(("dp", "fsdp"), None),
        P(("dp", "fsdp"), None),
        P(("dp", "fsdp"), None),
        P(("dp", "fsdp"), None),
        P(("dp", "fsdp"), None),
        P(("dp", "fsdp"), None),
        P(("dp", "fsdp"), None),
        P(("dp", "fsdp"), None),
        P(("dp", "fsdp"), None),
        P(("dp", "fsdp"), None),
        P(("dp", "fsdp"), None),
        P(("dp", "fsdp")),
        P(("dp", "fsdp")),
        P(("dp", "fsdp")),
        P(),
        P(),
    )
    out_specs = (
        P(("dp", "fsdp"), None),
        P(("dp", "fsdp"), None),
        P(("dp", "fsdp"), None),
        P(("dp", "fsdp"), None),
        P(("dp", "fsdp"), None),
        P(("dp", "fsdp"), None),
        P(("dp", "fsdp"), None),
        P(("dp", "fsdp"), None),
        P(("dp", "fsdp"), None),
        P(("dp", "fsdp"), None),
        P(("dp", "fsdp"), None),
        P(("dp", "fsdp"), None),
        P(("dp", "fsdp"), None),
        P(("dp", "fsdp"), None),
        P(("dp", "fsdp"), None),
        P(("dp", "fsdp")),
        P(("dp", "fsdp")),
        P(("dp", "fsdp")),
        P(),
        P(),
        P(("dp", "fsdp"), None),
    )
    return jax.shard_map(
        per_device, mesh=mesh, in_specs=in_specs, out_specs=out_specs, check_vma=False
    )
```

profile of v0, /device:TPU:0, one launch (start us, length us, event | category | flops | bytes accessed | tf_op | source)
XLA Modules:
  0.0 2532.4 jit_solution(1309992860366846603)
XLA Ops:
  12.3 10.8 copy.210
  23.0 61.8 %gather_fusion.2 = bf16[16384,24]{1,0:T(8,128)(2,1)} fusion(bf16[24,50304]{0,1:T(8,128)(2,1)} %copy.210, s32[16384]{0:T(1024)S(1)} %fusion.106), kind=kCustom, calls=%fused_computation.2.clone | custom fusion | bytes 1638400 | tf_op jit(solution)/shard_map/jit(_take)/gather | solution.py:351
  84.9 11.5 broadcast_select_fusion
  100.9 7.3 all-to-all-start.2
  109.1 61.8 %gather_fusion = bf16[16384,24]{1,0:T(8,128)(2,1)} fusion(bf16[24,50304]{0,1:T(8,128)(2,1)} %copy.210, s32[16384]{0:T(1024)S(1)} %fusion.105), kind=kCustom, calls=%fused_computation.clone | custom fusion | bytes 1638400 | tf_op jit(solution)/shard_map/jit(_take)/gather | solution.py:351
  170.9 11.5 broadcast_select_fusion.1
  193.9 54.6 %all-reduce = bf16[10752]{0:T(1024)(128)(2,1)S(1)} all-reduce(bf16[10752]{0:T(1024)(128)(2,1)S(1)} %dynamic-update-slice), channel_id=1, replica_groups=mesh['dp'=4,'fsdp'=8] {'dp','fsdp'}, use_global_device_ids=true, to_apply=%add | all-reduce | flops 10752 | bytes 43008
  266.8 7.1 convolution_add_fusion.4
  341.0 31.4 %fusion.16 = (bf16[512,3072]{1,0:T(8,128)(2,1)}, bf16[512,3072]{1,0:T(8,128)(2,1)}, f32[512,3072]{1,0:T(8,128)}) fusion(f32[3072]{0:T(1024)S(1)} %slice.367, f32[512,3072]{1,0:T(8,128)S(1)} %fusion.169, bf16[512,768]{1,0:T(8,128)(2,1)S(1)} %copy-done.44, bf16[768,3072]{1,0:T(8,128)(2,1)S(1)} %copy-done.35), kind=kOutput, calls=%fused_computation.59 | convolution fusion | flops 2623537152 | bytes 24391680 | tf_op jit(solution)/shard_map/dot_general | solution.py:183
  372.4 7.5 fusion.164
  401.7 43.8 %all-gather.20.cloned.1.call-done = bf16[1024,768]{1,0:T(8,128)(2,1)} async-done(((bf16[32,768]{1,0:T(8,128)(2,1)}), bf16[1024,768]{1,0:T(8,128)(2,1)}) %all-gather.20.cloned.1.call-update) | async-done | bytes 1572880 | tf_op jit(solution)/shard_map/all_gather | solution.py:299
  445.5 7.6 fusion.167
  453.1 40.1 %all-gather.3 = f32[32768]{0:T(1024)S(1)} all-gather(f32[1024]{0:T(1024)S(1)} %get-tuple-element.499), channel_id=5, replica_groups=mesh['dp'=4,'fsdp'=8] {'dp','fsdp'}, dimensions={0}, use_global_device_ids=true | all-gather | bytes 135168 | tf_op jit(solution)/shard_map/all_gather | solution.py:25
  493.2 9.9 all-gather.18.cloned.1.call-done
  512.3 39.9 %all-gather.2 = f32[32768]{0:T(1024)S(1)} all-gather(f32[1024]{0:T(1024)S(1)} %get-tuple-element.314), channel_id=4, replica_groups=mesh['dp'=4,'fsdp'=8] {'dp','fsdp'}, dimensions={0}, use_global_device_ids=true | all-gather | bytes 135168 | tf_op jit(solution)/shard_map/all_gather | solution.py:25
  552.3 37.2 %all-gather = f32[32768]{0:T(1024)S(1)} all-gather(f32[1024]{0:T(1024)S(1)} %get-tuple-element.497), channel_id=2, replica_groups=mesh['dp'=4,'fsdp'=8] {'dp','fsdp'}, dimensions={0}, use_global_device_ids=true | all-gather | bytes 135168 | tf_op jit(solution)/shard_map/all_gather | solution.py:25
  589.4 38.5 %all-gather.1 = f32[32768]{0:T(1024)S(1)} all-gather(f32[1024]{0:T(1024)S(1)} %get-tuple-element.315), channel_id=3, replica_groups=mesh['dp'=4,'fsdp'=8] {'dp','fsdp'}, dimensions={0}, use_global_device_ids=true | all-gather | bytes 135168 | tf_op jit(solution)/shard_map/all_gather | solution.py:25
  628.0 37.2 %all-gather.4 = f32[32768]{0:T(1024)S(1)} all-gather(f32[1024]{0:T(1024)S(1)} %get-tuple-element.338), channel_id=6, replica_groups=mesh['dp'=4,'fsdp'=8] {'dp','fsdp'}, dimensions={0}, use_global_device_ids=true | all-gather | bytes 135168 | tf_op jit(solution)/shard_map/all_gather | solution.py:25
  665.1 38.5 %all-gather.5 = f32[32768]{0:T(1024)S(1)} all-gather(f32[1024]{0:T(1024)S(1)} %get-tuple-element.339), channel_id=7, replica_groups=mesh['dp'=4,'fsdp'=8] {'dp','fsdp'}, dimensions={0}, use_global_device_ids=true | all-gather | bytes 135168 | tf_op jit(solution)/shard_map/all_gather | solution.py:25
  705.7 48.8 %while.4 = (s32[]{:T(128)}, f32[1024]{0:T(1024)S(1)}, f32[1024]{0:T(1024)S(1)}, f32[1024]{0:T(1024)S(1)}, f32[31,1024]{1,0:T(8,128)}, /*index=5*/f32[31,1024]{1,0:T(8,128)S(1)}, f32[31,1024]{1,0:T(8,128)}, s32[]{:T(128)}) while((s32[]{:T(128)}, f32[1024]{0:T(1024)S(1)}, f32[1024]{0:T(1024)S(1)}, f32[1024]{0:T(1024)S(1)}, ...), condition=%wide.region_10.13_spmd, body=%wide.region_9.12_spmd.sunk | while | flops 7170 | bytes 61541 | solution.py:28
  756.0 9.5 fusion.141
  765.5 25.8 %while.5 = (s32[]{:T(128)}, f32[1024]{0:T(1024)S(1)}, f32[1024]{0:T(1024)S(1)}, f32[1024]{0:T(1024)S(1)}, f32[31,1024]{1,0:T(8,128)}, /*index=5*/f32[31,1024]{1,0:T(8,128)S(1)}, f32[31,1024]{1,0:T(8,128)S(1)}, s32[]{:T(128)}) while((s32[]{:T(128)}, f32[1024]{0:T(1024)S(1)}, f32[1024]{0:T(1024)S(1)}, f32[1024]{0:T(1024)S(1)}, ...), condition=%wide.region_29.32_spmd, body=%wide.region_28.31_spmd.sunk | while | flops 7170 | bytes 61541 | solution.py:28
  792.6 9.6 fusion.137
  808.1 56.2 %reduce-scatter.6.cloned.1.call-done = f32[32,768]{1,0:T(8,128)} async-done(((f32[1024,768]{1,0:T(8,128)}), f32[32,768]{1,0:T(8,128)}) %reduce-scatter.6.cloned.1.call-update) | async-done | bytes 98320 | tf_op jit(solution)/shard_map/reduce_scatter | solution.py:318
  869.8 101.0 %reduce-scatter.8.cloned.1.call-done = f32[32,768]{1,0:T(8,128)} async-done(((f32[1024,768]{1,0:T(8,128)}), f32[32,768]{1,0:T(8,128)}) %reduce-scatter.8.cloned.1.call-update) | async-done | bytes 98320 | tf_op jit(solution)/shard_map/reduce_scatter | solution.py:318
  990.0 8.9 convolution_bitcast_fusion.1
  998.9 9.9 multiply_reduce_fusion.4
  1008.9 7.5 multiply_convert_fusion.3
  1033.2 9.0 convolution_bitcast_fusion
  1042.1 9.9 multiply_reduce_fusion.3
  1052.1 7.2 multiply_convert_fusion.2
  1064.9 10.5 convert_reduce_fusion.1
  1099.7 16.0 fusion.49
  1125.3 15.0 multiply_convert_fusion
  1140.3 24.8 copy.238
  1194.4 15.1 fusion.48
  1209.4 10.3 multiply_convert_fusion.1
  1219.8 58.4 %copy.236 = bf16[4,768,3072]{2,0,1:T(4,128)(2,1)} copy(bf16[4,768,3072]{2,1,0:T(8,128)(2,1)S(1)} %multiply_convert_fusion.1) | data formatting | bytes 37748736 | tf_op jit(solution)/shard_map/convert_element_type | solution.py:280
  1278.2 379.9 %all-to-all-done.5 = bf16[4,768,3072]{2,0,1:T(4,128)(2,1)} async-done(((bf16[4,768,3072]{2,0,1:T(4,128)(2,1)}), bf16[4,768,3072]{2,0,1:T(4,128)(2,1)}, u32[]{:S(2)}, u32[]{:S(2)}) %all-to-all-start.5) | async-done | bytes 18874400 | tf_op jit(solution)/shard_map/all_to_all | solution.py:281
  1720.0 425.9 %all-reduce.1 = f32[10752]{0:T(1024)S(1)} all-reduce(f32[10752]{0:T(1024)S(1)} %add.586), channel_id=17, replica_groups=mesh['dp'=4,'fsdp'=8] {'dp','fsdp'}, use_global_device_ids=true, to_apply=%region_58.61.clone | all-reduce | flops 10752 | bytes 86016
  2150.9 10.0 copy.233
  2160.9 184.4 %scatter_custom_fusion.2 = f32[24,50304]{0,1:T(8,128)} fusion(s32[32768]{0:T(1024)} %bitcast.298, f32[32768,24]{1,0:T(8,128)} %copy.233, f32[]{:T(128)} %constant.90.clone.1), kind=kCustom, calls=%fused_computation.20 | custom fusion | flops 786432 | bytes 4829696 | tf_op jit(solution)/shard_map/add | solution.py:439
  2345.2 12.8 multiply_reduce_fusion.2
  2367.1 15.5 copy.234
  2382.6 38.6 %psum.7 = f32[]{:T(128)} all-reduce(f32[]{:T(128)S(6)} %add.544), channel_id=1, replica_groups=mesh['dp'=4,'fsdp'=8] {'dp','fsdp'}, use_global_device_ids=true, to_apply=%region_70.73 | all-reduce | flops 1 | bytes 8 | tf_op jit(solution)/shard_map/psum | solution.py:447
  2430.6 13.5 multiply_subtract_fusion
  2451.3 31.4 %multiply_reduce_fusion = f32[768,3072]{1,0:T(8,128)} fusion(bf16[4,768,3072]{2,0,1:T(4,128)(2,1)} %all-to-all-done.5), kind=kLoop, calls=%fused_computation.15 | loop fusion | flops 25952256 | bytes 28311552 | tf_op jit(solution)/shard_map/reduce_sum | solution.py:284
  2486.9 31.4 %multiply_reduce_fusion.1 = f32[768,3072]{1,0:T(8,128)} fusion(bf16[4,768,3072]{2,0,1:T(4,128)(2,1)} %all-to-all-done.4), kind=kLoop, calls=%fused_computation.17 | loop fusion | flops 25952256 | bytes 28311552 | tf_op jit(solution)/shard_map/reduce_sum | solution.py:284
  (885 shorter events, 424.2 us)
Async XLA Ops:
  7.2 796.9 %copy-start = (bf16[768,768]{1,0:T(8,128)(2,1)S(1)}, bf16[768,768]{1,0:T(8,128)(2,1)}, u32[]{:S(2)}) copy-start(bf16[768,768]{1,0:T(8,128)(2,1)} %param.58) | copy-start | bytes 3538948
  7.2 259.6 %all-gather.12.cloned.1.call-start = ((), (), s32[]{:S(2)}) async-start(), calls=%async_computation.11 | async-start | bytes 3649536 | tf_op jit(solution)/shard_map/all_gather | solution.py:330
  9.0 324.7 %all-gather.14.cloned.1.call-start = ((), (), s32[]{:S(2)}) async-start(), calls=%async_computation.12 | async-start | bytes 4866048 | tf_op jit(solution)/shard_map/all_gather | solution.py:331
  100.9 86.2 %all-to-all-start.2 = ((bf16[24,32,512]{2,0,1:T(8,128)(2,1)}), bf16[24,32,512]{2,0,1:T(8,128)(2,1)S(1)}, u32[]{:S(2)}, u32[]{:S(2)}) async-start(bf16[24,32,512]{2,0,1:T(8,128)(2,1)} %copy.222), calls=%async_computation.3 | async-start | bytes 1572864 | tf_op jit(solution)/shard_map/all_to_all | solution.py:352
  108.2 264.1 %all-gather.16.cloned.1.call-start = ((), (), s32[]{:S(2)}) async-start(), calls=%async_computation.13 | async-start | bytes 6082560 | tf_op jit(solution)/shard_map/all_gather | solution.py:332
  182.4 67.9 %copy-start.153 = (s32[2,1,512]{2,1,0:T(1,128)S(1)}, s32[2,1,512]{2,1,0:T(1,128)}, u32[]{:S(2)}) copy-start(s32[2,1,512]{2,1,0:T(1,128)} %param.36) | copy-start | bytes 12292
  187.1 65.8 %all-to-all-start = ((bf16[24,32,512]{2,0,1:T(8,128)(2,1)}), bf16[24,32,512]{2,0,1:T(8,128)(2,1)S(1)}, u32[]{:S(2)}, u32[]{:S(2)}) async-start(bf16[24,32,512]{2,0,1:T(8,128)(2,1)} %copy.211), calls=%async_computation | async-start | bytes 1572864 | tf_op jit(solution)/shard_map/all_to_all | solution.py:352
  193.0 252.6 %all-gather.20.cloned.1.call-start = ((), (), s32[]{:S(2)}) async-start(), calls=%async_computation.16 | async-start | bytes 1622016 | tf_op jit(solution)/shard_map/all_gather | solution.py:299
  249.1 89.2 %copy-start.101 = (f32[3072]{0:T(1024)}, f32[3072]{0:T(1024)S(1)}, u32[]{:S(2)}) copy-start(f32[3072]{0:T(1024)S(1)} %slice.367) | copy-start | bytes 36868
  253.0 33.0 %copy-start.99 = (f32[512]{0:T(512)}, f32[512]{0:T(512)S(1)}, u32[]{:S(2)}) copy-start(f32[512]{0:T(512)S(1)} %broadcast_multiply_fusion.5) | copy-start | bytes 6148
  260.8 25.2 copy-start.3
  266.8 66.9 %copy-start.24 = (bf16[512,768]{1,0:T(8,128)(2,1)}, bf16[512,768]{1,0:T(8,128)(2,1)S(1)}, u32[]{:S(2)}) copy-start(bf16[512,768]{1,0:T(8,128)(2,1)S(1)} %get-tuple-element.473) | copy-start | bytes 2359300
  341.0 31.4 %copy-start.40 = (bf16[512,768]{1,0:T(8,128)(2,1)S(1)}, bf16[512,768]{1,0:T(8,128)(2,1)}, u32[]{:S(2)}) copy-start(bf16[512,768]{1,0:T(8,128)(2,1)} %copy.215) | copy-start | bytes 2359300
  341.0 31.4 %copy-start.142 = (f32[768]{0:T(1024)S(1)}, f32[768]{0:T(1024)}, u32[]{:S(2)}) copy-start(f32[768]{0:T(1024)} %get-tuple-element.454) | copy-start | bytes 9220
  390.4 112.7 %all-gather.18.cloned.1.call-start = ((), (), s32[]{:S(2)}) async-start(), calls=%async_computation.14 | async-start | bytes 1622016 | tf_op jit(solution)/shard_map/all_gather | solution.py:299
  393.9 470.4 %reduce-scatter.6.cloned.1.call-start = ((), (), s32[]{:S(2)}) async-start(), calls=%async_computation.15 | async-start | bytes 3244032 | tf_op jit(solution)/shard_map/reduce_scatter | solution.py:318
  394.8 113.4 %copy-start.129 = (s32[1024]{0:T(1024)}, s32[1024]{0:T(1024)S(1)}, u32[]{:S(2)}) copy-start(s32[1024]{0:T(1024)S(1)} %eq.154) | copy-start | bytes 12292
  394.9 361.1 %copy-start.131 = (s32[1024]{0:T(1024)}, s32[1024]{0:T(1024)S(1)}, u32[]{:S(2)}) copy-start(s32[1024]{0:T(1024)S(1)} %eq.146) | copy-start | bytes 12292
  401.7 106.4 %copy-start.114 = (s32[1572]{0:T(1024)}, s32[1572]{0:T(1024)S(1)}, u32[]{:S(2)}) copy-start(s32[1572]{0:T(1024)S(1)} %iota_add_fusion) | copy-start | bytes 18868
  508.2 195.5 %slice-start.23 = ((f32[32768]{0:T(1024)}), f32[31744]{0:T(1024)S(1)}, s32[]{:S(2)}) async-start(f32[32768]{0:T(1024)} %copy-done.82), calls=%async_computation.44 | async-start | bytes 253952 | tf_op jit(solution)/shard_map/slice | solution.py:27
  765.5 205.3 %reduce-scatter.8.cloned.1.call-start = ((), (), s32[]{:S(2)}) async-start(), calls=%async_computation.17 | async-start | bytes 3244032 | tf_op jit(solution)/shard_map/reduce_scatter | solution.py:318
  805.8 167.4 %copy-start.117 = (f32[512]{0:T(512)S(1)}, f32[512]{0:T(512)}, u32[]{:S(2)}) copy-start(f32[512]{0:T(512)} %copy-done.116) | copy-start | bytes 6148
  805.8 167.4 %copy-start.119 = (f32[512]{0:T(512)S(1)}, f32[512]{0:T(512)}, u32[]{:S(2)}) copy-start(f32[512]{0:T(512)} %copy-done.118) | copy-start | bytes 6148
  1096.1 25.5 %all-to-all-start.3 = ((bf16[32,24,512]{2,1,0:T(8,128)(2,1)}), bf16[32,24,512]{2,1,0:T(8,128)(2,1)S(1)}, u32[]{:S(2)}, u32[]{:S(2)}) async-start(bf16[32,24,512]{2,1,0:T(8,128)(2,1)} %bitcast.276), calls=%async_computation.5 | async-start | bytes 1572864 | tf_op jit(solution)/shard_map/all_to_all | solution.py:359
  1121.6 43.5 %all-to-all-start.1 = ((bf16[32,24,512]{2,1,0:T(8,128)(2,1)}), bf16[32,24,512]{2,1,0:T(8,128)(2,1)}, u32[]{:S(2)}, u32[]{:S(2)}) async-start(bf16[32,24,512]{2,1,0:T(8,128)(2,1)} %bitcast.277), calls=%async_computation.2 | async-start | bytes 1572864 | tf_op jit(solution)/shard_map/all_to_all | solution.py:359
  1165.1 493.0 %all-to-all-start.5 = ((bf16[4,768,3072]{2,0,1:T(4,128)(2,1)}), bf16[4,768,3072]{2,0,1:T(4,128)(2,1)}, u32[]{:S(2)}, u32[]{:S(2)}) async-start(bf16[4,768,3072]{2,0,1:T(4,128)(2,1)} %copy.238), calls=%async_computation.7 | async-start | bytes 37748736 | tf_op jit(solution)/shard_map/all_to_all | solution.py:281
  1171.0 1188.4 %reduce-scatter.10.cloned.1.call-start = ((), (), s32[]{:S(2)}) async-start(), calls=%async_computation.18 | async-start | bytes 7299072 | tf_op jit(solution)/shard_map/reduce_scatter | solution.py:340
  1181.3 1180.3 %reduce-scatter.12.cloned.1.call-start = ((), (), s32[]{:S(2)}) async-start(), calls=%async_computation.19 | async-start | bytes 9732096 | tf_op jit(solution)/shard_map/reduce_scatter | solution.py:341
  1278.2 387.9 %copy-start.16 = (f32[512,768]{1,0:T(8,128)S(1)}, f32[512,768]{1,0:T(8,128)}, u32[]{:S(2)}) copy-start(f32[512,768]{1,0:T(8,128)} %copy-done.14) | copy-start | bytes 4718596
  1278.2 387.9 %copy-start.41 = (bf16[512,768]{1,0:T(8,128)(2,1)S(1)}, bf16[512,768]{1,0:T(8,128)(2,1)}, u32[]{:S(2)}) copy-start(bf16[512,768]{1,0:T(8,128)(2,1)} %copy.215) | copy-start | bytes 2359300
  1658.1 828.8 %all-to-all-start.4 = ((bf16[4,768,3072]{2,0,1:T(4,128)(2,1)}), bf16[4,768,3072]{2,0,1:T(4,128)(2,1)}, u32[]{:S(2)}, u32[]{:S(2)}) async-start(bf16[4,768,3072]{2,0,1:T(4,128)(2,1)} %copy.236), calls=%async_computation.6 | async-start | bytes 37748736 | tf_op jit(solution)/shard_map/all_to_all | solution.py:281
  1662.0 702.0 %reduce-scatter.14.cloned.1.call-start = ((), (), s32[]{:S(2)}) async-start(), calls=%async_computation.20 | async-start | bytes 12165120 | tf_op jit(solution)/shard_map/reduce_scatter | solution.py:342
  1688.7 21.4 copy-start.135
  1688.7 25.3 copy-start.134
  1688.7 26.6 %copy-start.155 = (f32[768]{0:T(1024)S(1)}, f32[768]{0:T(1024)}, u32[]{:S(2)}) copy-start(f32[768]{0:T(1024)} %get-tuple-element.329) | copy-start | bytes 9220
  1688.7 27.9 %copy-start.154 = (f32[768]{0:T(1024)S(1)}, f32[768]{0:T(1024)}, u32[]{:S(2)}) copy-start(f32[768]{0:T(1024)} %get-tuple-element.327) | copy-start | bytes 9220
  1688.7 29.2 %copy-start.133 = (f32[768]{0:T(1024)S(1)}, f32[768]{0:T(1024)}, u32[]{:S(2)}) copy-start(f32[768]{0:T(1024)} %get-tuple-element.320) | copy-start | bytes 9220
  2367.0 55.0 %copy-start.141 = (f32[336]{0:T(512)S(1)}, f32[336]{0:T(512)}, u32[]{:S(2)}) copy-start(f32[336]{0:T(512)} %param.55) | copy-start | bytes 4036
  2367.0 55.0 %copy-start.159 = (f32[336]{0:T(512)S(1)}, f32[336]{0:T(512)}, u32[]{:S(2)}) copy-start(f32[336]{0:T(512)} %param.57) | copy-start | bytes 4036
  2367.0 55.0 %copy-start.160 = (f32[336]{0:T(512)S(1)}, f32[336]{0:T(512)}, u32[]{:S(2)}) copy-start(f32[336]{0:T(512)} %param.56) | copy-start | bytes 4036
  2367.0 56.3 %copy-start.62 = (f32[120,768]{1,0:T(8,128)S(1)}, f32[120,768]{1,0:T(8,128)}, u32[]{:S(2)}) copy-start(f32[120,768]{1,0:T(8,128)} %param.52) | copy-start | bytes 1105924
  2367.0 56.3 %copy-start.63 = (f32[120,768]{1,0:T(8,128)S(1)}, f32[120,768]{1,0:T(8,128)}, u32[]{:S(2)}) copy-start(f32[120,768]{1,0:T(8,128)} %reduce-scatter.14.cloned.1.call-done) | copy-start | bytes 1105924
  2367.0 56.3 %copy-start.83 = (f32[120,768]{1,0:T(8,128)S(1)}, f32[120,768]{1,0:T(8,128)}, u32[]{:S(2)}) copy-start(f32[120,768]{1,0:T(8,128)} %param.54) | copy-start | bytes 1105924
  2367.0 58.7 %copy-start.66 = (f32[24,2304]{1,0:T(8,128)S(1)}, f32[24,2304]{1,0:T(8,128)}, u32[]{:S(2)}) copy-start(f32[24,2304]{1,0:T(8,128)} %reduce-scatter.10.cloned.1.call-done) | copy-start | bytes 663556
  2367.1 58.7 %copy-start.67 = (f32[24,2304]{1,0:T(8,128)S(1)}, f32[24,2304]{1,0:T(8,128)}, u32[]{:S(2)}) copy-start(f32[24,2304]{1,0:T(8,128)} %param.46) | copy-start | bytes 663556
  2367.1 58.6 %copy-start.93 = (f32[24,2304]{1,0:T(8,128)S(1)}, f32[24,2304]{1,0:T(8,128)}, u32[]{:S(2)}) copy-start(f32[24,2304]{1,0:T(8,128)} %param.48) | copy-start | bytes 663556
  2367.1 61.3 %copy-start.64 = (f32[24,3072]{1,0:T(8,128)S(1)}, f32[24,3072]{1,0:T(8,128)}, u32[]{:S(2)}) copy-start(f32[24,3072]{1,0:T(8,128)} %param.49) | copy-start | bytes 884740
  2367.1 61.3 %copy-start.65 = (f32[24,3072]{1,0:T(8,128)S(1)}, f32[24,3072]{1,0:T(8,128)}, u32[]{:S(2)}) copy-start(f32[24,3072]{1,0:T(8,128)} %reduce-scatter.12.cloned.1.call-done) | copy-start | bytes 884740
  (159 other events, 1127.7 us)
Sparse Core Ops, SparseCore 0:
  11.6 62.9 all-gather.11
  78.2 67.7 all-gather.13
  149.6 79.5 all-gather.15
  390.6 54.9 all-gather.19
  448.9 54.1 all-gather.17
  765.6 98.6 reduce-scatter.5
  870.3 100.4 reduce-scatter.7
  1181.4 236.1 reduce-scatter.9
  1424.5 185.2 reduce-scatter.11
  1678.1 281.1 reduce-scatter.13
where the time goes:
time: 2550 us; the launch traced here: 2530 us
  blocking collectives  750 us (29%)
  waiting for transfers between devices  593 us (23%)
  local copies, waits for them, and re-layouts  430 us (17%)
  other arithmetic  424 us (17%)
  matrix products  275 us (11%)
  starting transfers between devices  31.2 us (1%)
  between operations  26.6 us (1%)
    unnamed x2, blocking collectives  481 us
    all_to_all x2, waiting for transfers between devices, doc_scales(): lax.all_to_all(blocks, ('dp', 'fsdp'), split_axis=1, concat_axis=0, tiled...  380 us
    all_gather x6, blocking collectives, merged(): pieces = jax.tree.map(lambda part: lax.all_gather(part, axis), value)  231 us
    add x1, other arithmetic, per_device(): grad_in_table + embed_back(grad_embedded[None], flat_ids, vocab)  184 us
    reduce_scatter x2, waiting for transfers between devices, head_step(): lax.psum_scatter(jnp.dot(grad_logits, table_group, preferred_element_type...  157 us
    gather x2, local copies, waits for them, and re-layouts, lookup(): columns = jnp.take(table_half, flat_ids, axis=1)  124 us
    convert_element_type x2, local copies, waits for them, and re-layouts, doc_scales(): blocks = (jnp.einsum('nsa,sb->nab', masked, rot_out, preferred_element_ty...  83.1 us
    dynamic_slice x124, local copies, waits for them, and re-layouts, merged(): lax.scan(lambda total, piece: (join(total, piece), None), head, tail)  71.7 us
  transfers between devices with their start and end apart: 16, of which 6 were waited for; matrix products, arithmetic and copies ran while one was open for 34% of the time, Pallas kernels for 0%

commit v1 on v0

v1 whole, which is shorter than its diff:
```python
import math

import jax
import jax.numpy as jnp
from jax import lax
from jax.experimental import pallas as pl
from jax.experimental.pallas import tpu as pltpu
from jax.sharding import PartitionSpec as P

HEADS = 12
ROT = 16
DOCS = 4


half_type = jnp.bfloat16
full_type = jnp.float32
clip_limit = 0.01
decay_first = 0.9
decay_second = 0.95
adam_epsilon = 1e-08
weight_decay = 0.01
step_rates = (1.0, 0.07, 0.04, 0.04, 0.04, 0.3)


def split_vector(vector, width, hidden):
    lengths = (3 * width, hidden, width, width, width, width, width, width, width)
    pieces = []
    offset = 0
    for length in lengths:
        pieces.append(vector[offset : offset + length])
        offset = offset + length
    return pieces


def normalize(inputs):
    centred = inputs - jnp.mean(inputs, 1, keepdims=True)
    inv_std = lax.rsqrt(jnp.mean(centred * centred, 1, keepdims=True) + 1e-05)
    return (centred * inv_std, inv_std)


def norm_back(grad_out, normed, inv_std):
    return inv_std * (
        grad_out
        - jnp.mean(grad_out, 1, keepdims=True)
        - normed * jnp.mean(grad_out * normed, 1, keepdims=True)
    )


def gelu_slope(inputs):
    return 0.5 * (1.0 + lax.erf(inputs * (1.0 / math.sqrt(2.0)))) + inputs * jnp.exp(
        -0.5 * inputs * inputs
    ) * (1.0 / math.sqrt(2.0 * math.pi))


LANES = 128


def lane_pack(width):
    pad = 8
    while pad < width:
        pad *= 2
    return (pad, LANES // pad)


def copies_matrix(width, dtype):
    pad, _ = lane_pack(width)
    feature = lax.broadcasted_iota(jnp.int32, (width, LANES), 0)
    lane = lax.broadcasted_iota(jnp.int32, (width, LANES), 1)
    return jnp.where(lane % pad == feature, 1.0, 0.0).astype(dtype)


def gather_kernel(ids_ref, table_ref, out_ref, rows_ref, stage_ref):
    width, vocab = table_ref.shape
    tokens = ids_ref.shape[2]
    pad, groups = lane_pack(width)
    stride = tokens // groups

    @pl.when(pl.program_id(0) == 0)
    def _():
        spread = copies_matrix(width, half_type)
        step = 3 * LANES if vocab % (3 * LANES) == 0 else LANES

        def build(chunk, carry):
            start = pl.multiple_of(chunk * step, LANES)
            piece = table_ref[:, pl.ds(start, step)].astype(half_type)
            rows_ref[pl.ds(start, step), :] = lax.dot_general(
                piece, spread, (((0,), (0,)), ((), ())), preferred_element_type=full_type
            )
            return carry

        lax.fori_loop(0, vocab // step, build, 0)

    lane_group = lax.broadcasted_iota(jnp.int32, (1, LANES), 1) // pad
    unroll = 8

    def pick(block, carry):
        base = block * unroll
        for inner in range(unroll):
            row = None
            for group in range(groups):
                found = rows_ref[pl.ds(ids_ref[0, 0, group * stride + base + inner], 1), :]
                row = found if row is None else jnp.where(lane_group == group, found, row)
            stage_ref[pl.ds(base + inner, 1), :] = row
        return carry

    lax.fori_loop(0, stride // unroll, pick, 0)
    turned = jnp.transpose(stage_ref[...])
    for group in range(groups):
        out_ref[0, :, group * stride : (group + 1) * stride] = turned[
            group * pad : group * pad + width, :
        ].astype(half_type)


def gather_features(table, ids):
    width, vocab = table.shape
    count, _, tokens = ids.shape
    _, groups = lane_pack(width)
    return pl.pallas_call(
        gather_kernel,
        out_shape=jax.ShapeDtypeStruct((count, width, tokens), half_type),
        grid=(count,),
        in_specs=[
            pl.BlockSpec((1, 1, tokens), lambda i: (i, 0, 0), memory_space=pltpu.SMEM),
            pl.BlockSpec((width, vocab), lambda i: (0, 0), pipeline_mode=pl.Buffered(1)),
        ],
        out_specs=pl.BlockSpec((1, width, tokens), lambda i: (i, 0, 0)),
        scratch_shapes=[
            pltpu.VMEM((vocab, LANES), full_type),
            pltpu.VMEM((tokens // groups, LANES), full_type),
        ],
        compiler_params=pltpu.CompilerParams(
            dimension_semantics=("arbitrary",), vmem_limit_bytes=44 * 1024 * 1024
        ),
    )(ids, table)


def quarter(vocab, groups):
    return -(-vocab // (groups * LANES)) * LANES


def scatter_kernel(places_ref, grad_ref, out_ref, square_ref, mask_ref, stage_ref, *sums):
    width, vocab = out_ref.shape
    runs, _, tokens = places_ref.shape
    pad, groups = lane_pack(width)
    shift = groups.bit_length() - 1
    span = quarter(vocab, groups)

    @pl.when(pl.program_id(0) == 0)
    def _():
        lane_group = lax.broadcasted_iota(jnp.int32, mask_ref.shape, 1) // pad
        mask_ref[...] = jnp.where(
            lane_group == lax.broadcasted_iota(jnp.int32, mask_ref.shape, 0), 1.0, 0.0
        )

        def clear(block, carry):
            start = pl.multiple_of(block * LANES, LANES)
            for total in sums:
                total[pl.ds(start, LANES), :] = jnp.zeros((LANES, LANES), full_type)
            return carry

        lax.fori_loop(0, span // LANES, clear, 0)

    spread = copies_matrix(width, half_type)
    for run in range(runs):
        stage_ref[run] = lax.dot_general(
            grad_ref[run], spread, (((0,), (0,)), ((), ())), preferred_element_type=full_type
        )
    unroll = 4

    def add(block, carry):
        base = block * unroll
        for inner in range(unroll):
            for run in range(runs):
                place = places_ref[run, 0, base + inner]
                row = pl.ds(place >> shift, 1)
                group = pl.ds(place & (groups - 1), 1)
                sums[run][row, :] = (
                    sums[run][row, :] + stage_ref[run, pl.ds(base + inner, 1), :] * mask_ref[group, :]
                )
        return carry

    lax.fori_loop(0, tokens // unroll, add, 0)

    @pl.when(pl.program_id(0) == pl.num_programs(0) - 1)
    def _():
        def finish(block, squares):
            start = pl.multiple_of(block * LANES, LANES)
            whole = sums[0][pl.ds(start, LANES), :]
            for total in sums[1:]:
                whole = whole + total[pl.ds(start, LANES), :]
            turned = jnp.transpose(whole)
            for group in range(groups):
                column = pl.multiple_of(group * span + start, LANES)

                @pl.when(column < vocab)
                def _():
                    out_ref[:, pl.ds(column, LANES)] = turned[group * pad : group * pad + width, :]

            return squares + jnp.sum((whole * whole).reshape(LANES // 8, 8, LANES), 0)

        square_ref[...] = lax.fori_loop(0, span // LANES, finish, jnp.zeros((8, LANES), full_type))


def scatter_features(grads, places, vocab):
    count, width, tokens = grads.shape
    pad, groups = lane_pack(width)
    runs = 4
    return pl.pallas_call(
        scatter_kernel,
        out_shape=(
            jax.ShapeDtypeStruct((width, vocab), full_type),
            jax.ShapeDtypeStruct((8, LANES), full_type),
        ),
        grid=(count // runs,),
        in_specs=[
            pl.BlockSpec((runs, 1, tokens), lambda i: (i, 0, 0), memory_space=pltpu.SMEM),
            pl.BlockSpec((runs, width, tokens), lambda i: (i, 0, 0)),
        ],
        out_specs=(
            pl.BlockSpec((width, vocab), lambda i: (0, 0)),
            pl.BlockSpec((8, LANES), lambda i: (0, 0)),
        ),
        scratch_shapes=[
            pltpu.VMEM((max(8, groups), LANES), full_type),
            pltpu.VMEM((runs, tokens, LANES), full_type),
        ]
        + [pltpu.VMEM((quarter(vocab, groups), LANES), full_type) for _ in range(runs)],
        compiler_params=pltpu.CompilerParams(
            dimension_semantics=("arbitrary",), vmem_limit_bytes=52 * 1024 * 1024
        ),
    )(places, grads)


def scatter_places(ids, width, vocab):
    _, groups = lane_pack(width)
    span = quarter(vocab, groups)
    return (ids % span) * groups + ids // span


def turn_tables(row_length, head_width):
    halfway = ROT // 2
    dims = jnp.arange(LANES) % head_width
    inverse = 10000.0 ** (-2.0 * (dims % halfway).astype(full_type) / ROT)
    angles = jnp.arange(row_length, dtype=full_type)[:, None] * inverse[None, :]
    cosine = jnp.where(dims < ROT, jnp.cos(angles), 1.0)
    above = jnp.where(dims < halfway, -jnp.sin(angles), 0.0)
    below = jnp.where((dims >= halfway) & (dims < ROT), jnp.sin(angles), 0.0)
    return jnp.stack([cosine, above, below], 0)


def turned(values_in, tables_ref, forward):
    halfway = ROT // 2
    higher = pltpu.roll(values_in, LANES - halfway, 1) * tables_ref[1]
    lower = pltpu.roll(values_in, halfway, 1) * tables_ref[2]
    straight = values_in * tables_ref[0]
    return straight + (higher + lower) if forward else straight - (higher + lower)


def dot_of(left, right, dims):
    return lax.dot_general(left, right, (dims, ((), ())), preferred_element_type=full_type)


def key_window(block, block_rows):
    return (block + 1) * block_rows


def allowed_block(row_ref, column_ref, block, block_rows):
    reach = key_window(block, block_rows)
    start = block * block_rows
    key_place = lax.broadcasted_iota(jnp.int32, (reach, block_rows), 0)
    query_place = start + lax.broadcasted_iota(jnp.int32, (reach, block_rows), 1)
    same = column_ref[0, :reach, :] == row_ref[0, :, start : start + block_rows]
    return (key_place <= query_place) & same


def forward_kernel(
    query_in, key_in, value_in, tables_ref, row_ref, column_ref, context_ref, query_ref, key_ref, value_ref, logsum_ref
):
    row_length = query_in.shape[0]
    head_width = LANES // 2
    block_rows = row_length // 2
    scale = 1.0 / math.sqrt(head_width)
    query_ref[...] = turned(query_in[...], tables_ref, True).astype(half_type)
    key_ref[...] = turned(key_in[...], tables_ref, True).astype(half_type)
    value_ref[...] = value_in[...].astype(half_type)
    for block in range(2):
        start = block * block_rows
        reach = key_window(block, block_rows)
        allowed = allowed_block(row_ref, column_ref, block, block_rows)
        for head in range(2):
            lanes = slice(head * head_width, (head + 1) * head_width)
            scores = dot_of(key_ref[:reach, lanes], query_ref[start : start + block_rows, lanes], ((1,), (1,)))
            scores = jnp.where(allowed, scores * scale, -1e30)
            peak = jnp.max(scores, 0, keepdims=True)
            powers = jnp.exp(scores - peak)
            total = jnp.sum(powers, 0, keepdims=True)
            logsum_ref[0, 0, head : head + 1, start : start + block_rows] = peak + jnp.log(total)
            weights_soft = (powers * (1.0 / total)).astype(half_type)
            context_ref[start : start + block_rows, lanes] = dot_of(
                weights_soft, value_ref[:reach, lanes], ((0,), (0,))
            ).astype(half_type)


def attention_specs(row_length, pairs):
    def part(offset):
        return pl.BlockSpec((row_length, LANES), lambda m, h: (m, offset * pairs + h))

    tables = pl.BlockSpec((3, row_length, LANES), lambda m, h: (0, 0, 0))
    row = pl.BlockSpec((1, 1, row_length), lambda m, h: (m, 0, 0))
    column = pl.BlockSpec((1, row_length, 1), lambda m, h: (m, 0, 0))
    logsum = pl.BlockSpec((1, 1, 2, row_length), lambda m, h: (m, h, 0, 0))
    return (part, tables, row, column, logsum)


def attention_forward(mixed, tables, segments):
    micro_count, row_length = segments.shape
    tokens = mixed.shape[0]
    width = mixed.shape[1] // 3
    pairs = width // LANES
    part, tables_spec, row, column, logsum = attention_specs(row_length, pairs)
    flat = jax.ShapeDtypeStruct((tokens, width), half_type)
    return pl.pallas_call(
        forward_kernel,
        out_shape=(flat, flat, flat, flat, jax.ShapeDtypeStruct((micro_count, pairs, 2, row_length), full_type)),
        grid=(micro_count, pairs),
        in_specs=[part(0), part(1), part(2), tables_spec, row, column],
        out_specs=(part(0), part(0), part(0), part(0), logsum),
        compiler_params=pltpu.CompilerParams(
            dimension_semantics=("arbitrary", "arbitrary"), vmem_limit_bytes=40 * 1024 * 1024
        ),
    )(mixed, mixed, mixed, tables, segments[:, None, :], segments[:, :, None])


def backward_kernel(
    query_ref, key_ref, value_ref, grad_ref, tables_ref, row_ref, column_ref, logsum_ref, out_ref, query_sum, key_sum, value_sum
):
    row_length = query_ref.shape[0]
    head_width = LANES // 2
    block_rows = row_length // 2
    scale = 1.0 / math.sqrt(head_width)
    for block in reversed(range(2)):
        start = block * block_rows
        reach = key_window(block, block_rows)
        rows = slice(start, start + block_rows)
        allowed = allowed_block(row_ref, column_ref, block, block_rows)
        for head in range(2):
            lanes = slice(head * head_width, (head + 1) * head_width)
            query = query_ref[rows, lanes]
            key = key_ref[:reach, lanes]
            grad = grad_ref[rows, lanes]
            scores = jnp.where(allowed, dot_of(key, query, ((1,), (1,))) * scale, -1e30)
            weights_soft = jnp.exp(scores - logsum_ref[0, 0, head : head + 1, rows])
            grad_value = dot_of(weights_soft.astype(half_type), grad, ((1,), (0,)))
            grad_weights = dot_of(value_ref[:reach, lanes], grad, ((1,), (1,)))
            leaning = jnp.sum(weights_soft * grad_weights, 0, keepdims=True)
            grad_scores = (weights_soft * (grad_weights - leaning)).astype(half_type)
            query_sum[rows, lanes] = dot_of(grad_scores, key, ((0,), (0,))) * scale
            grad_key = dot_of(grad_scores, query, ((1,), (0,))) * scale
            if block == 1:
                value_sum[:, lanes] = grad_value
                key_sum[:, lanes] = grad_key
            else:
                value_sum[:reach, lanes] = value_sum[:reach, lanes] + grad_value
                key_sum[:reach, lanes] = key_sum[:reach, lanes] + grad_key
    out_ref[0] = turned(query_sum[...], tables_ref, False).astype(half_type)
    out_ref[1] = turned(key_sum[...], tables_ref, False).astype(half_type)
    out_ref[2] = value_sum[...].astype(half_type)


def attention_backward(queries, keys_all, values_all, grad_context, logsum, tables, segments):
    micro_count, row_length = segments.shape
    tokens, width = queries.shape
    pairs = width // LANES
    part, tables_spec, row, column, logsum_spec = attention_specs(row_length, pairs)
    return pl.pallas_call(
        backward_kernel,
        out_shape=jax.ShapeDtypeStruct((3, tokens, width), half_type),
        grid=(micro_count, pairs),
        in_specs=[part(0), part(0), part(0), part(0), tables_spec, row, column, logsum_spec],
        out_specs=pl.BlockSpec((3, row_length, LANES), lambda m, h: (0, m, h)),
        scratch_shapes=[pltpu.VMEM((row_length, LANES), full_type) for _ in range(3)],
        compiler_params=pltpu.CompilerParams(
            dimension_semantics=("arbitrary", "arbitrary"), vmem_limit_bytes=40 * 1024 * 1024
        ),
    )(queries, keys_all, values_all, grad_context, tables, segments[:, None, :], segments[:, :, None], logsum)


def document_kernel(starts_ref, total_ref, in_ref, out_ref, sum_ref, turned_ref, spill_ref):
    micro_count, docs = starts_ref.shape[0], starts_ref.shape[1] - 1
    row_length = in_ref.shape[0] // micro_count
    reach = row_length // 2
    step = 16

    def bounds(micro, doc):
        start, end = starts_ref[micro, doc], starts_ref[micro, doc + 1]
        window = jnp.minimum((start // step) * step, row_length - reach)
        base = pl.multiple_of(micro * row_length + window, step)
        return (start - window, end - window, base)

    @pl.when(pl.program_id(0) == 0)
    def _():
        for micro in range(micro_count):
            for doc in range(docs):
                begin, end, base = bounds(micro, doc)
                place = lax.broadcasted_iota(jnp.int32, (reach, in_ref.shape[1]), 0)
                rows = in_ref[pl.ds(base, reach), :].astype(full_type)
                kept = jnp.where((place >= begin) & (place < end), rows, 0.0)
                turned_ref[micro * docs + doc] = jnp.transpose(kept).astype(half_type)

                @pl.when(end > reach)
                def _():
                    place = reach + lax.broadcasted_iota(jnp.int32, (step, in_ref.shape[1]), 0)
                    rows = in_ref[pl.ds(base + reach, step), :].astype(full_type)
                    spill_ref[micro * docs + doc] = jnp.where(place < end, rows, 0.0).astype(half_type)

    total = total_ref[0]
    for micro in range(micro_count):
        for doc in range(docs):
            begin, end, base = bounds(micro, doc)
            place = micro * docs + doc
            first = place == 0

            def add(block):
                block = (block * total).astype(half_type).astype(full_type)
                sum_ref[...] = block * block if first else sum_ref[...] + block * block

            block = dot_of(turned_ref[place], out_ref[pl.ds(base, reach), :], ((1,), (0,)))

            @pl.when(end <= reach)
            def _():
                add(block)

            @pl.when(end > reach)
            def _():
                more = dot_of(spill_ref[place], out_ref[pl.ds(base + reach, step), :], ((0,), (0,)))
                add(block + more)


def document_squares(rot_in, rot_out, segments, total):
    micro_count, row_length = segments.shape
    tokens, width = rot_in.shape
    hidden = rot_out.shape[1]
    tile = 2 * LANES
    slots = jnp.arange(DOCS + 1)
    starts = jnp.sum(segments[:, :, None] < slots[None, None, :], 1).astype(jnp.int32)
    return pl.pallas_call(
        document_kernel,
        out_shape=jax.ShapeDtypeStruct((width, hidden), full_type),
        grid=(hidden // tile,),
        in_specs=[
            pl.BlockSpec(memory_space=pltpu.SMEM),
            pl.BlockSpec(memory_space=pltpu.SMEM),
            pl.BlockSpec((tokens, width), lambda i: (0, 0)),
            pl.BlockSpec((tokens, tile), lambda i: (0, i)),
        ],
        out_specs=pl.BlockSpec((width, tile), lambda i: (0, i)),
        scratch_shapes=[
            pltpu.VMEM((micro_count * DOCS, width, row_length // 2), half_type),
            pltpu.VMEM((micro_count * DOCS, 16, width), half_type),
        ],
        compiler_params=pltpu.CompilerParams(
            dimension_semantics=("arbitrary",), vmem_limit_bytes=40 * 1024 * 1024
        ),
    )(starts, total.reshape(1), rot_in, rot_out)


AXES = ("dp", "fsdp")


def partner_pairs(count, bit):
    return [(place, place ^ (1 << bit)) for place in range(count)]


class Stream:
    def __init__(self, chunks, order, wire, relative=False):
        self.count = chunks.shape[0]
        bits = self.count.bit_length() - 1
        self.held = chunks.reshape((2,) * bits + chunks.shape[1:])
        self.left = list(order) if relative else list(range(bits - 1, -1, -1))
        self.relative = relative
        self.order = list(order)
        self.wire = wire
        self.sent = self.kept = self.got = None

    def land(self, arrived):
        self.held = self.kept + arrived.astype(full_type)
        self.got = None

    def split(self):
        bit = self.order[0]
        axis = self.left.index(bit)
        mine = 0 if self.relative else (lax.axis_index(AXES) >> bit) & 1
        self.sent = lax.dynamic_index_in_dim(self.held, 1 - mine, axis, keepdims=False)
        self.kept = lax.dynamic_index_in_dim(self.held, mine, axis, keepdims=False)
        if bit != 0:
            self.sent = self.sent.astype(self.wire)
        self.left.pop(axis)

    def send(self, ready):
        self.got = lax.ppermute(ready, AXES, partner_pairs(self.count, self.order.pop(0)))


def link_orders(bits):
    near = list(range(1, bits - 2))
    return ([0, bits - 2, bits - 1] + near, [0, bits - 1, bits - 2] + near)


def flipped(folded, place):
    bits = lax.axis_size(AXES).bit_length() - 1
    for axis in range(bits):
        mine = (place >> (bits - 1 - axis)) & 1
        folded = jnp.where(mine == 1, jnp.flip(folded, axis), folded)
    return folded


def by_device(stacked, order, place):
    bits = len(order)
    folded = stacked.reshape((2,) * bits + stacked.shape[1:])
    natural = [order.index(bit) for bit in range(bits - 1, -1, -1)]
    folded = jnp.transpose(folded, natural + list(range(bits, folded.ndim)))
    return flipped(folded, place).reshape(stacked.shape)


def by_partner(ordered, order, place):
    bits = len(order)
    folded = flipped(ordered.reshape((2,) * bits + ordered.shape[1:]), place)
    stacked = [bits - 1 - bit for bit in order]
    folded = jnp.transpose(folded, stacked + list(range(bits, folded.ndim)))
    return folded.reshape(ordered.shape)


def gather_trees(blocks, orders):
    held = [block[None] for block in blocks]
    for step in range(len(orders[0])):
        for m, order in enumerate(orders):
            count = 1 << len(order)
            arrived = lax.ppermute(held[m], AXES, partner_pairs(count, order[-1 - step]))
            held[m] = jnp.concatenate([held[m], arrived], 0)
    return held


def streams_of(full, count, wire=full_type):
    rows = full.shape[0] // count
    half = full.shape[1] // 2
    chunks = full.reshape(count, rows, full.shape[1])
    order_a, order_b = link_orders(count.bit_length() - 1)
    return [Stream(chunks[:, :, :half], order_a, wire), Stream(chunks[:, :, half:], order_b, wire)]


def advance(anchor, streams):
    flying = [stream for stream in streams if stream.got is not None]
    anchor, landed = lax.optimization_barrier((anchor, [stream.got for stream in flying]))
    for stream, arrived in zip(flying, landed):
        stream.land(arrived)
    going = [stream for stream in streams if stream.order]
    for stream in going:
        stream.split()
    anchor, ready = lax.optimization_barrier((anchor, [stream.sent for stream in going]))
    for stream, block in zip(going, ready):
        stream.send(block)
    return anchor


def finished(streams):
    return jnp.concatenate([stream.held for stream in streams], 1)


def run_all(anchor, streams):
    while any(stream.order or stream.got is not None for stream in streams):
        anchor = advance(anchor, streams)
    return anchor


def shared_by_all(own, count):
    return lax.all_to_all(
        jnp.broadcast_to(own[None], (count,) + own.shape), AXES, split_axis=0, concat_axis=0, tiled=True
    )


def adam_update(weight, gradient, moment_one, moment_two, rate, step_value):
    next_one = decay_first * moment_one + (1.0 - decay_first) * gradient
    next_two = decay_second * moment_two + (1.0 - decay_second) * gradient * gradient
    fix_one = 1.0 - decay_first**step_value
    fix_two = 1.0 - decay_second**step_value
    update = next_one / fix_one / (jnp.sqrt(next_two / fix_two) + adam_epsilon)
    return [weight - rate * (update + weight_decay * weight), next_one, next_two]


def per_device(
    step_count,
    token_ids,
    segment_ids,
    loss_positions,
    label_ids,
    label_mask,
    embed_in,
    embed_in_first,
    embed_in_second,
    embed_out,
    embed_out_first,
    embed_out_second,
    proj_in,
    proj_in_first,
    proj_in_second,
    proj_up,
    proj_up_first,
    proj_up_second,
    proj_mix,
    proj_mix_first,
    proj_mix_second,
    vector_params,
    vector_first,
    vector_second,
    basis_in,
    basis_out,
):
    micro_count = token_ids.shape[0]
    row_length = token_ids.shape[2]
    pick_count = loss_positions.shape[2]
    tokens = micro_count * row_length
    count = lax.axis_size(AXES)
    total = jnp.maximum(jnp.sum(label_mask.astype(full_type)), 1.0)
    vocab = embed_in.shape[1]
    own_width = embed_in.shape[0]
    width = proj_mix.shape[1]
    hidden = proj_up.shape[1]
    head_width = width // HEADS

    weight_in = lax.all_gather(proj_in.astype(half_type), AXES, axis=0, tiled=True)
    weight_up = lax.all_gather(proj_up.astype(half_type), AXES, axis=0, tiled=True)
    weight_mix = lax.all_gather(proj_mix.astype(half_type), AXES, axis=0, tiled=True)
    vector = shared_by_all(vector_params.astype(half_type), count).reshape(-1).astype(full_type)
    (
        bias_in,
        bias_up,
        bias_mix,
        shift_first,
        shift_second,
        shift_last,
        gain_first,
        gain_second,
        gain_last,
    ) = split_vector(vector, width, hidden)

    flat_ids = jnp.transpose(token_ids, (1, 0, 2)).reshape(-1)
    ids_by_run = flat_ids.reshape(count, 1, tokens)
    columns = gather_features(embed_in, ids_by_run)
    arrived = lax.all_to_all(columns, AXES, split_axis=0, concat_axis=0, tiled=True)
    embedded = arrived.reshape(width, tokens).T.astype(full_type)
    places = scatter_places(ids_by_run, own_width, vocab)
    segments = segment_ids[:, 0]
    picks = loss_positions[:, 0] + row_length * jnp.arange(micro_count)[:, None]
    picks = picks.reshape(-1)

    normed, inv_std = normalize(embedded)
    first_in = (normed * gain_first + shift_first).astype(half_type)
    second_in = (normed * gain_second + shift_second).astype(half_type)
    mixed = jnp.dot(first_in, weight_in, preferred_element_type=full_type) + bias_in
    tables = turn_tables(row_length, head_width)
    context, queries, keys_all, values_all, logsum = attention_forward(mixed, tables, segments)
    hidden_pre = jnp.dot(second_in, weight_up, preferred_element_type=full_type) + bias_up
    active = (hidden_pre * (0.5 + 0.5 * lax.erf(hidden_pre * (1.0 / math.sqrt(2.0))))).astype(half_type)
    joined = jnp.concatenate([context, active], 1)
    residual = embedded + jnp.dot(joined, weight_mix, preferred_element_type=full_type) + bias_mix
    normed_last, inv_last = normalize(residual)
    final = normed_last * gain_last + shift_last
    picked = jnp.take(final, picks, axis=0, mode="clip").astype(half_type)

    bits = count.bit_length() - 1
    orders = link_orders(bits)
    place = lax.axis_index(AXES)
    picked = picked.reshape(micro_count, pick_count, width)
    gathered = jnp.stack(gather_trees(picked, orders)).reshape(-1, width)
    table_out = embed_out.astype(half_type)
    vocab_rows = embed_out.shape[0]
    vocab_ids = place * vocab_rows + jnp.arange(vocab_rows)
    labels_flat = jnp.stack([by_partner(label_ids[m], orders[m], place) for m in range(micro_count)]).reshape(-1)
    mask_flat = jnp.stack([by_partner(label_mask[m], orders[m], place) for m in range(micro_count)]).reshape(-1)
    mask_flat = mask_flat.astype(full_type)
    logits = jnp.einsum("rd,vd->rv", gathered, table_out, preferred_element_type=full_type)
    matches = labels_flat[:, None] == vocab_ids[None, :]
    label_part = jnp.sum(jnp.where(matches, logits, 0.0), 1)
    local_max = jnp.max(logits, 1)
    local_sum = jnp.sum(jnp.exp(logits - local_max[:, None]), 1)
    parts = jnp.stack([local_max, local_sum, label_part], 0).reshape(3, micro_count, count, pick_count)
    parts = jnp.transpose(parts, (1, 2, 0, 3))
    parts = jnp.stack([by_device(parts[m], orders[m], place) for m in range(micro_count)], 1)
    parts = lax.all_to_all(
        parts.reshape(count, 1, -1), AXES, split_axis=0, concat_axis=0, tiled=True
    ).reshape(count, micro_count, 3, pick_count)
    peak = jnp.max(parts[:, :, 0], 0)
    own_logsum = peak + jnp.log(jnp.sum(parts[:, :, 1] * jnp.exp(parts[:, :, 0] - peak[None]), 0))
    own_mask = lax.dynamic_index_in_dim(label_mask, place, 1, keepdims=False).astype(full_type)
    loss_part = jnp.sum(own_mask * (own_logsum - jnp.sum(parts[:, :, 2], 0))) / total
    logsum_all = shared_by_all(own_logsum.reshape(1, -1), count).reshape(count, micro_count, pick_count)
    logsum_all = jnp.stack([by_partner(logsum_all[:, m], orders[m], place) for m in range(micro_count)]).reshape(-1)
    grad_logits = (
        (jnp.exp(logits - logsum_all[:, None]) - matches.astype(full_type))
        * (mask_flat / total)[:, None]
    ).astype(half_type)
    back = jnp.dot(grad_logits, table_out, preferred_element_type=full_type)
    back = back.reshape(micro_count, count, pick_count, width)
    pick_streams = [Stream(back[m], orders[m], full_type, relative=True) for m in range(micro_count)]
    grad_logits = advance(grad_logits, pick_streams)
    grad_out_table = jnp.einsum("rv,rd->vd", grad_logits, gathered, preferred_element_type=full_type)
    run_all(jnp.zeros((), full_type), pick_streams)
    grad_picked = jnp.concatenate([stream.held for stream in pick_streams], 0)

    grad_final = jnp.zeros((tokens, width), full_type).at[picks].add(grad_picked)
    grad_residual = norm_back(grad_final * gain_last, normed_last, inv_last)
    grad_branch = grad_residual.astype(half_type)
    grad_mix = jnp.einsum("sa,sb->ab", joined, grad_branch, preferred_element_type=full_type)
    mix_streams = streams_of(grad_mix, count)
    grad_branch = advance(grad_branch, mix_streams)
    grad_joined = jnp.einsum("sb,ab->sa", grad_branch, weight_mix, preferred_element_type=full_type)
    grad_context = (
        grad_joined[:, :width].astype(half_type)
    )
    grad_hidden = (grad_joined[:, width:] * gelu_slope(hidden_pre)).astype(half_type)
    grad_hidden = advance(grad_hidden, mix_streams)
    grad_up = jnp.einsum("sa,sb->ab", second_in, grad_hidden, preferred_element_type=full_type)
    grad_second = jnp.einsum("sb,ab->sa", grad_hidden, weight_up, preferred_element_type=full_type)
    up_streams = streams_of(grad_up, count)
    (grad_hidden, grad_second) = advance((grad_hidden, grad_second), mix_streams + up_streams)

    rot_in = jnp.dot(second_in, basis_in, preferred_element_type=full_type).astype(half_type)
    rot_out = jnp.dot(grad_hidden, basis_out, preferred_element_type=full_type).astype(half_type)
    (rot_in, rot_out) = advance((rot_in, rot_out), mix_streams + up_streams)
    scale_sum = document_squares(rot_in, rot_out, segments, total)
    scale_streams = streams_of(scale_sum, count, half_type)
    grad_context = advance(grad_context, mix_streams + up_streams + scale_streams)

    grad_parts = attention_backward(
        queries, keys_all, values_all, grad_context, logsum, tables, segments
    )
    grad_mixed = jnp.concatenate([grad_parts[0], grad_parts[1], grad_parts[2]], 1)
    grad_mixed = advance(grad_mixed, mix_streams + up_streams + scale_streams)
    grad_in = jnp.einsum("sa,sb->ab", first_in, grad_mixed, preferred_element_type=full_type)
    in_streams = streams_of(grad_in, count)
    grad_mixed = advance(grad_mixed, up_streams + scale_streams + in_streams)
    grad_first = jnp.einsum("sb,ab->sa", grad_mixed, weight_in, preferred_element_type=full_type)
    grad_embedded = grad_residual + norm_back(
        grad_first * gain_first + grad_second * gain_second, normed, inv_std
    )
    sending = grad_embedded.astype(half_type).T.reshape(count, own_width, tokens)
    returned = lax.all_to_all(sending, AXES, split_axis=0, concat_axis=0, tiled=True)
    vector_grad = jnp.concatenate(
        [
            jnp.sum(grad_mixed.astype(full_type), 0),
            jnp.sum(grad_hidden.astype(full_type), 0),
            jnp.sum(grad_residual, 0),
            jnp.sum(grad_first, 0),
            jnp.sum(grad_second, 0),
            jnp.sum(grad_final, 0),
            jnp.sum(grad_first * normed, 0),
            jnp.sum(grad_second * normed, 0),
            jnp.sum(grad_final * normed_last, 0),
        ]
    )
    vector_parts = lax.all_to_all(
        vector_grad.reshape(count, 1, -1), AXES, split_axis=0, concat_axis=0, tiled=True
    )
    own_vector = jnp.sum(vector_parts, (0, 1))
    late = mix_streams + up_streams + scale_streams + in_streams
    own_vector = advance(own_vector, late)
    own_vector = advance(own_vector, late)
    returned, own_vector = lax.optimization_barrier((returned, own_vector))
    grad_in_table, in_squares = scatter_features(returned, places, vocab)
    in_squares = run_all(in_squares, late)
    own_mix = finished(mix_streams)
    own_up = finished(up_streams)
    own_in = finished(in_streams)
    eigen_scales = finished(scale_streams) / float(micro_count * count * DOCS)
    grads = (grad_in_table, grad_out_table, own_in, own_up, own_mix, own_vector)
    squares = jnp.sum(in_squares) + sum((jnp.sum(gradient * gradient) for gradient in grads[1:]))
    both = jnp.sum(shared_by_all(jnp.stack([squares, loss_part])[None], count), (0, 1))
    grad_norm = jnp.sqrt(both[0])
    loss_value = both[1]
    factor = jnp.minimum(1.0, clip_limit / (grad_norm + 1e-06))
    step_value = step_count[0].astype(full_type)
    weights = (embed_in, embed_out, proj_in, proj_up, proj_mix, vector_params)
    firsts = (
        embed_in_first,
        embed_out_first,
        proj_in_first,
        proj_up_first,
        proj_mix_first,
        vector_first,
    )
    seconds = (
        embed_in_second,
        embed_out_second,
        proj_in_second,
        proj_up_second,
        proj_mix_second,
        vector_second,
    )
    results = []
    for weight, gradient, moment_one, moment_two, rate in zip(
        weights, grads, firsts, seconds, step_rates
    ):
        results.extend(
            adam_update(weight, gradient * factor, moment_one, moment_two, rate, step_value)
        )
    return tuple(results) + (loss_value, grad_norm, eigen_scales)


def solution(mesh):
    in_specs = (
        P(),
        P(),
        P(None, ("dp", "fsdp"), None),
        P(None, ("dp", "fsdp"), None),
        P(),
        P(),
        P(("dp", "fsdp"), None),
        P(("dp", "fsdp"), None),
        P(("dp", "fsdp"), None),
        P(("dp", "fsdp"), None),
        P(("dp", "fsdp"), None),
        P(("dp", "fsdp"), None),
        P(("dp", "fsdp"), None),
        P(("dp", "fsdp"), None),
        P(("dp", "fsdp"), None),
        P(("dp", "fsdp"), None),
        P(("dp", "fsdp"), None),
        P(("dp", "fsdp"), None),
        P(("dp", "fsdp"), None),
        P(("dp", "fsdp"), None),
        P(("dp", "fsdp"), None),
        P(("dp", "fsdp")),
        P(("dp", "fsdp")),
        P(("dp", "fsdp")),
        P(),
        P(),
    )
    out_specs = (
        P(("dp", "fsdp"), None),
        P(("dp", "fsdp"), None),
        P(("dp", "fsdp"), None),
        P(("dp", "fsdp"), None),
        P(("dp", "fsdp"), None),
        P(("dp", "fsdp"), None),
        P(("dp", "fsdp"), None),
        P(("dp", "fsdp"), None),
        P(("dp", "fsdp"), None),
        P(("dp", "fsdp"), None),
        P(("dp", "fsdp"), None),
        P(("dp", "fsdp"), None),
        P(("dp", "fsdp"), None),
        P(("dp", "fsdp"), None),
        P(("dp", "fsdp"), None),
        P(("dp", "fsdp")),
        P(("dp", "fsdp")),
        P(("dp", "fsdp")),
        P(),
        P(),
        P(("dp", "fsdp"), None),
    )
    return jax.shard_map(
        per_device, mesh=mesh, in_specs=in_specs, out_specs=out_specs, check_vma=False
    )
```

time: 2550 us -> 1000 us (0.39)
  blocking collectives: 750 us -> 0 us
  waiting for transfers between devices: 593 us -> 215 us
  local copies, waits for them, and re-layouts: 430 us -> 122 us
  other arithmetic: 424 us -> 148 us
  Pallas kernels: 0 us -> 257 us
  matrix products: 275 us -> 129 us
  starting transfers between devices: 31.2 us -> 96.9 us
    unnamed x2 -> x0, blocking collectives: 481 us -> none
    all_to_all x6 -> x7, waiting for transfers between devices: 382 us -> 77.8 us  [the longest x1 54.5 us: per_device(): lax.all_to_all(columns, AXES, split_axis=0, concat_axis=0, tiled=True)]
    pallas_call x0 -> x5, Pallas kernels: none -> 257 us  [the longest x1 97.4 us: scatter_features(): pl.pallas_call(scatter_kernel, out_shape=(jax.ShapeDtypeStruct((width, vo...]
    all_gather x6 -> x0, blocking collectives: 231 us -> none  [merged(): pieces = jax.tree.map(lambda part: lax.all_gather(part, axis), value)]
    reduce_scatter x5 -> x0, waiting for transfers between devices: 157 us -> none  [the longest x2 157 us: head_step(): lax.psum_scatter(jnp.dot(grad_logits, table_group, preferred_element_type...]
    dot_general x42 -> x14, matrix products: 275 us -> 129 us  [the longest x1 22.7 us: per_device(): jnp.dot(grad_hidden, basis_out, preferred_element_type=full_type)]
    add x131 -> x54, other arithmetic: 190 us -> 47.7 us  [the longest x50 43.8 us: land(): self.held = self.kept + arrived.astype(full_type)]
    gather x4 -> x1, local copies, waits for them, and re-layouts: 127 us -> 2.37 us  [per_device(): picked = jnp.take(final, picks, axis=0, mode='clip').astype(half_type)]
  transfers between devices with their start and end apart: 16 -> 70, of which waited for: 6 -> 39; matrix products, arithmetic and copies ran while one was open for 34% -> 20% of each run, Pallas kernels for 0% -> 26%
where the time goes in v1:
time: 1000 us; the launch traced here: 992 us
  Pallas kernels  257 us (26%)
  waiting for transfers between devices  215 us (22%)
  other arithmetic  148 us (15%)
  matrix products  129 us (13%)
  local copies, waits for them, and re-layouts  122 us (12%)
  starting transfers between devices  96.9 us (10%)
  between operations  24.3 us (2%)
    ppermute x50, waiting for transfers between devices, send(): lax.ppermute(ready, AXES, partner_pairs(self.count, self.order.pop(0)))  106 us
    pallas_call x1, Pallas kernels, scatter_features(): pl.pallas_call(scatter_kernel, out_shape=(jax.ShapeDtypeStruct((width, vo...  97.4 us
    pallas_call x1, Pallas kernels, gather_features(): pl.pallas_call(gather_kernel, out_shape=jax.ShapeDtypeStruct((count, widt...  64.5 us
    all_to_all x1, waiting for transfers between devices, per_device(): lax.all_to_all(columns, AXES, split_axis=0, concat_axis=0, tiled=True)  54.5 us
    ppermute x50, starting transfers between devices, send(): lax.ppermute(ready, AXES, partner_pairs(self.count, self.order.pop(0)))  54.2 us
    add x50, other arithmetic, land(): self.held = self.kept + arrived.astype(full_type)  43.8 us
    unnamed x274, local copies, waits for them, and re-layouts  43 us
    pallas_call x1, Pallas kernels, document_squares(): pl.pallas_call(document_kernel, out_shape=jax.ShapeDtypeStruct((width, hi...  41.8 us
  transfers between devices with their start and end apart: 70, of which 39 were waited for; matrix products, arithmetic and copies ran while one was open for 20% of the time, Pallas kernels for 26%

profile of v1, /device:TPU:0, one launch (start us, length us, event | category | flops | bytes accessed | tf_op | source)
XLA Modules:
  0.0 992.2 jit_solution(5931793526376967343)
XLA Ops:
  15.2 7.3 all-to-all-start.1
  30.7 64.5 %shard_map.409 = bf16[32,24,1024]{2,1,0:T(8,128)(2,1)} custom-call(s32[32,1,1024]{2,1,0:T(1,128)S(1)} %reshape_reshape.3.ids_ref, f32[24,50304]{1,0:T(8,128)S(1)} %copy-done.2), custom_call_target="tpu_custom_call" | custom-call | tf_op jit(solution)/shard_map/pallas_call | solution.py:118
  95.2 5.9 all-to-all-start
  104.4 54.5 %all-to-all-done = bf16[32,24,1024]{2,1,0:T(8,128)(2,1)} async-done(((bf16[32,24,1024]{2,1,0:T(8,128)(2,1)}), bf16[32,24,1024]{2,1,0:T(8,128)(2,1)}, u32[]{:S(2)}, u32[]{:S(2)}) %all-to-all-start) | async-done | bytes 1572896 | tf_op jit(solution)/shard_map/all_to_all | solution.py:648
  165.9 10.2 %convolution_add_fusion.query_in.key_in.value_in = f32[1024,2304]{1,0:T(8,128)} fusion(bf16[1024,768]{0,1:T(8,128)(2,1)} %get-tuple-element.353, bf16[768,2304]{1,0:T(8,128)(2,1)} %all-gather.4.cloned.1.call-done, f32[2304]{0:T(1024)S(1)} %slice.180), kind=kOutput, calls=%fused_computation.23 | convolution fusion | flops 3626237952 | bytes 14558208 | tf_op jit(solution)/shard_map/dot_general | solution.py:658
  176.1 20.9 %shard_map.410 = (bf16[1024,768]{1,0:T(8,128)(2,1)S(1)}, bf16[1024,768]{1,0:T(8,128)(2,1)S(1)}, bf16[1024,768]{1,0:T(8,128)(2,1)S(1)}, bf16[1024,768]{1,0:T(8,128)(2,1)S(1)}, f32[2,6,2,512]{3,2,1,0:T(2,128)S(1)}) custom-call(f32[1024,2304]{1,0:T(8,128)} %convolution_add_fusion.query_in.key_in.value_in, ...), custom_call_target="tpu_custom_call" | custom-call | tf_op jit(solution)/shard_map/pallas_call | solution.py:322
  202.2 12.2 %multiply_convert_fusion = (bf16[1024,3072]{1,0:T(8,128)(2,1)}, f32[1024,3072]{1,0:T(8,128)}) fusion(f32[3072]{0:T(1024)S(1)} %slice.183, bf16[1024,768]{0,1:T(8,128)(2,1)} %get-tuple-element.354, bf16[768,3072]{1,0:T(8,128)(2,1)} %all-gather.6.cloned.1.call-done), kind=kOutput, calls=%fused_computation.17 | convolution fusion | flops 4850712576 | bytes 25178112 | tf_op jit(solution)/shard_map/dot_general | solution.py:661
  214.5 12.2 %all-gather.8.cloned.1.call-done = bf16[3840,768]{1,0:T(8,128)(2,1)} async-done(((bf16[120,768]{1,0:T(8,128)(2,1)}), bf16[3840,768]{1,0:T(8,128)(2,1)}) %all-gather.8.cloned.1.call-update) | async-done | bytes 5898256 | tf_op jit(solution)/shard_map/all_gather | solution.py:631
  226.7 11.2 %fusion.106 = (f32[1024]{0:T(1024)S(1)}, f32[1024,768]{0,1:T(8,128)S(1)}) fusion(f32[768]{0:T(1024)S(1)} %get-tuple-element.384, bf16[3840,768]{1,0:T(8,128)(2,1)} %all-gather.8.cloned.1.call-done, bf16[1024,3072]{1,0:T(8,128)(2,1)} %get-tuple-element.402, bf16[1024,768]{1,0:T(8,128)(2,1)} %copy-done.17, bf16[32,24,1024]{2,1,0:T(8,128)(2,1)} %all-to-all-done), kind=kOutput, calls=%fused_computation.385 | convolution fusion | flops 6058671104 | bytes 18488320 | tf_op jit(solution)/shard_map/dot_general | solution.py:664
  269.1 4.5 collective-permute-done.3
  278.9 8.3 fusion.107
  287.3 6.8 exponential_reduce_fusion
  295.7 4.6 all-to-all-start.2
  301.1 6.6 all-to-all-done.2
  312.0 7.0 all-to-all-done.3
  320.7 7.1 fusion.3
  330.4 9.0 fusion.42
  347.4 18.4 %collective-permute-done.12 = f32[2,2,2,32,768]{4,3,2,1,0:T(8,128)S(1)} collective-permute-done((f32[2,2,2,32,768]{4,3,2,1,0:T(8,128)S(1)}, f32[2,2,2,32,768]{4,3,2,1,0:T(8,128)S(1)}, u32[]{:S(2)}, u32[]{:S(2)}) %collective-permute-start.12) | collective-permute-done | bytes 786464 | tf_op jit(solution)/shard_map/ppermute | solution.py:500
  371.1 7.3 collective-permute-done.14
  405.7 4.6 multiply_reduce_fusion.1
  414.8 9.8 fusion.10
  424.5 7.6 fusion.94
  432.2 4.9 constant_dynamic-slice_fusion.9
  441.2 9.3 fusion.108
  452.6 10.9 %fusion.9 = bf16[1024,3072]{1,0:T(8,128)(2,1)S(1)} fusion(f32[1024,3840]{1,0:T(8,128)} %fusion.108, f32[1024,3072]{1,0:T(8,128)} %get-tuple-element.403, f32[3072]{0:T(1024)S(1)} %slice.183), kind=kLoop, calls=%fused_computation.15 | loop fusion | flops 34603008 | bytes 31469568 | tf_op jit(solution)/shard_map/convert_element_type | solution.py:719
  463.5 4.6 bitcast_add_fusion.1
  476.1 7.5 fusion.110
  483.7 6.9 fusion.96
  496.7 6.7 fusion.109
  503.4 4.7 collective-permute-done.22
  514.8 22.7 %convolution_convert_fusion.out_ref = bf16[1024,3072]{1,0:T(8,128)(2,1)S(1)} fusion(bf16[1024,3072]{1,0:T(8,128)(2,1)S(1)} %fusion.9, bf16[3072,3072]{1,0:T(8,128)(2,1)} %param.51), kind=kOutput, calls=%fused_computation.24 | convolution fusion | flops 19330498560 | bytes 31457280 | tf_op jit(solution)/shard_map/dot_general | solution.py:727
  548.7 41.8 %shard_map.411 = f32[768,3072]{1,0:T(8,128)} custom-call(s32[2,5]{1,0:T(2,128)S(1)} %copy.265.starts_ref, f32[1]{0:T(128)} %bitcast.92.total_ref, bf16[1024,768]{1,0:T(8,128)(2,1)S(1)} %copy-done.11, bf16[1024,3072]{1,0:T(8,128)(2,1)S(1)} %convolution_convert_fusion.out_ref), custom_call_target="tpu_custom_call" | custom-call | tf_op jit(solution)/shard_map/pallas_call | solution.py:446
  590.5 4.6 fusion.95
  611.2 7.8 multiply_reduce_fusion
  626.9 3.9 convert_reduce_fusion
  630.8 4.0 collective-permute-start.32
  636.1 32.5 %shard_map.412 = bf16[3,1024,768]{2,1,0:T(8,128)(2,1)S(1)} custom-call(bf16[1024,768]{1,0:T(8,128)(2,1)S(1)} %copy-done.6, bf16[1024,768]{1,0:T(8,128)(2,1)S(1)} %copy-done.8, bf16[1024,768]{1,0:T(8,128)(2,1)S(1)} %copy-done.10, bf16[1024,768]{1,0:T(8,128)(2,1)S(1)} %slice.213.grad_ref, f32[3,512,128]{2,1,0:T(8,128)S(1)} %pad_maximum_fusion.7.tables_ref, ...), custom_call_target="tpu_custom_call" | custom-call | tf_op jit(solution)/shard_map/pallas_call | solution.py:375
  671.5 8.0 collective-permute-done.33
  717.8 7.8 fusion.86
  735.0 4.4 all-to-all-start.5
  773.1 26.6 %collective-permute-done.48 = bf16[2,24,1536]{2,1,0:T(8,128)(2,1)S(1)} collective-permute-done((bf16[2,24,1536]{2,1,0:T(8,128)(2,1)}, bf16[2,24,1536]{2,1,0:T(8,128)(2,1)S(1)}, u32[]{:S(2)}, u32[]{:S(2)}) %collective-permute-start.48) | collective-permute-done | bytes 147488 | tf_op jit(solution)/shard_map/ppermute | solution.py:500
  813.4 4.4 collective-permute-start.52
  817.8 97.4 %shard_map.413 = (f32[24,50304]{1,0:T(8,128)}, f32[8,128]{1,0:T(8,128)S(1)}) custom-call(s32[32,1,1024]{2,1,0:T(1,128)S(1)} %copy-done.12, bf16[32,24,1024]{2,1,0:T(8,128)(2,1)S(1)} %all-to-all-done.4.grad_ref), custom_call_target="tpu_custom_call" | custom-call | tf_op jit(solution)/shard_map/pallas_call | solution.py:208
  922.0 5.4 collective-permute-done.56
  933.4 6.1 collective-permute-done.58
  950.4 6.3 all-to-all-done.6
  965.8 11.9 %add_subtract_fusion = (f32[24,50304]{1,0:T(8,128)}, f32[24,50304]{1,0:T(8,128)}, f32[24,50304]{1,0:T(8,128)}) fusion(f32[24,50304]{1,0:T(8,128)} %table_ref.1, f32[]{:T(128)} %bitcast.159, f32[]{:T(128)} %bitcast.158, f32[24,50304]{1,0:T(8,128)} %get-tuple-element.264, f32[]{:T(128)S(6)} %min.3, f32[24,50304]{1,0:T(8,128)} %param.34, f32[24,50304]{1,0:T(8,128)} %param.33), kind=kLoop, calls=%fused_computation.32 | loop fusion | flops 18109440 | bytes 33804300 | tf_op jit(solution)/shard_map/sub | solution.py:586
  977.8 6.5 multiply_subtract_fusion
  (684 shorter events, 309.7 us)
Async XLA Ops:
  7.2 158.7 %all-gather.4.cloned.1.call-start = ((), (), s32[]{:S(2)}) async-start(), calls=%async_computation.7 | async-start | bytes 3649536 | tf_op jit(solution)/shard_map/all_gather | solution.py:629
  9.0 193.3 %all-gather.6.cloned.1.call-start = ((), (), s32[]{:S(2)}) async-start(), calls=%async_computation.8 | async-start | bytes 4866048 | tf_op jit(solution)/shard_map/all_gather | solution.py:630
  10.7 216.0 %all-gather.8.cloned.1.call-start = ((), (), s32[]{:S(2)}) async-start(), calls=%async_computation.9 | async-start | bytes 6082560 | tf_op jit(solution)/shard_map/all_gather | solution.py:631
  15.2 80.0 %all-to-all-start.1 = ((bf16[32,2,168]{2,1,0:T(2,128)(2,1)}), bf16[32,2,168]{2,1,0:T(2,128)(2,1)S(1)}, u32[]{:S(2)}, u32[]{:S(2)}) async-start(bf16[32,2,168]{2,1,0:T(2,128)(2,1)} %reshape.606), calls=%async_computation.1 | async-start | bytes 65536 | tf_op jit(solution)/shard_map/all_to_all | solution.py:575
  95.2 63.7 %all-to-all-start = ((bf16[32,24,1024]{2,1,0:T(8,128)(2,1)}), bf16[32,24,1024]{2,1,0:T(8,128)(2,1)}, u32[]{:S(2)}, u32[]{:S(2)}) async-start(bf16[32,24,1024]{2,1,0:T(8,128)(2,1)} %shard_map.409), calls=%async_computation | async-start | bytes 3145728 | tf_op jit(solution)/shard_map/all_to_all | solution.py:648
  262.7 10.9 %collective-permute-start.3 = (bf16[8,32,768]{2,1,0:T(8,128)(2,1)S(1)}, bf16[8,32,768]{2,1,0:T(8,128)(2,1)S(1)}, u32[]{:S(2)}, u32[]{:S(2)}) collective-permute-start(bf16[8,32,768]{2,1,0:T(8,128)(2,1)S(1)} %pad_maximum_fusion.8), channel_id=1, source_target_pairs={{0,8},{1,9},{2,10},{3,11},{4,12},{5,13},{6,14},{7,15},{8,0},{9,1},... | collective-permute-start | bytes 1179656 | tf_op jit(solution)/shard_map/ppermute | solution.py:537
  295.7 11.9 %all-to-all-start.2 = ((f32[32,1,192]{2,1,0:T(1,128)}), f32[32,1,192]{2,1,0:T(1,128)S(1)}, u32[]{:S(2)}, u32[]{:S(2)}) async-start(f32[32,1,192]{2,1,0:T(1,128)} %reshape.582), calls=%async_computation.2 | async-start | bytes 65536 | tf_op jit(solution)/shard_map/all_to_all | solution.py:688
  346.1 19.6 %collective-permute-start.12 = (f32[2,2,2,32,768]{4,3,2,1,0:T(8,128)S(1)}, f32[2,2,2,32,768]{4,3,2,1,0:T(8,128)S(1)}, u32[]{:S(2)}, u32[]{:S(2)}) collective-permute-start(f32[2,2,2,32,768]{4,3,2,1,0:T(8,128)S(1)} %slice_bitcast_fusion.5), channel_id=1, source_target_pairs={{0,8},{1,9},{2,10},{3,11},{4,12},{5,13},{6,14},{7,15},{8,0},{9,1},... | collective-permute-start | bytes 2359304 | tf_op jit(solution)/shard_map/ppermute | solution.py:500
  346.8 19.3 %collective-permute-start.13 = (f32[2,2,2,32,768]{4,3,2,1,0:T(8,128)S(1)}, f32[2,2,2,32,768]{4,3,2,1,0:T(8,128)S(1)}, u32[]{:S(2)}, u32[]{:S(2)}) collective-permute-start(f32[2,2,2,32,768]{4,3,2,1,0:T(8,128)S(1)} %slice_bitcast_fusion.4), channel_id=1, source_target_pairs={{0,16},{1,17},{2,18},{3,19},{4,20},{5,21},{6,22},{7,23},{8,24},{9,... | collective-permute-start | bytes 2359304 | tf_op jit(solution)/shard_map/ppermute | solution.py:500
  368.0 10.4 %collective-permute-start.14 = (f32[2,2,32,768]{3,2,1,0:T(8,128)}, f32[2,2,32,768]{3,2,1,0:T(8,128)}, u32[]{:S(2)}, u32[]{:S(2)}) collective-permute-start(f32[2,2,32,768]{3,2,1,0:T(8,128)} %slice_bitcast_fusion.9), channel_id=1, source_target_pairs={{0,16},{1,17},{2,18},{3,19},{4,20},{5,21},{6,22},{7,23},{8,24},{9,... | collective-permute-start | bytes 1179656 | tf_op jit(solution)/shard_map/ppermute | solution.py:500
  440.7 22.8 %collective-permute-start.20 = (f32[2,2,2,2,120,384]{5,4,3,2,0,1:T(8,128)}, f32[2,2,2,2,120,384]{5,4,3,2,0,1:T(8,128)}, u32[]{:S(2)}, u32[]{:S(2)}) collective-permute-start(f32[2,2,2,2,120,384]{5,4,3,2,0,1:T(8,128)} %bitcast.394), channel_id=1, source_target_pairs={{0,1},{1,0},{2,3},{3,2},{4,5},{5,4},{6,7},{7,6},{8,9},{9,8},{10,11... | collective-permute-start | bytes 8847368 | tf_op jit(solution)/shard_map/ppermute | solution.py:500
  440.7 22.8 %collective-permute-start.21 = (f32[2,2,2,2,120,384]{5,4,3,2,1,0:T(8,128)}, f32[2,2,2,2,120,384]{5,4,3,2,1,0:T(8,128)}, u32[]{:S(2)}, u32[]{:S(2)}) collective-permute-start(f32[2,2,2,2,120,384]{5,4,3,2,1,0:T(8,128)} %dynamic-slice_bitcast_fusion), channel_id=1, source_target_pairs={{0,1},{1,0},{2,3},{3,2},{4,5},{5,4},{6,7},{7,6},{8,9},{9,8},{10,11... | collective-permute-start | bytes 8847368 | tf_op jit(solution)/shard_map/ppermute | solution.py:500
  473.7 34.4 %collective-permute-start.22 = (f32[2,2,2,120,384]{4,3,2,1,0:T(8,128)}, f32[2,2,2,120,384]{4,3,2,1,0:T(8,128)}, u32[]{:S(2)}, u32[]{:S(2)}) collective-permute-start(f32[2,2,2,120,384]{4,3,2,1,0:T(8,128)} %dynamic-slice_bitcast_fusion.4), channel_id=1, source_target_pairs={{0,8},{1,9},{2,10},{3,11},{4,12},{5,13},{6,14},{7,15},{8,0},{9,1},... | collective-permute-start | bytes 4423688 | tf_op jit(solution)/shard_map/ppermute | solution.py:500
  475.1 34.1 %collective-permute-start.23 = (f32[2,2,2,120,384]{4,3,2,1,0:T(8,128)}, f32[2,2,2,120,384]{4,3,2,1,0:T(8,128)}, u32[]{:S(2)}, u32[]{:S(2)}) collective-permute-start(f32[2,2,2,120,384]{4,3,2,1,0:T(8,128)} %dynamic-slice_bitcast_fusion.3), channel_id=1, source_target_pairs={{0,16},{1,17},{2,18},{3,19},{4,20},{5,21},{6,22},{7,23},{8,24},{9,... | collective-permute-start | bytes 4423688 | tf_op jit(solution)/shard_map/ppermute | solution.py:500
  512.4 25.0 %collective-permute-start.24 = (f32[2,2,120,384]{3,2,1,0:T(8,128)S(1)}, f32[2,2,120,384]{3,2,1,0:T(8,128)S(1)}, u32[]{:S(2)}, u32[]{:S(2)}) collective-permute-start(f32[2,2,120,384]{3,2,1,0:T(8,128)S(1)} %dynamic-slice_bitcast_fusion.10), channel_id=1, source_target_pairs={{0,16},{1,17},{2,18},{3,19},{4,20},{5,21},{6,22},{7,23},{8,24},{9,... | collective-permute-start | bytes 2211848 | tf_op jit(solution)/shard_map/ppermute | solution.py:500
  513.6 23.9 %collective-permute-start.25 = (f32[2,2,120,384]{3,2,1,0:T(8,128)S(1)}, f32[2,2,120,384]{3,2,1,0:T(8,128)S(1)}, u32[]{:S(2)}, u32[]{:S(2)}) collective-permute-start(f32[2,2,120,384]{3,2,1,0:T(8,128)S(1)} %dynamic-slice_bitcast_fusion.9), channel_id=1, source_target_pairs={{0,8},{1,9},{2,10},{3,11},{4,12},{5,13},{6,14},{7,15},{8,0},{9,1},... | collective-permute-start | bytes 2211848 | tf_op jit(solution)/shard_map/ppermute | solution.py:500
  514.2 23.2 %collective-permute-start.26 = (f32[2,2,2,2,24,1536]{5,4,3,2,0,1:T(8,128)}, f32[2,2,2,2,24,1536]{5,4,3,2,0,1:T(8,128)S(1)}, u32[]{:S(2)}, u32[]{:S(2)}) collective-permute-start(f32[2,2,2,2,24,1536]{5,4,3,2,0,1:T(8,128)} %bitcast.397), channel_id=1, source_target_pairs={{0,1},{1,0},{2,3},{3,2},{4,5},{5,4},{6,7},{7,6},{8,9},{9,8},{10,11... | collective-permute-start | bytes 7077896 | tf_op jit(solution)/shard_map/ppermute | solution.py:500
  514.3 24.6 %collective-permute-start.27 = (f32[2,2,2,2,24,1536]{5,4,3,2,1,0:T(8,128)}, f32[2,2,2,2,24,1536]{5,4,3,2,1,0:T(8,128)}, u32[]{:S(2)}, u32[]{:S(2)}) collective-permute-start(f32[2,2,2,2,24,1536]{5,4,3,2,1,0:T(8,128)} %dynamic-slice_bitcast_fusion.1), channel_id=1, source_target_pairs={{0,1},{1,0},{2,3},{3,2},{4,5},{5,4},{6,7},{7,6},{8,9},{9,8},{10,11... | collective-permute-start | bytes 7077896 | tf_op jit(solution)/shard_map/ppermute | solution.py:500
  544.2 57.6 %collective-permute-start.28 = (f32[2,120,384]{2,1,0:T(8,128)S(1)}, f32[2,120,384]{2,1,0:T(8,128)S(1)}, u32[]{:S(2)}, u32[]{:S(2)}) collective-permute-start(f32[2,120,384]{2,1,0:T(8,128)S(1)} %dynamic-slice_bitcast_fusion.16), channel_id=1, source_target_pairs={{0,2},{1,3},{2,0},{3,1},{4,6},{5,7},{6,4},{7,5},{8,10},{9,11},{10,... | collective-permute-start | bytes 1105928 | tf_op jit(solution)/shard_map/ppermute | solution.py:500
  544.3 57.5 %collective-permute-start.29 = (f32[2,120,384]{2,1,0:T(8,128)S(1)}, f32[2,120,384]{2,1,0:T(8,128)S(1)}, u32[]{:S(2)}, u32[]{:S(2)}) collective-permute-start(f32[2,120,384]{2,1,0:T(8,128)S(1)} %dynamic-slice_bitcast_fusion.15), channel_id=1, source_target_pairs={{0,2},{1,3},{2,0},{3,1},{4,6},{5,7},{6,4},{7,5},{8,10},{9,11},{10,... | collective-permute-start | bytes 1105928 | tf_op jit(solution)/shard_map/ppermute | solution.py:500
  546.3 55.5 %collective-permute-start.30 = (f32[2,2,2,24,1536]{4,3,2,1,0:T(8,128)}, f32[2,2,2,24,1536]{4,3,2,1,0:T(8,128)}, u32[]{:S(2)}, u32[]{:S(2)}) collective-permute-start(f32[2,2,2,24,1536]{4,3,2,1,0:T(8,128)} %dynamic-slice_bitcast_fusion.6), channel_id=1, source_target_pairs={{0,8},{1,9},{2,10},{3,11},{4,12},{5,13},{6,14},{7,15},{8,0},{9,1},... | collective-permute-start | bytes 3538952 | tf_op jit(solution)/shard_map/ppermute | solution.py:500
  547.7 54.9 %collective-permute-start.31 = (f32[2,2,2,24,1536]{4,3,2,1,0:T(8,128)S(1)}, f32[2,2,2,24,1536]{4,3,2,1,0:T(8,128)}, u32[]{:S(2)}, u32[]{:S(2)}) collective-permute-start(f32[2,2,2,24,1536]{4,3,2,1,0:T(8,128)S(1)} %dynamic-slice_bitcast_fusion.5), channel_id=1, source_target_pairs={{0,16},{1,17},{2,18},{3,19},{4,20},{5,21},{6,22},{7,23},{8,24},{9,... | collective-permute-start | bytes 3538952 | tf_op jit(solution)/shard_map/ppermute | solution.py:500
  609.7 69.8 %collective-permute-start.36 = (f32[2,2,2,2,24,1536]{5,4,2,3,0,1:T(8,128)}, f32[2,2,2,2,24,1536]{5,4,2,3,0,1:T(8,128)}, u32[]{:S(2)}, u32[]{:S(2)}) collective-permute-start(f32[2,2,2,2,24,1536]{5,4,2,3,0,1:T(8,128)} %bitcast.396), channel_id=1, source_target_pairs={{0,1},{1,0},{2,3},{3,2},{4,5},{5,4},{6,7},{7,6},{8,9},{9,8},{10,11... | collective-permute-start | bytes 7077896 | tf_op jit(solution)/shard_map/ppermute | solution.py:500
  611.1 68.4 %collective-permute-start.37 = (f32[2,2,2,2,24,1536]{5,4,2,3,1,0:T(8,128)}, f32[2,2,2,2,24,1536]{5,4,2,3,1,0:T(8,128)}, u32[]{:S(2)}, u32[]{:S(2)}) collective-permute-start(f32[2,2,2,2,24,1536]{5,4,2,3,1,0:T(8,128)} %bitcast.395), channel_id=1, source_target_pairs={{0,1},{1,0},{2,3},{3,2},{4,5},{5,4},{6,7},{7,6},{8,9},{9,8},{10,11... | collective-permute-start | bytes 7077896 | tf_op jit(solution)/shard_map/ppermute | solution.py:500
  630.8 38.1 %collective-permute-start.32 = (f32[120,384]{1,0:T(8,128)S(1)}, f32[120,384]{1,0:T(8,128)S(1)}, u32[]{:S(2)}, u32[]{:S(2)}) collective-permute-start(f32[120,384]{1,0:T(8,128)S(1)} %copy-done.88), channel_id=1, source_target_pairs={{0,4},{1,5},{2,6},{3,7},{4,0},{5,1},{6,2},{7,3},{8,12},{9,13},{10,... | collective-permute-start | bytes 552968 | tf_op jit(solution)/shard_map/ppermute | solution.py:500
  634.8 44.7 %collective-permute-start.34 = (f32[2,2,24,1536]{3,2,1,0:T(8,128)}, f32[2,2,24,1536]{3,2,1,0:T(8,128)S(1)}, u32[]{:S(2)}, u32[]{:S(2)}) collective-permute-start(f32[2,2,24,1536]{3,2,1,0:T(8,128)} %dynamic-slice_bitcast_fusion.12), channel_id=1, source_target_pairs={{0,16},{1,17},{2,18},{3,19},{4,20},{5,21},{6,22},{7,23},{8,24},{9,... | collective-permute-start | bytes 1769480 | tf_op jit(solution)/shard_map/ppermute | solution.py:500
  636.0 43.5 %collective-permute-start.35 = (f32[2,2,24,1536]{3,2,1,0:T(8,128)S(1)}, f32[2,2,24,1536]{3,2,1,0:T(8,128)S(1)}, u32[]{:S(2)}, u32[]{:S(2)}) collective-permute-start(f32[2,2,24,1536]{3,2,1,0:T(8,128)S(1)} %copy-done.78), channel_id=1, source_target_pairs={{0,8},{1,9},{2,10},{3,11},{4,12},{5,13},{6,14},{7,15},{8,0},{9,1},... | collective-permute-start | bytes 1769480 | tf_op jit(solution)/shard_map/ppermute | solution.py:500
  669.5 10.0 %collective-permute-start.33 = (f32[120,384]{1,0:T(8,128)S(1)}, f32[120,384]{1,0:T(8,128)S(1)}, u32[]{:S(2)}, u32[]{:S(2)}) collective-permute-start(f32[120,384]{1,0:T(8,128)S(1)} %copy-done.87), channel_id=1, source_target_pairs={{0,4},{1,5},{2,6},{3,7},{4,0},{5,1},{6,2},{7,3},{8,12},{9,13},{10,... | collective-permute-start | bytes 552968 | tf_op jit(solution)/shard_map/ppermute | solution.py:500
  685.8 13.5 %collective-permute-start.38 = (f32[2,24,1536]{2,1,0:T(8,128)}, f32[2,24,1536]{2,1,0:T(8,128)}, u32[]{:S(2)}, u32[]{:S(2)}) collective-permute-start(f32[2,24,1536]{2,1,0:T(8,128)} %dynamic-slice_bitcast_fusion.18), channel_id=1, source_target_pairs={{0,2},{1,3},{2,0},{3,1},{4,6},{5,7},{6,4},{7,5},{8,10},{9,11},{10,... | collective-permute-start | bytes 884744 | tf_op jit(solution)/shard_map/ppermute | solution.py:500
  685.9 15.6 %collective-permute-start.39 = (f32[2,24,1536]{2,1,0:T(8,128)}, f32[2,24,1536]{2,1,0:T(8,128)}, u32[]{:S(2)}, u32[]{:S(2)}) collective-permute-start(f32[2,24,1536]{2,1,0:T(8,128)} %dynamic-slice_bitcast_fusion.17), channel_id=1, source_target_pairs={{0,2},{1,3},{2,0},{3,1},{4,6},{5,7},{6,4},{7,5},{8,10},{9,11},{10,... | collective-permute-start | bytes 884744 | tf_op jit(solution)/shard_map/ppermute | solution.py:500
  687.9 14.8 %collective-permute-start.40 = (bf16[2,2,2,24,1536]{4,3,1,2,0:T(8,128)(2,1)S(1)}, bf16[2,2,2,24,1536]{4,3,1,2,0:T(8,128)(2,1)}, u32[]{:S(2)}, u32[]{:S(2)}) collective-permute-start(bf16[2,2,2,24,1536]{4,3,1,2,0:T(8,128)(2,1)S(1)} %fusion.48), channel_id=1, source_target_pairs={{0,8},{1,9},{2,10},{3,11},{4,12},{5,13},{6,14},{7,15},{8,0},{9,1},... | collective-permute-start | bytes 1769480 | tf_op jit(solution)/shard_map/ppermute | solution.py:500
  689.6 14.5 %collective-permute-start.41 = (bf16[2,2,2,24,1536]{4,3,1,2,0:T(8,128)(2,1)S(1)}, bf16[2,2,2,24,1536]{4,3,1,2,0:T(8,128)(2,1)}, u32[]{:S(2)}, u32[]{:S(2)}) collective-permute-start(bf16[2,2,2,24,1536]{4,3,1,2,0:T(8,128)(2,1)S(1)} %fusion.49), channel_id=1, source_target_pairs={{0,16},{1,17},{2,18},{3,19},{4,20},{5,21},{6,22},{7,23},{8,24},{9,... | collective-permute-start | bytes 1769480 | tf_op jit(solution)/shard_map/ppermute | solution.py:500
  711.3 28.1 %collective-permute-start.42 = (f32[24,1536]{1,0:T(8,128)}, f32[24,1536]{1,0:T(8,128)}, u32[]{:S(2)}, u32[]{:S(2)}) collective-permute-start(f32[24,1536]{1,0:T(8,128)} %dynamic-slice_bitcast_fusion.24), channel_id=1, source_target_pairs={{0,4},{1,5},{2,6},{3,7},{4,0},{5,1},{6,2},{7,3},{8,12},{9,13},{10,... | collective-permute-start | bytes 442376 | tf_op jit(solution)/shard_map/ppermute | solution.py:500
  712.5 38.0 %collective-permute-start.44 = (bf16[2,2,24,1536]{3,2,0,1:T(8,128)(2,1)S(1)}, bf16[2,2,24,1536]{3,2,0,1:T(8,128)(2,1)}, u32[]{:S(2)}, u32[]{:S(2)}) collective-permute-start(bf16[2,2,24,1536]{3,2,0,1:T(8,128)(2,1)S(1)} %fusion.54), channel_id=1, source_target_pairs={{0,16},{1,17},{2,18},{3,19},{4,20},{5,21},{6,22},{7,23},{8,24},{9,... | collective-permute-start | bytes 884744 | tf_op jit(solution)/shard_map/ppermute | solution.py:500
  713.0 37.5 %collective-permute-start.45 = (bf16[2,2,24,1536]{3,2,0,1:T(8,128)(2,1)S(1)}, bf16[2,2,24,1536]{3,2,0,1:T(8,128)(2,1)}, u32[]{:S(2)}, u32[]{:S(2)}) collective-permute-start(bf16[2,2,24,1536]{3,2,0,1:T(8,128)(2,1)S(1)} %fusion.55), channel_id=1, source_target_pairs={{0,8},{1,9},{2,10},{3,11},{4,12},{5,13},{6,14},{7,15},{8,0},{9,1},... | collective-permute-start | bytes 884744 | tf_op jit(solution)/shard_map/ppermute | solution.py:500
  713.3 37.2 %collective-permute-start.46 = (f32[2,2,2,2,24,1152]{5,4,3,2,0,1:T(8,128)}, f32[2,2,2,2,24,1152]{5,4,3,2,0,1:T(8,128)}, u32[]{:S(2)}, u32[]{:S(2)}) collective-permute-start(f32[2,2,2,2,24,1152]{5,4,3,2,0,1:T(8,128)} %bitcast.398), channel_id=1, source_target_pairs={{0,1},{1,0},{2,3},{3,2},{4,5},{5,4},{6,7},{7,6},{8,9},{9,8},{10,11... | collective-permute-start | bytes 5308424 | tf_op jit(solution)/shard_map/ppermute | solution.py:500
  713.3 37.2 %collective-permute-start.47 = (f32[2,2,2,2,24,1152]{5,4,3,2,1,0:T(8,128)}, f32[2,2,2,2,24,1152]{5,4,3,2,1,0:T(8,128)}, u32[]{:S(2)}, u32[]{:S(2)}) collective-permute-start(f32[2,2,2,2,24,1152]{5,4,3,2,1,0:T(8,128)} %dynamic-slice_bitcast_fusion.2), channel_id=1, source_target_pairs={{0,1},{1,0},{2,3},{3,2},{4,5},{5,4},{6,7},{7,6},{8,9},{9,8},{10,11... | collective-permute-start | bytes 5308424 | tf_op jit(solution)/shard_map/ppermute | solution.py:500
  735.0 11.7 %all-to-all-start.5 = ((f32[32,1,336]{2,1,0:T(1,128)}), f32[32,1,336]{2,1,0:T(1,128)}, u32[]{:S(2)}, u32[]{:S(2)}) async-start(f32[32,1,336]{2,1,0:T(1,128)} %reshape.564), calls=%async_computation.5 | async-start | bytes 98304 | tf_op jit(solution)/shard_map/all_to_all | solution.py:760
  739.3 11.2 %collective-permute-start.43 = (f32[24,1536]{1,0:T(8,128)}, f32[24,1536]{1,0:T(8,128)}, u32[]{:S(2)}, u32[]{:S(2)}) collective-permute-start(f32[24,1536]{1,0:T(8,128)} %dynamic-slice_bitcast_fusion.23), channel_id=1, source_target_pairs={{0,4},{1,5},{2,6},{3,7},{4,0},{5,1},{6,2},{7,3},{8,12},{9,13},{10,... | collective-permute-start | bytes 442376 | tf_op jit(solution)/shard_map/ppermute | solution.py:500
  760.2 42.3 %collective-permute-start.50 = (f32[2,2,2,24,1152]{4,3,2,1,0:T(8,128)}, f32[2,2,2,24,1152]{4,3,2,1,0:T(8,128)}, u32[]{:S(2)}, u32[]{:S(2)}) collective-permute-start(f32[2,2,2,24,1152]{4,3,2,1,0:T(8,128)} %dynamic-slice_bitcast_fusion.8), channel_id=1, source_target_pairs={{0,8},{1,9},{2,10},{3,11},{4,12},{5,13},{6,14},{7,15},{8,0},{9,1},... | collective-permute-start | bytes 2654216 | tf_op jit(solution)/shard_map/ppermute | solution.py:500
  761.9 40.7 %collective-permute-start.51 = (f32[2,2,2,24,1152]{4,3,2,1,0:T(8,128)}, f32[2,2,2,24,1152]{4,3,2,1,0:T(8,128)}, u32[]{:S(2)}, u32[]{:S(2)}) collective-permute-start(f32[2,2,2,24,1152]{4,3,2,1,0:T(8,128)} %dynamic-slice_bitcast_fusion.7), channel_id=1, source_target_pairs={{0,16},{1,17},{2,18},{3,19},{4,20},{5,21},{6,22},{7,23},{8,24},{9,... | collective-permute-start | bytes 2654216 | tf_op jit(solution)/shard_map/ppermute | solution.py:500
  767.0 50.8 %all-to-all-start.4 = ((bf16[32,24,1024]{2,1,0:T(8,128)(2,1)}), bf16[32,24,1024]{2,1,0:T(8,128)(2,1)S(1)}, u32[]{:S(2)}, u32[]{:S(2)}) async-start(bf16[32,24,1024]{2,1,0:T(8,128)(2,1)} %bitcast.418), calls=%async_computation.4 | async-start | bytes 3145728 | tf_op jit(solution)/shard_map/all_to_all | solution.py:746
  770.1 29.7 %collective-permute-start.48 = (bf16[2,24,1536]{2,1,0:T(8,128)(2,1)}, bf16[2,24,1536]{2,1,0:T(8,128)(2,1)S(1)}, u32[]{:S(2)}, u32[]{:S(2)}) collective-permute-start(bf16[2,24,1536]{2,1,0:T(8,128)(2,1)} %fusion.64), channel_id=1, source_target_pairs={{0,2},{1,3},{2,0},{3,1},{4,6},{5,7},{6,4},{7,5},{8,10},{9,11},{10,... | collective-permute-start | bytes 442376 | tf_op jit(solution)/shard_map/ppermute | solution.py:500
  772.0 30.6 %collective-permute-start.49 = (bf16[2,24,1536]{2,1,0:T(8,128)(2,1)}, bf16[2,24,1536]{2,1,0:T(8,128)(2,1)S(1)}, u32[]{:S(2)}, u32[]{:S(2)}) collective-permute-start(bf16[2,24,1536]{2,1,0:T(8,128)(2,1)} %fusion.65), channel_id=1, source_target_pairs={{0,2},{1,3},{2,0},{3,1},{4,6},{5,7},{6,4},{7,5},{8,10},{9,11},{10,... | collective-permute-start | bytes 442376 | tf_op jit(solution)/shard_map/ppermute | solution.py:500
  808.6 107.2 %collective-permute-start.54 = (f32[2,2,24,1152]{3,2,1,0:T(8,128)}, f32[2,2,24,1152]{3,2,1,0:T(8,128)}, u32[]{:S(2)}, u32[]{:S(2)}) collective-permute-start(f32[2,2,24,1152]{3,2,1,0:T(8,128)} %dynamic-slice_bitcast_fusion.14), channel_id=1, source_target_pairs={{0,16},{1,17},{2,18},{3,19},{4,20},{5,21},{6,22},{7,23},{8,24},{9,... | collective-permute-start | bytes 1327112 | tf_op jit(solution)/shard_map/ppermute | solution.py:500
  810.3 105.5 %collective-permute-start.55 = (f32[2,2,24,1152]{3,2,1,0:T(8,128)}, f32[2,2,24,1152]{3,2,1,0:T(8,128)}, u32[]{:S(2)}, u32[]{:S(2)}) collective-permute-start(f32[2,2,24,1152]{3,2,1,0:T(8,128)} %dynamic-slice_bitcast_fusion.13), channel_id=1, source_target_pairs={{0,8},{1,9},{2,10},{3,11},{4,12},{5,13},{6,14},{7,15},{8,0},{9,1},... | collective-permute-start | bytes 1327112 | tf_op jit(solution)/shard_map/ppermute | solution.py:500
  813.4 102.4 %collective-permute-start.52 = (bf16[24,1536]{1,0:T(8,128)(2,1)}, bf16[24,1536]{1,0:T(8,128)(2,1)S(1)}, u32[]{:S(2)}, u32[]{:S(2)}) collective-permute-start(bf16[24,1536]{1,0:T(8,128)(2,1)} %fusion.70), channel_id=1, source_target_pairs={{0,4},{1,5},{2,6},{3,7},{4,0},{5,1},{6,2},{7,3},{8,12},{9,13},{10,... | collective-permute-start | bytes 221192 | tf_op jit(solution)/shard_map/ppermute | solution.py:500
  817.7 98.1 %collective-permute-start.53 = (bf16[24,1536]{1,0:T(8,128)(2,1)S(1)}, bf16[24,1536]{1,0:T(8,128)(2,1)S(1)}, u32[]{:S(2)}, u32[]{:S(2)}) collective-permute-start(bf16[24,1536]{1,0:T(8,128)(2,1)S(1)} %fusion.71), channel_id=1, source_target_pairs={{0,4},{1,5},{2,6},{3,7},{4,0},{5,1},{6,2},{7,3},{8,12},{9,13},{10,... | collective-permute-start | bytes 221192 | tf_op jit(solution)/shard_map/ppermute | solution.py:500
  (147 other events, 2053.1 us)
Sparse Core Ops, SparseCore 0:
  11.6 63.3 all-gather.3
  78.6 78.5 all-gather.5
  160.7 65.8 all-gather.7

commit v2 on v1

--- a/solution.py
+++ b/solution.py
@@ -77,21 +77,26 @@
 
     @pl.when(pl.program_id(0) == 0)
     def _():
-        spread = copies_matrix(width, half_type)
-        step = 3 * LANES if vocab % (3 * LANES) == 0 else LANES
-
-        def build(chunk, carry):
-            start = pl.multiple_of(chunk * step, LANES)
-            piece = table_ref[:, pl.ds(start, step)].astype(half_type)
-            rows_ref[pl.ds(start, step), :] = lax.dot_general(
-                piece, spread, (((0,), (0,)), ((), ())), preferred_element_type=full_type
-            )
+        chunks = vocab // LANES
+        many = 8
+        filler = jnp.zeros((pad - width, LANES), full_type)
+
+        def build(start):
+            piece = table_ref[:, pl.ds(start, LANES)].astype(half_type).astype(full_type)
+            tall = jnp.concatenate([piece, filler] * groups, 0) if pad > width else jnp.concatenate([piece] * groups, 0)
+            rows_ref[pl.ds(start, LANES), :] = jnp.transpose(tall)
+
+        def several(block, carry):
+            for inner in range(many):
+                build(pl.multiple_of((block * many + inner) * LANES, LANES))
             return carry
 
-        lax.fori_loop(0, vocab // step, build, 0)
+        lax.fori_loop(0, chunks // many, several, 0)
+        for rest in range(chunks // many * many, chunks):
+            build(rest * LANES)
 
     lane_group = lax.broadcasted_iota(jnp.int32, (1, LANES), 1) // pad
-    unroll = 8
+    unroll = 16
 
     def pick(block, carry):
         base = block * unroll
@@ -138,7 +143,7 @@
     return -(-vocab // (groups * LANES)) * LANES
 
 
-def scatter_kernel(places_ref, grad_ref, out_ref, square_ref, mask_ref, stage_ref, *sums):
+def scatter_kernel(places_ref, groups_ref, grad_ref, out_ref, square_ref, mask_ref, stage_ref, *sums):
     width, vocab = out_ref.shape
     runs, _, tokens = places_ref.shape
     pad, groups = lane_pack(width)
@@ -165,18 +170,19 @@
         stage_ref[run] = lax.dot_general(
             grad_ref[run], spread, (((0,), (0,)), ((), ())), preferred_element_type=full_type
         )
-    unroll = 4
+    unroll = 32
 
     def add(block, carry):
         base = block * unroll
         for inner in range(unroll):
+            rows = [pl.ds(places_ref[run, 0, base + inner], 1) for run in range(runs)]
+            new = [
+                sums[run][rows[run], :]
+                + stage_ref[run, pl.ds(base + inner, 1), :] * mask_ref[pl.ds(groups_ref[run, 0, base + inner], 1), :]
+                for run in range(runs)
+            ]
             for run in range(runs):
-                place = places_ref[run, 0, base + inner]
-                row = pl.ds(place >> shift, 1)
-                group = pl.ds(place & (groups - 1), 1)
-                sums[run][row, :] = (
-                    sums[run][row, :] + stage_ref[run, pl.ds(base + inner, 1), :] * mask_ref[group, :]
-                )
+                sums[run][rows[run], :] = new[run]
         return carry
 
     lax.fori_loop(0, tokens // unroll, add, 0)
@@ -213,6 +219,7 @@
         ),
         grid=(count // runs,),
         in_specs=[
+            pl.BlockSpec((runs, 1, tokens), lambda i: (i, 0, 0), memory_space=pltpu.SMEM),
             pl.BlockSpec((runs, 1, tokens), lambda i: (i, 0, 0), memory_space=pltpu.SMEM),
             pl.BlockSpec((runs, width, tokens), lambda i: (i, 0, 0)),
         ],
@@ -228,13 +235,13 @@
         compiler_params=pltpu.CompilerParams(
             dimension_semantics=("arbitrary",), vmem_limit_bytes=52 * 1024 * 1024
         ),
-    )(places, grads)
+    )(places[0], places[1], grads)
 
 
 def scatter_places(ids, width, vocab):
     _, groups = lane_pack(width)
     span = quarter(vocab, groups)
-    return (ids % span) * groups + ids // span
+    return (ids % span, ids // span)
 
 
 def turn_tables(row_length, head_width):
@@ -385,11 +392,15 @@
     )(queries, keys_all, values_all, grad_context, tables, segments[:, None, :], segments[:, :, None], logsum)
 
 
-def document_kernel(starts_ref, total_ref, in_ref, out_ref, sum_ref, turned_ref, spill_ref):
+def document_kernel(
+    starts_ref, total_ref, in_ref, out_ref, other_ref, own_ref, turned_ref, shift_ref, window_ref
+):
     micro_count, docs = starts_ref.shape[0], starts_ref.shape[1] - 1
     row_length = in_ref.shape[0] // micro_count
     reach = row_length // 2
     step = 16
+    half = other_ref.shape[0]
+    places = [(micro, doc) for micro in range(micro_count) for doc in range(docs)]
 
     def bounds(micro, doc):
         start, end = starts_ref[micro, doc], starts_ref[micro, doc + 1]
@@ -399,41 +410,52 @@
 
     @pl.when(pl.program_id(0) == 0)
     def _():
-        for micro in range(micro_count):
-            for doc in range(docs):
-                begin, end, base = bounds(micro, doc)
-                place = lax.broadcasted_iota(jnp.int32, (reach, in_ref.shape[1]), 0)
-                rows = in_ref[pl.ds(base, reach), :].astype(full_type)
-                kept = jnp.where((place >= begin) & (place < end), rows, 0.0)
-                turned_ref[micro * docs + doc] = jnp.transpose(kept).astype(half_type)
-
-                @pl.when(end > reach)
-                def _():
-                    place = reach + lax.broadcasted_iota(jnp.int32, (step, in_ref.shape[1]), 0)
-                    rows = in_ref[pl.ds(base + reach, step), :].astype(full_type)
-                    spill_ref[micro * docs + doc] = jnp.where(place < end, rows, 0.0).astype(half_type)
-
-    total = total_ref[0]
-    for micro in range(micro_count):
-        for doc in range(docs):
+        row = lax.broadcasted_iota(jnp.int32, (reach, in_ref.shape[1]), 0)
+        for place, (micro, doc) in enumerate(places):
             begin, end, base = bounds(micro, doc)
-            place = micro * docs + doc
-            first = place == 0
-
-            def add(block):
-                block = (block * total).astype(half_type).astype(full_type)
-                sum_ref[...] = block * block if first else sum_ref[...] + block * block
-
-            block = dot_of(turned_ref[place], out_ref[pl.ds(base, reach), :], ((1,), (0,)))
 
             @pl.when(end <= reach)
             def _():
-                add(block)
+                rows = in_ref[pl.ds(base, reach), :].astype(full_type)
+                kept = jnp.where((row >= begin) & (row < end), rows, 0.0)
+                turned_ref[place] = jnp.transpose(kept).astype(half_type)
 
             @pl.when(end > reach)
             def _():
-                more = dot_of(spill_ref[place], out_ref[pl.ds(base + reach, step), :], ((0,), (0,)))
-                add(block + more)
+                to = lax.broadcasted_iota(jnp.int32, (reach, reach + step), 0)
+                source = lax.broadcasted_iota(jnp.int32, (reach, reach + step), 1)
+                shift_ref[place] = jnp.where(to + begin == source, 1.0, 0.0).astype(half_type)
+                rows = dot_of(shift_ref[place], in_ref[pl.ds(base, reach + step), :], ((1,), (0,)))
+                kept = jnp.where(row < end - begin, rows, 0.0)
+                turned_ref[place] = jnp.transpose(kept).astype(half_type)
+
+    for place, (micro, doc) in enumerate(places):
+        begin, end, base = bounds(micro, doc)
+
+        @pl.when(end <= reach)
+        def _():
+            window_ref[place] = out_ref[pl.ds(base, reach), :]
+
+        @pl.when(end > reach)
+        def _():
+            window_ref[place] = dot_of(
+                shift_ref[place], out_ref[pl.ds(base, reach + step), :], ((1,), (0,))
+            ).astype(half_type)
+
+    total = total_ref[0]
+    parts = 2
+    rows = half // parts
+    for part in range(2 * parts):
+        found = None
+        for place in range(len(places)):
+            block = dot_of(
+                turned_ref[place, part * rows : (part + 1) * rows, :], window_ref[place], ((1,), (0,))
+            )
+            block = (block * total).astype(half_type).astype(full_type)
+            found = block * block if found is None else found + block * block
+        target = other_ref if part < parts else own_ref
+        start = (part % parts) * rows
+        target[start : start + rows, :] = found
 
 
 def document_squares(rot_in, rot_out, segments, total):
@@ -445,7 +467,7 @@
     starts = jnp.sum(segments[:, :, None] < slots[None, None, :], 1).astype(jnp.int32)
     return pl.pallas_call(
         document_kernel,
-        out_shape=jax.ShapeDtypeStruct((width, hidden), full_type),
+        out_shape=(jax.ShapeDtypeStruct((width // 2, hidden), full_type),) * 2,
         grid=(hidden // tile,),
         in_specs=[
             pl.BlockSpec(memory_space=pltpu.SMEM),
@@ -453,10 +475,11 @@
             pl.BlockSpec((tokens, width), lambda i: (0, 0)),
             pl.BlockSpec((tokens, tile), lambda i: (0, i)),
         ],
-        out_specs=pl.BlockSpec((width, tile), lambda i: (0, i)),
+        out_specs=(pl.BlockSpec((width // 2, tile), lambda i: (0, i)),) * 2,
         scratch_shapes=[
             pltpu.VMEM((micro_count * DOCS, width, row_length // 2), half_type),
-            pltpu.VMEM((micro_count * DOCS, 16, width), half_type),
+            pltpu.VMEM((micro_count * DOCS, row_length // 2, row_length // 2 + 16), half_type),
+            pltpu.VMEM((micro_count * DOCS, row_length // 2, tile), half_type),
         ],
         compiler_params=pltpu.CompilerParams(
             dimension_semantics=("arbitrary",), vmem_limit_bytes=40 * 1024 * 1024
@@ -472,32 +495,91 @@
 
 
 class Stream:
-    def __init__(self, chunks, order, wire, relative=False):
-        self.count = chunks.shape[0]
-        bits = self.count.bit_length() - 1
-        self.held = chunks.reshape((2,) * bits + chunks.shape[1:])
-        self.left = list(order) if relative else list(range(bits - 1, -1, -1))
-        self.relative = relative
+    def __init__(self, chunks, order, left, wire, relative=False):
+        self.held = chunks.reshape((2,) * len(order) + chunks.shape[1:])
+        self.left = list(left)
         self.order = list(order)
         self.wire = wire
+        self.relative = relative
         self.sent = self.kept = self.got = None
 
     def land(self, arrived):
         self.held = self.kept + arrived.astype(full_type)
         self.got = None
+        return [self]
 
     def split(self):
         bit = self.order[0]
         axis = self.left.index(bit)
         mine = 0 if self.relative else (lax.axis_index(AXES) >> bit) & 1
-        self.sent = lax.dynamic_index_in_dim(self.held, 1 - mine, axis, keepdims=False)
+        self.sent = lax.dynamic_index_in_dim(self.held, 1 - mine, axis, keepdims=False).astype(self.wire)
         self.kept = lax.dynamic_index_in_dim(self.held, mine, axis, keepdims=False)
-        if bit != 0:
-            self.sent = self.sent.astype(self.wire)
         self.left.pop(axis)
 
     def send(self, ready):
-        self.got = lax.ppermute(ready, AXES, partner_pairs(self.count, self.order.pop(0)))
+        self.got = lax.ppermute(ready, AXES, partner_pairs(lax.axis_size(AXES), self.order.pop(0)))
+
+
+class FirstStep:
+    def __init__(self, other, own, rows, wire):
+        self.sent, self.kept, self.rows, self.wire = other, own, rows, wire
+        self.order = [0]
+        self.got = None
+        self.streams = None
+
+    def land(self, arrived):
+        held = (self.kept + arrived).reshape(-1, self.rows, self.kept.shape[1])
+        half = held.shape[2] // 2
+        bits = lax.axis_size(AXES).bit_length() - 1
+        order_a, order_b = link_orders(bits)
+        left = range(bits - 1, 0, -1)
+        self.got = None
+        self.streams = [
+            Stream(held[:, :, :half], order_a[1:], left, self.wire),
+            Stream(held[:, :, half:], order_b[1:], left, self.wire),
+        ]
+        return self.streams
+
+    def split(self):
+        pass
+
+    def send(self, ready):
+        self.order = []
+        self.got = lax.ppermute(ready, AXES, partner_pairs(lax.axis_size(AXES), 0))
+
+    def finished(self):
+        return jnp.concatenate([stream.held for stream in self.streams], 1)
+
+
+def advance(anchor, live):
+    flying = [stream for stream in live if stream.got is not None]
+    anchor, landed = lax.optimization_barrier((anchor, [stream.got for stream in flying]))
+    going = [stream for stream in live if stream.got is None]
+    for stream, arrived in zip(flying, landed):
+        going.extend(stream.land(arrived))
+    going = [stream for stream in going if stream.order]
+    for stream in going:
+        stream.split()
+    anchor, ready = lax.optimization_barrier((anchor, [stream.sent for stream in going]))
+    for stream, block in zip(going, ready):
+        stream.send(block)
+    live[:] = going
+    return anchor
+
+
+def run_all(anchor, live):
+    while live:
+        anchor = advance(anchor, live)
+    return anchor
+
+
+def pair_first(width, rows, place):
+    to = lax.broadcasted_iota(jnp.int32, (width, width), 1)
+    source = lax.broadcasted_iota(jnp.int32, (width, width), 0)
+    core = jnp.where(to < width // 2, 1 - (place & 1), place & 1)
+    inside = to % (width // 2)
+    wanted = (inside // rows) * (2 * rows) + core * rows + inside % rows
+    return (source == wanted).astype(half_type)
 
 
 def link_orders(bits):
@@ -537,38 +619,6 @@
             arrived = lax.ppermute(held[m], AXES, partner_pairs(count, order[-1 - step]))
             held[m] = jnp.concatenate([held[m], arrived], 0)
     return held
-
-
-def streams_of(full, count, wire=full_type):
-    rows = full.shape[0] // count
-    half = full.shape[1] // 2
-    chunks = full.reshape(count, rows, full.shape[1])
-    order_a, order_b = link_orders(count.bit_length() - 1)
-    return [Stream(chunks[:, :, :half], order_a, wire), Stream(chunks[:, :, half:], order_b, wire)]
-
-
-def advance(anchor, streams):
-    flying = [stream for stream in streams if stream.got is not None]
-    anchor, landed = lax.optimization_barrier((anchor, [stream.got for stream in flying]))
-    for stream, arrived in zip(flying, landed):
-        stream.land(arrived)
-    going = [stream for stream in streams if stream.order]
-    for stream in going:
-        stream.split()
-    anchor, ready = lax.optimization_barrier((anchor, [stream.sent for stream in going]))
-    for stream, block in zip(going, ready):
-        stream.send(block)
-    return anchor
-
-
-def finished(streams):
-    return jnp.concatenate([stream.held for stream in streams], 1)
-
-
-def run_all(anchor, streams):
-    while any(stream.order or stream.got is not None for stream in streams):
-        anchor = advance(anchor, streams)
-    return anchor
 
 
 def shared_by_all(own, count):
@@ -626,10 +676,22 @@
     hidden = proj_up.shape[1]
     head_width = width // HEADS
 
-    weight_in = lax.all_gather(proj_in.astype(half_type), AXES, axis=0, tiled=True)
-    weight_up = lax.all_gather(proj_up.astype(half_type), AXES, axis=0, tiled=True)
+    place = lax.axis_index(AXES)
+    flat_ids = jnp.transpose(token_ids, (1, 0, 2)).reshape(-1)
+    ids_by_run = flat_ids.reshape(count, 1, tokens)
+    columns = gather_features(embed_in, ids_by_run)
+    columns, vector_half = lax.optimization_barrier((columns, vector_params.astype(half_type)))
+    arrived = lax.all_to_all(columns, AXES, split_axis=0, concat_axis=0, tiled=True)
+    embedded = arrived.reshape(width, tokens).T.astype(full_type)
+    places = scatter_places(ids_by_run, own_width, vocab)
+
+    both = jnp.concatenate([proj_in.astype(half_type), proj_up.astype(half_type)], 1)
+    both = lax.all_gather(both, AXES, axis=0, tiled=True)
+    weight_in, weight_up = both[:, : 3 * width], both[:, 3 * width :]
     weight_mix = lax.all_gather(proj_mix.astype(half_type), AXES, axis=0, tiled=True)
-    vector = shared_by_all(vector_params.astype(half_type), count).reshape(-1).astype(full_type)
+    vector = shared_by_all(vector_half, count).reshape(-1).astype(full_type)
+    pairing = pair_first(width, own_width, place)
+    basis_paired = jnp.dot(basis_in, pairing, preferred_element_type=full_type).astype(half_type)
     (
         bias_in,
         bias_up,
@@ -642,12 +704,6 @@
         gain_last,
     ) = split_vector(vector, width, hidden)
 
-    flat_ids = jnp.transpose(token_ids, (1, 0, 2)).reshape(-1)
-    ids_by_run = flat_ids.reshape(count, 1, tokens)
-    columns = gather_features(embed_in, ids_by_run)
-    arrived = lax.all_to_all(columns, AXES, split_axis=0, concat_axis=0, tiled=True)
-    embedded = arrived.reshape(width, tokens).T.astype(full_type)
-    places = scatter_places(ids_by_run, own_width, vocab)
     segments = segment_ids[:, 0]
     picks = loss_positions[:, 0] + row_length * jnp.arange(micro_count)[:, None]
     picks = picks.reshape(-1)
@@ -668,7 +724,6 @@
 
     bits = count.bit_length() - 1
     orders = link_orders(bits)
-    place = lax.axis_index(AXES)
     picked = picked.reshape(micro_count, pick_count, width)
     gathered = jnp.stack(gather_trees(picked, orders)).reshape(-1, width)
     table_out = embed_out.astype(half_type)
@@ -700,44 +755,51 @@
     ).astype(half_type)
     back = jnp.dot(grad_logits, table_out, preferred_element_type=full_type)
     back = back.reshape(micro_count, count, pick_count, width)
-    pick_streams = [Stream(back[m], orders[m], full_type, relative=True) for m in range(micro_count)]
-    grad_logits = advance(grad_logits, pick_streams)
+    pick_streams = [
+        Stream(back[m], orders[m], orders[m], full_type, relative=True) for m in range(micro_count)
+    ]
+    live = list(pick_streams)
+    grad_logits = advance(grad_logits, live)
     grad_out_table = jnp.einsum("rv,rd->vd", grad_logits, gathered, preferred_element_type=full_type)
-    run_all(jnp.zeros((), full_type), pick_streams)
+    out_squares = jnp.sum(grad_out_table * grad_out_table)
+    second_paired, out_squares = advance((second_in, out_squares), live)
+    rot_in = jnp.dot(second_paired, basis_paired, preferred_element_type=full_type).astype(half_type)
+    first_turned = lax.dot_general(
+        pairing, first_in, (((0,), (1,)), ((), ())), preferred_element_type=full_type
+    ).astype(half_type)
+    rot_in, first_turned = advance((rot_in, first_turned), live)
+    run_all(jnp.zeros((), full_type), live)
     grad_picked = jnp.concatenate([stream.held for stream in pick_streams], 0)
 
     grad_final = jnp.zeros((tokens, width), full_type).at[picks].add(grad_picked)
     grad_residual = norm_back(grad_final * gain_last, normed_last, inv_last)
     grad_branch = grad_residual.astype(half_type)
     grad_mix = jnp.einsum("sa,sb->ab", joined, grad_branch, preferred_element_type=full_type)
-    mix_streams = streams_of(grad_mix, count)
-    grad_branch = advance(grad_branch, mix_streams)
+    own_mix = lax.psum_scatter(grad_mix, AXES, scatter_dimension=0, tiled=True)
     grad_joined = jnp.einsum("sb,ab->sa", grad_branch, weight_mix, preferred_element_type=full_type)
     grad_context = (
         grad_joined[:, :width].astype(half_type)
     )
     grad_hidden = (grad_joined[:, width:] * gelu_slope(hidden_pre)).astype(half_type)
-    grad_hidden = advance(grad_hidden, mix_streams)
     grad_up = jnp.einsum("sa,sb->ab", second_in, grad_hidden, preferred_element_type=full_type)
     grad_second = jnp.einsum("sb,ab->sa", grad_hidden, weight_up, preferred_element_type=full_type)
-    up_streams = streams_of(grad_up, count)
-    (grad_hidden, grad_second) = advance((grad_hidden, grad_second), mix_streams + up_streams)
-
-    rot_in = jnp.dot(second_in, basis_in, preferred_element_type=full_type).astype(half_type)
+    own_up = lax.psum_scatter(grad_up, AXES, scatter_dimension=0, tiled=True)
+
     rot_out = jnp.dot(grad_hidden, basis_out, preferred_element_type=full_type).astype(half_type)
-    (rot_in, rot_out) = advance((rot_in, rot_out), mix_streams + up_streams)
-    scale_sum = document_squares(rot_in, rot_out, segments, total)
-    scale_streams = streams_of(scale_sum, count, half_type)
-    grad_context = advance(grad_context, mix_streams + up_streams + scale_streams)
-
+    scale_other, scale_own = document_squares(rot_in, rot_out, segments, total)
+    scale_step = FirstStep(scale_other, scale_own, own_width, half_type)
+    live = [scale_step]
+    grad_context = advance(grad_context, live)
     grad_parts = attention_backward(
         queries, keys_all, values_all, grad_context, logsum, tables, segments
     )
     grad_mixed = jnp.concatenate([grad_parts[0], grad_parts[1], grad_parts[2]], 1)
-    grad_mixed = advance(grad_mixed, mix_streams + up_streams + scale_streams)
-    grad_in = jnp.einsum("sa,sb->ab", first_in, grad_mixed, preferred_element_type=full_type)
-    in_streams = streams_of(grad_in, count)
-    grad_mixed = advance(grad_mixed, up_streams + scale_streams + in_streams)
+    grad_mixed = advance(grad_mixed, live)
+    in_other = jnp.dot(first_turned[: width // 2], grad_mixed, preferred_element_type=full_type)
+    in_own = jnp.dot(first_turned[width // 2 :], grad_mixed, preferred_element_type=full_type)
+    in_step = FirstStep(in_other, in_own, own_width, full_type)
+    live.append(in_step)
+    grad_mixed = advance(grad_mixed, live)
     grad_first = jnp.einsum("sb,ab->sa", grad_mixed, weight_in, preferred_element_type=full_type)
     grad_embedded = grad_residual + norm_back(
         grad_first * gain_first + grad_second * gain_second, normed, inv_std
@@ -757,22 +819,22 @@
             jnp.sum(grad_final * normed_last, 0),
         ]
     )
-    vector_parts = lax.all_to_all(
-        vector_grad.reshape(count, 1, -1), AXES, split_axis=0, concat_axis=0, tiled=True
-    )
-    own_vector = jnp.sum(vector_parts, (0, 1))
-    late = mix_streams + up_streams + scale_streams + in_streams
-    own_vector = advance(own_vector, late)
-    own_vector = advance(own_vector, late)
-    returned, own_vector = lax.optimization_barrier((returned, own_vector))
+    vector_grad = advance(vector_grad, live)
+    vector_grad = advance(vector_grad, live)
+    returned, vector_grad = lax.optimization_barrier((returned, vector_grad))
+    own_vector = jnp.sum(
+        lax.all_to_all(
+            vector_grad.reshape(count, 1, -1), AXES, split_axis=0, concat_axis=0, tiled=True
+        ),
+        (0, 1),
+    )
     grad_in_table, in_squares = scatter_features(returned, places, vocab)
-    in_squares = run_all(in_squares, late)
-    own_mix = finished(mix_streams)
-    own_up = finished(up_streams)
-    own_in = finished(in_streams)
-    eigen_scales = finished(scale_streams) / float(micro_count * count * DOCS)
+    in_squares = run_all(in_squares, live)
+    own_in = in_step.finished()
+    eigen_scales = scale_step.finished() / float(micro_count * count * DOCS)
     grads = (grad_in_table, grad_out_table, own_in, own_up, own_mix, own_vector)
-    squares = jnp.sum(in_squares) + sum((jnp.sum(gradient * gradient) for gradient in grads[1:]))
+    squares = jnp.sum(in_squares) + out_squares
+    squares = squares + sum((jnp.sum(gradient * gradient) for gradient in grads[2:]))
     both = jnp.sum(shared_by_all(jnp.stack([squares, loss_part])[None], count), (0, 1))
     grad_norm = jnp.sqrt(both[0])
     loss_value = both[1]

time: 1000 us -> 799 us (0.80)
  local copies, waits for them, and re-layouts: 122 us -> 56.1 us
  Pallas kernels: 257 us -> 195 us
  other arithmetic: 148 us -> 116 us
  starting transfers between devices: 96.9 us -> 66.5 us
  waiting for transfers between devices: 215 us -> 190 us
  matrix products: 129 us -> 141 us
    add x50 -> x26, other arithmetic: 43.8 us -> 11.1 us  [land(): self.held = self.kept + arrived.astype(full_type)]
    ppermute x50 -> x28, starting transfers between devices: 54.2 us -> 28.6 us  [the longest x26 28.6 us: send(): lax.ppermute(ready, AXES, partner_pairs(lax.axis_size(AXES), self.order.p...]
    pallas_call x1, Pallas kernels: 64.5 us -> 40.6 us  [gather_features(): pl.pallas_call(gather_kernel, out_shape=jax.ShapeDtypeStruct((count, widt...]
    pallas_call x1, Pallas kernels: 41.8 us -> 21.3 us  [document_squares(): pl.pallas_call(document_kernel, out_shape=(jax.ShapeDtypeStruct((width //...]
    ppermute x50 -> x28, waiting for transfers between devices: 106 us -> 85.7 us  [the longest x26 85.7 us: send(): lax.ppermute(ready, AXES, partner_pairs(lax.axis_size(AXES), self.order.p...]
    slice x4 -> x2, local copies, waits for them, and re-layouts: 19.6 us -> 0.59 us  [land(): held[:, :, half:]]
    all_to_all x1, waiting for transfers between devices: 0.01 us -> 18.5 us  [per_device(): lax.all_to_all(sending, AXES, split_axis=0, concat_axis=0, tiled=True)]
    pallas_call x1, Pallas kernels: 97.4 us -> 79.1 us  [scatter_features(): pl.pallas_call(scatter_kernel, out_shape=(jax.ShapeDtypeStruct((width, vo...]
  transfers between devices with their start and end apart: 70 -> 49, of which waited for: 39 -> 32; matrix products, arithmetic and copies ran while one was open for 20% -> 19% of each run, Pallas kernels for 26% -> 25%
where the time goes in v2:
time: 799 us; the launch traced here: 789 us
  Pallas kernels  195 us (24%)
  waiting for transfers between devices  190 us (24%)
  matrix products  141 us (18%)
  other arithmetic  116 us (15%)
  starting transfers between devices  66.5 us (8%)
  local copies, waits for them, and re-layouts  56.1 us (7%)
  between operations  24 us (3%)
    ppermute x26, waiting for transfers between devices, send(): lax.ppermute(ready, AXES, partner_pairs(lax.axis_size(AXES), self.order.p...  85.7 us
    pallas_call x1, Pallas kernels, scatter_features(): pl.pallas_call(scatter_kernel, out_shape=(jax.ShapeDtypeStruct((width, vo...  79.1 us
    pallas_call x1, Pallas kernels, gather_features(): pl.pallas_call(gather_kernel, out_shape=jax.ShapeDtypeStruct((count, widt...  40.6 us
    all_to_all x1, waiting for transfers between devices, per_device(): lax.all_to_all(columns, AXES, split_axis=0, concat_axis=0, tiled=True)  40.3 us
    pallas_call x1, Pallas kernels, attention_backward(): pl.pallas_call(backward_kernel, out_shape=jax.ShapeDtypeStruct((3, tokens...  32.7 us
    ppermute x26, starting transfers between devices, send(): lax.ppermute(ready, AXES, partner_pairs(lax.axis_size(AXES), self.order.p...  28.6 us
    dot_general x1, matrix products, per_device(): jnp.dot(grad_hidden, basis_out, preferred_element_type=full_type)  26.5 us
    unnamed x213, local copies, waits for them, and re-layouts  25.9 us
  transfers between devices with their start and end apart: 49, of which 32 were waited for; matrix products, arithmetic and copies ran while one was open for 19% of the time, Pallas kernels for 25%

profile of v2, /device:TPU:0, one launch (start us, length us, event | category | flops | bytes accessed | tf_op | source)
XLA Modules:
  0.0 788.6 jit_solution(4614526173681692698)
XLA Ops:
  16.1 40.6 %shard_map.409 = bf16[32,24,1024]{2,1,0:T(8,128)(2,1)} custom-call(s32[32,1,1024]{2,1,0:T(1,128)S(1)} %reshape_reshape.3.ids_ref, f32[24,50304]{1,0:T(8,128)S(1)} %copy-done.2), custom_call_target="tpu_custom_call" | custom-call | tf_op jit(solution)/shard_map/pallas_call | solution.py:123
  58.7 7.3 all-to-all-start.1
  68.0 5.6 all-to-all-done.1
  73.6 3.4 all-to-all-start
  84.4 40.3 %all-to-all-done = bf16[32,24,1024]{2,1,0:T(8,128)(2,1)} async-done(((bf16[32,24,1024]{2,1,0:T(8,128)(2,1)}), bf16[32,24,1024]{2,1,0:T(8,128)(2,1)}, u32[]{:S(2)}, u32[]{:S(2)}) %all-to-all-start) | async-done | bytes 1572896 | tf_op jit(solution)/shard_map/all_to_all | solution.py:684
  131.6 10.4 %convolution_add_fusion.query_in.key_in.value_in = f32[1024,2304]{1,0:T(8,128)} fusion(bf16[1024,768]{0,1:T(8,128)(2,1)} %get-tuple-element.256, f32[2304]{0:T(1024)S(1)} %slice.181, bf16[768,5376]{1,0:T(8,128)(2,1)} %all-gather.3.cloned.1.call-done), kind=kOutput, calls=%fused_computation.23 | convolution fusion | flops 3626237952 | bytes 14558208 | tf_op jit(solution)/shard_map/dot_general | solution.py:714
  142.0 21.3 %shard_map.410 = (bf16[1024,768]{1,0:T(8,128)(2,1)S(1)}, bf16[1024,768]{1,0:T(8,128)(2,1)S(1)}, bf16[1024,768]{1,0:T(8,128)(2,1)S(1)}, bf16[1024,768]{1,0:T(8,128)(2,1)S(1)}, f32[2,6,2,512]{3,2,1,0:T(2,128)S(1)}) custom-call(f32[1024,2304]{1,0:T(8,128)} %convolution_add_fusion.query_in.key_in.value_in, ...), custom_call_target="tpu_custom_call" | custom-call | tf_op jit(solution)/shard_map/pallas_call | solution.py:329
  167.9 10.1 %multiply_convert_fusion = (bf16[1024,3072]{1,0:T(8,128)(2,1)}, f32[1024,3072]{1,0:T(8,128)}) fusion(f32[3072]{0:T(1024)S(1)} %slice.185, bf16[1024,768]{0,1:T(8,128)(2,1)S(1)} %copy-done.34, bf16[768,5376]{1,0:T(8,128)(2,1)S(1)} %bitcast.320), kind=kOutput, calls=%fused_computation.17 | convolution fusion | flops 4850712576 | bytes 25178112 | tf_op jit(solution)/shard_map/dot_general | solution.py:717
  178.0 11.2 %fusion.147 = (f32[1024]{0:T(1024)S(1)}, f32[1024,768]{0,1:T(8,128)S(1)}) fusion(f32[768]{0:T(1024)S(1)} %get-tuple-element.293, bf16[3840,768]{1,0:T(8,128)(2,1)} %all-gather.5.cloned.1.call-done, bf16[1024,3072]{1,0:T(8,128)(2,1)} %get-tuple-element.311, bf16[1024,768]{1,0:T(8,128)(2,1)} %copy-done.18, bf16[32,24,1024]{2,1,0:T(8,128)(2,1)} %all-to-all-done), kind=kOutput, calls=%fused_computation.372 | convolution fusion | flops 6058671104 | bytes 18488320 | tf_op jit(solution)/shard_map/dot_general | solution.py:720
  217.3 5.4 collective-permute-done.3
  227.5 8.3 %fusion.148 = (f32[2048]{0:T(1024)S(1)}, f32[2048,1572]{0,1:T(8,128)}) fusion(bf16[2048,768]{1,0:T(8,128)(2,1)S(1)} %bitcast.290, f32[1572,768]{1,0:T(8,128)S(1)} %bitcast.287), kind=kOutput, calls=%fused_computation.373 | convolution fusion | flops 4949509120 | bytes 20860928 | tf_op jit(solution)/shard_map/rd,vd->rv/dot_general | solution.py:735
  235.9 6.8 exponential_reduce_fusion
  247.7 6.5 all-to-all-done.2
  258.8 6.9 all-to-all-done.3
  267.5 6.9 fusion.3
  274.4 9.0 %fusion.55 = f32[2048,768]{1,0:T(8,128)S(1)} fusion(bf16[2048,1572]{0,1:T(8,128)(2,1)S(1)} %fusion.3, f32[1572,768]{1,0:T(8,128)} %param.35), kind=kOutput, calls=%fused_computation.99 | convolution fusion | flops 4946291712 | bytes 17559552 | tf_op jit(solution)/shard_map/dot_general | solution.py:756
  287.4 7.9 %multiply_reduce_fusion = (f32[]{:T(128)}, f32[1572,768]{1,0:T(8,128)}) fusion(bf16[2048,1572]{0,1:T(8,128)(2,1)S(1)} %fusion.3, bf16[2048,768]{1,0:T(8,128)(2,1)S(1)} %bitcast.291), kind=kOutput, calls=%fused_computation.30 | convolution fusion | flops 4947499008 | bytes 14413828 | tf_op jit(solution)/shard_map/rv,rd->vd/dot_general | solution.py:763
  300.0 5.2 convolution_convert_fusion.2.in_ref
  305.2 13.3 %collective-permute-done.12 = f32[2,2,2,32,768]{4,3,2,1,0:T(8,128)} collective-permute-done((f32[2,2,2,32,768]{4,3,2,1,0:T(8,128)}, f32[2,2,2,32,768]{4,3,2,1,0:T(8,128)}, u32[]{:S(2)}, u32[]{:S(2)}) %collective-permute-start.12) | collective-permute-done | bytes 786464 | tf_op jit(solution)/shard_map/ppermute | solution.py:520
  323.8 7.7 collective-permute-done.14
  334.0 4.4 collective-permute-done.16
  343.7 4.7 collective-permute-done.18
  352.4 3.9 copy.206
  356.4 4.6 multiply_reduce_fusion.1
  364.3 10.0 %fusion.67 = f32[1024,3840]{1,0:T(8,128)S(1)} fusion(bf16[3840,768]{1,0:T(8,128)(2,1)} %all-gather.5.cloned.1.call-done, f32[1024,768]{0,1:T(8,128)} %get-tuple-element.241), kind=kOutput, calls=%fused_computation.124 | convolution fusion | flops 6040584192 | bytes 24772608 | tf_op jit(solution)/shard_map/sb,ab->sa/dot_general | solution.py:779
  374.3 13.0 %convert_reduce_fusion = (f32[3072]{0:T(1024)S(1)}, bf16[1024,3072]{1,0:T(8,128)(2,1)S(1)}) fusion(f32[1024,3072]{1,0:T(8,128)} %get-tuple-element.312, f32[3072]{0:T(1024)S(1)} %copy-done.63, f32[1024,3840]{1,0:T(8,128)S(1)} %fusion.67), kind=kLoop, calls=%fused_computation.16 | loop fusion | flops 40891392 | bytes 31481856 | tf_op jit(solution)/shard_map/reduce_sum | solution.py:812
  390.0 7.4 fusion.149
  399.8 26.5 %convolution_convert_fusion.out_ref = bf16[1024,3072]{1,0:T(8,128)(2,1)} fusion(bf16[1024,3072]{1,0:T(8,128)(2,1)} %copy-done.27, bf16[3072,3072]{1,0:T(8,128)(2,1)} %param.51), kind=kOutput, calls=%fused_computation.24 | convolution fusion | flops 19330498560 | bytes 31457280 | tf_op jit(solution)/shard_map/dot_general | solution.py:788
  426.3 21.3 %shard_map.411 = (f32[384,3072]{1,0:T(8,128)}, f32[384,3072]{1,0:T(8,128)S(1)}) custom-call(s32[2,5]{1,0:T(2,128)S(1)} %copy.207.starts_ref, f32[1]{0:T(128)} %bitcast.58.total_ref, bf16[1024,768]{1,0:T(8,128)(2,1)S(1)} %copy-done.6, bf16[1024,3072]{1,0:T(8,128)(2,1)} %convolution_convert_fusion.out_ref), custom_call_target="tpu_custom_call" | custom-call | tf_op jit(solution)/shard_map/pallas_call | solution.py:468
  452.7 12.6 %fusion.10 = f32[3840,768]{1,0:T(8,128)} fusion(bf16[1024,3072]{1,0:T(8,128)(2,1)} %get-tuple-element.311, bf16[1024,768]{1,0:T(8,128)(2,1)} %copy-done.18, f32[1024,768]{0,1:T(8,128)} %get-tuple-element.241), kind=kOutput, calls=%fused_computation.25 | convolution fusion | flops 6056312832 | bytes 22806528 | tf_op jit(solution)/shard_map/sa,sb->ab/dot_general | solution.py:777
  470.6 32.7 %shard_map.412 = bf16[3,1024,768]{2,1,0:T(8,128)(2,1)S(1)} custom-call(bf16[1024,768]{1,0:T(8,128)(2,1)S(1)} %copy-done.8, bf16[1024,768]{1,0:T(8,128)(2,1)S(1)} %copy-done.10, bf16[1024,768]{1,0:T(8,128)(2,1)S(1)} %copy-done.12, bf16[1024,768]{1,0:T(8,128)(2,1)S(1)} %slice.223.grad_ref, f32[3,512,128]{2,1,0:T(8,128)S(1)} %pad_maximum_fusion.7.tables_ref, ...), custom_call_target="tpu_custom_call" | custom-call | tf_op jit(solution)/shard_map/pallas_call | solution.py:382
  510.0 5.4 collective-permute-start.22
  517.4 3.8 fusion.64
  521.2 6.7 collective-permute-done.21
  534.6 5.5 fusion.43
  540.2 8.8 %fusion.128 = (f32[1024]{0:T(1024)S(1)}, f32[1024]{0:T(1024)S(1)}, f32[768]{0:T(1024)S(1)}, f32[768]{0:T(1024)S(1)}, f32[768]{0:T(1024)S(1)}, /*index=5*/f32[768]{0:T(1024)S(1)}, f32[1024,768]{0,1:T(8,128)S(1)}) fusion(f32[1024]{0:T(1024)S(1)} %copy-done.66, f32[1024]{0:T(1024)S(1)} %copy-done.57, bf16[32,24,1024]{2,1,0:T(8,128)(2,1)} %all-to-all-done, ...), kind=kOutput, calls=%fused_computation.360 | convolution fusion | flops 4843628544 | bytes 18911232 | tf_op jit(solution)/shard_map/sb,ab->sa/dot_general | solution.py:785
  557.4 3.7 fusion.38
  564.3 18.6 %collective-permute-done.26 = f32[2,2,2,24,1152]{4,3,2,1,0:T(8,128)S(1)} collective-permute-done((f32[2,2,2,24,1152]{4,3,2,1,0:T(8,128)}, f32[2,2,2,24,1152]{4,3,2,1,0:T(8,128)S(1)}, u32[]{:S(2)}, u32[]{:S(2)}) %collective-permute-start.26) | collective-permute-done | bytes 884768 | tf_op jit(solution)/shard_map/ppermute | solution.py:520
  583.8 6.0 collective-permute-done.27
  597.7 18.5 %all-to-all-done.4.grad_ref = bf16[32,24,1024]{2,1,0:T(8,128)(2,1)S(1)} async-done(((bf16[32,24,1024]{2,1,0:T(8,128)(2,1)}), bf16[32,24,1024]{2,1,0:T(8,128)(2,1)S(1)}, u32[]{:S(2)}, u32[]{:S(2)}) %all-to-all-start.4) | async-done | bytes 1572896 | tf_op jit(solution)/shard_map/all_to_all | solution.py:808
  625.4 79.1 %shard_map.413 = (f32[24,50304]{1,0:T(8,128)}, f32[8,128]{1,0:T(8,128)S(1)}) custom-call(s32[32,1,1024]{2,1,0:T(1,128)S(1)} %get-tuple-element.274.places_ref, s32[32,1,1024]{2,1,0:T(1,128)S(1)} %get-tuple-element.273.groups_ref, bf16[32,24,1024]{2,1,0:T(8,128)(2,1)S(1)} %all-to-all-done.4.grad_ref), custom_call_target="tpu_custom_call" | custom-call | tf_op jit(solution)/shard_map/pallas_call | solution.py:214
  710.6 5.4 collective-permute-done.34
  716.0 3.4 collective-permute-done.35
  723.4 6.7 collective-permute-done.36
  740.7 5.7 all-to-all-start.6
  747.1 6.4 all-to-all-done.6
  756.5 11.6 %add_subtract_fusion = (f32[24,50304]{1,0:T(8,128)}, f32[24,50304]{1,0:T(8,128)}, f32[24,50304]{1,0:T(8,128)}) fusion(f32[24,50304]{1,0:T(8,128)} %table_ref.1, f32[]{:T(128)} %bitcast.105, f32[]{:T(128)} %bitcast.104, f32[24,50304]{1,0:T(8,128)} %get-tuple-element.180, f32[]{:T(128)S(6)} %min.3, f32[24,50304]{1,0:T(8,128)} %param.34, f32[24,50304]{1,0:T(8,128)} %param.33), kind=kLoop, calls=%fused_computation.32 | loop fusion | flops 18109440 | bytes 33804300 | tf_op jit(solution)/shard_map/sub | solution.py:636
  768.1 10.3 %multiply_subtract_fusion = (f32[1572,768]{1,0:T(8,128)}, f32[1572,768]{1,0:T(8,128)}, f32[1572,768]{1,0:T(8,128)}) fusion(f32[1572,768]{1,0:T(8,128)S(1)} %bitcast.289, f32[]{:T(128)} %bitcast.105, f32[]{:T(128)} %bitcast.104, f32[1572,768]{1,0:T(8,128)} %get-tuple-element.318, f32[]{:T(128)S(6)} %min.3, f32[1572,768]{1,0:T(8,128)} %param.37, ...), kind=kLoop, calls=%fused_computation.28 | loop fusion | flops 19316736 | bytes 33804300 | tf_op jit(solution)/shard_map/sub | solution.py:636
  (535 shorter events, 183.6 us)
Async XLA Ops:
  7.2 124.3 %all-gather.3.cloned.1.call-start = ((), (), s32[]{:S(2)}) async-start(), calls=%async_computation.9 | async-start | bytes 8515584 | tf_op jit(solution)/shard_map/all_gather | solution.py:689
  10.0 168.0 %all-gather.5.cloned.1.call-start = ((), (), s32[]{:S(2)}) async-start(), calls=%async_computation.10 | async-start | bytes 6082560 | tf_op jit(solution)/shard_map/all_gather | solution.py:691
  58.7 14.9 %all-to-all-start.1 = ((bf16[32,2,168]{2,1,0:T(2,128)(2,1)}), bf16[32,2,168]{2,1,0:T(2,128)(2,1)S(1)}, u32[]{:S(2)}, u32[]{:S(2)}) async-start(bf16[32,2,168]{2,1,0:T(2,128)(2,1)} %reshape.577), calls=%async_computation.1 | async-start | bytes 65536 | tf_op jit(solution)/shard_map/all_to_all | solution.py:625
  73.6 51.1 %all-to-all-start = ((bf16[32,24,1024]{2,1,0:T(8,128)(2,1)}), bf16[32,24,1024]{2,1,0:T(8,128)(2,1)}, u32[]{:S(2)}, u32[]{:S(2)}) async-start(bf16[32,24,1024]{2,1,0:T(8,128)(2,1)} %shard_map.409), calls=%async_computation | async-start | bytes 3145728 | tf_op jit(solution)/shard_map/all_to_all | solution.py:684
  195.5 6.1 collective-permute-start
  195.6 6.7 collective-permute-start.5
  201.6 5.4 collective-permute-start.1
  202.3 6.2 collective-permute-start.6
  207.0 5.7 collective-permute-start.2
  208.6 7.5 collective-permute-start.7
  212.8 10.0 %collective-permute-start.3 = (bf16[8,32,768]{2,1,0:T(8,128)(2,1)S(1)}, bf16[8,32,768]{2,1,0:T(8,128)(2,1)S(1)}, u32[]{:S(2)}, u32[]{:S(2)}) collective-permute-start(bf16[8,32,768]{2,1,0:T(8,128)(2,1)S(1)} %pad_maximum_fusion.8), channel_id=1, source_target_pairs={{0,8},{1,9},{2,10},{3,11},{4,12},{5,13},{6,14},{7,15},{8,0},{9,1},... | collective-permute-start | bytes 1179656 | tf_op jit(solution)/shard_map/ppermute | solution.py:619
  216.2 7.8 collective-permute-start.8
  222.8 2.4 collective-permute-start.4
  244.4 9.8 %all-to-all-start.2 = ((f32[32,1,192]{2,1,0:T(1,128)}), f32[32,1,192]{2,1,0:T(1,128)S(1)}, u32[]{:S(2)}, u32[]{:S(2)}) async-start(f32[32,1,192]{2,1,0:T(1,128)} %reshape.553), calls=%async_computation.2 | async-start | bytes 65536 | tf_op jit(solution)/shard_map/all_to_all | solution.py:743
  255.9 9.8 %all-to-all-start.3 = ((f32[32,1,64]{2,1,0:T(1,128)}), f32[32,1,64]{2,1,0:T(1,128)S(1)}, u32[]{:S(2)}, u32[]{:S(2)}) async-start(f32[32,1,64]{2,1,0:T(1,128)} %broadcast_in_dim.48), calls=%async_computation.3 | async-start | bytes 32768 | tf_op jit(solution)/shard_map/all_to_all | solution.py:625
  258.6 475.4 %reduce-scatter.3.cloned.1.call-start = ((), (), s32[]{:S(2)}) async-start(), calls=%async_computation.11 | async-start | bytes 9732096 | tf_op jit(solution)/shard_map/reduce_scatter | solution.py:786
  284.0 11.3 %collective-permute-start.10 = (f32[2,2,2,2,32,768]{5,4,3,2,1,0:T(8,128)S(1)}, f32[2,2,2,2,32,768]{5,4,3,2,1,0:T(8,128)S(1)}, u32[]{:S(2)}, u32[]{:S(2)}) collective-permute-start(f32[2,2,2,2,32,768]{5,4,3,2,1,0:T(8,128)S(1)} %bitcast.295), channel_id=1, source_target_pairs={{0,1},{1,0},{2,3},{3,2},{4,5},{5,4},{6,7},{7,6},{8,9},{9,8},{10,11... | collective-permute-start | bytes 4718600 | tf_op jit(solution)/shard_map/ppermute | solution.py:520
  284.1 11.3 %collective-permute-start.11 = (f32[2,2,2,2,32,768]{5,4,3,2,1,0:T(8,128)S(1)}, f32[2,2,2,2,32,768]{5,4,3,2,1,0:T(8,128)S(1)}, u32[]{:S(2)}, u32[]{:S(2)}) collective-permute-start(f32[2,2,2,2,32,768]{5,4,3,2,1,0:T(8,128)S(1)} %bitcast.294), channel_id=1, source_target_pairs={{0,1},{1,0},{2,3},{3,2},{4,5},{5,4},{6,7},{7,6},{8,9},{9,8},{10,11... | collective-permute-start | bytes 4718600 | tf_op jit(solution)/shard_map/ppermute | solution.py:520
  298.9 19.7 %collective-permute-start.12 = (f32[2,2,2,32,768]{4,3,2,1,0:T(8,128)}, f32[2,2,2,32,768]{4,3,2,1,0:T(8,128)}, u32[]{:S(2)}, u32[]{:S(2)}) collective-permute-start(f32[2,2,2,32,768]{4,3,2,1,0:T(8,128)} %slice_bitcast_fusion.5), channel_id=1, source_target_pairs={{0,8},{1,9},{2,10},{3,11},{4,12},{5,13},{6,14},{7,15},{8,0},{9,1},... | collective-permute-start | bytes 2359304 | tf_op jit(solution)/shard_map/ppermute | solution.py:520
  299.4 19.4 %collective-permute-start.13 = (f32[2,2,2,32,768]{4,3,2,1,0:T(8,128)}, f32[2,2,2,32,768]{4,3,2,1,0:T(8,128)}, u32[]{:S(2)}, u32[]{:S(2)}) collective-permute-start(f32[2,2,2,32,768]{4,3,2,1,0:T(8,128)} %slice_bitcast_fusion.4), channel_id=1, source_target_pairs={{0,16},{1,17},{2,18},{3,19},{4,20},{5,21},{6,22},{7,23},{8,24},{9,... | collective-permute-start | bytes 2359304 | tf_op jit(solution)/shard_map/ppermute | solution.py:520
  321.6 9.8 %collective-permute-start.14 = (f32[2,2,32,768]{3,2,1,0:T(8,128)S(1)}, f32[2,2,32,768]{3,2,1,0:T(8,128)S(1)}, u32[]{:S(2)}, u32[]{:S(2)}) collective-permute-start(f32[2,2,32,768]{3,2,1,0:T(8,128)S(1)} %slice_bitcast_fusion.9), channel_id=1, source_target_pairs={{0,16},{1,17},{2,18},{3,19},{4,20},{5,21},{6,22},{7,23},{8,24},{9,... | collective-permute-start | bytes 1179656 | tf_op jit(solution)/shard_map/ppermute | solution.py:520
  322.3 9.5 %collective-permute-start.15 = (f32[2,2,32,768]{3,2,1,0:T(8,128)S(1)}, f32[2,2,32,768]{3,2,1,0:T(8,128)S(1)}, u32[]{:S(2)}, u32[]{:S(2)}) collective-permute-start(f32[2,2,32,768]{3,2,1,0:T(8,128)S(1)} %slice_bitcast_fusion.8), channel_id=1, source_target_pairs={{0,8},{1,9},{2,10},{3,11},{4,12},{5,13},{6,14},{7,15},{8,0},{9,1},... | collective-permute-start | bytes 1179656 | tf_op jit(solution)/shard_map/ppermute | solution.py:520
  332.0 6.5 collective-permute-start.16
  332.5 8.0 %collective-permute-start.17 = (f32[2,32,768]{2,1,0:T(8,128)S(1)}, f32[2,32,768]{2,1,0:T(8,128)S(1)}, u32[]{:S(2)}, u32[]{:S(2)}) collective-permute-start(f32[2,32,768]{2,1,0:T(8,128)S(1)} %slice_bitcast_fusion.12), channel_id=1, source_target_pairs={{0,2},{1,3},{2,0},{3,1},{4,6},{5,7},{6,4},{7,5},{8,10},{9,11},{10,... | collective-permute-start | bytes 589832 | tf_op jit(solution)/shard_map/ppermute | solution.py:520
  340.7 7.7 collective-permute-start.18
  341.3 8.2 %collective-permute-start.19 = (f32[32,768]{1,0:T(8,128)S(1)}, f32[32,768]{1,0:T(8,128)S(1)}, u32[]{:S(2)}, u32[]{:S(2)}) collective-permute-start(f32[32,768]{1,0:T(8,128)S(1)} %slice_bitcast_fusion.16), channel_id=1, source_target_pairs={{0,4},{1,5},{2,6},{3,7},{4,0},{5,1},{6,2},{7,3},{8,12},{9,13},{10,... | collective-permute-start | bytes 294920 | tf_op jit(solution)/shard_map/ppermute | solution.py:520
  397.4 339.5 %reduce-scatter.5.cloned.1.call-start = ((), (), s32[]{:S(2)}) async-start(), calls=%async_computation.12 | async-start | bytes 12165120 | tf_op jit(solution)/shard_map/reduce_scatter | solution.py:778
  450.0 54.3 %collective-permute-start.20 = (f32[384,3072]{1,0:T(8,128)}, f32[384,3072]{1,0:T(8,128)}, u32[]{:S(2)}, u32[]{:S(2)}) collective-permute-start(f32[384,3072]{1,0:T(8,128)} %get-tuple-element.149), channel_id=1, source_target_pairs={{0,1},{1,0},{2,3},{3,2},{4,5},{5,4},{6,7},{7,6},{8,9},{9,8},{10,11... | collective-permute-start | bytes 14155784 | tf_op jit(solution)/shard_map/ppermute | solution.py:548
  509.9 18.0 %collective-permute-start.21 = (bf16[2,2,2,24,1536]{4,3,2,1,0:T(8,128)(2,1)S(1)}, bf16[2,2,2,24,1536]{4,3,2,1,0:T(8,128)(2,1)S(1)}, u32[]{:S(2)}, u32[]{:S(2)}) collective-permute-start(bf16[2,2,2,24,1536]{4,3,2,1,0:T(8,128)(2,1)S(1)} %fusion.73), channel_id=1, source_target_pairs={{0,8},{1,9},{2,10},{3,11},{4,12},{5,13},{6,14},{7,15},{8,0},{9,1},... | collective-permute-start | bytes 1769480 | tf_op jit(solution)/shard_map/ppermute | solution.py:520
  510.0 21.2 %collective-permute-start.22 = (bf16[2,2,2,24,1536]{4,3,1,2,0:T(8,128)(2,1)S(1)}, bf16[2,2,2,24,1536]{4,3,1,2,0:T(8,128)(2,1)S(1)}, u32[]{:S(2)}, u32[]{:S(2)}) collective-permute-start(bf16[2,2,2,24,1536]{4,3,1,2,0:T(8,128)(2,1)S(1)} %fusion.74), channel_id=1, source_target_pairs={{0,16},{1,17},{2,18},{3,19},{4,20},{5,21},{6,22},{7,23},{8,24},{9,... | collective-permute-start | bytes 1769480 | tf_op jit(solution)/shard_map/ppermute | solution.py:520
  532.3 16.7 %collective-permute-start.24 = (bf16[2,2,24,1536]{3,2,1,0:T(8,128)(2,1)S(1)}, bf16[2,2,24,1536]{3,2,1,0:T(8,128)(2,1)S(1)}, u32[]{:S(2)}, u32[]{:S(2)}) collective-permute-start(bf16[2,2,24,1536]{3,2,1,0:T(8,128)(2,1)S(1)} %fusion.79), channel_id=1, source_target_pairs={{0,16},{1,17},{2,18},{3,19},{4,20},{5,21},{6,22},{7,23},{8,24},{9,... | collective-permute-start | bytes 884744 | tf_op jit(solution)/shard_map/ppermute | solution.py:520
  534.1 14.9 %collective-permute-start.25 = (bf16[2,2,24,1536]{3,2,0,1:T(8,128)(2,1)S(1)}, bf16[2,2,24,1536]{3,2,0,1:T(8,128)(2,1)S(1)}, u32[]{:S(2)}, u32[]{:S(2)}) collective-permute-start(bf16[2,2,24,1536]{3,2,0,1:T(8,128)(2,1)S(1)} %fusion.80), channel_id=1, source_target_pairs={{0,8},{1,9},{2,10},{3,11},{4,12},{5,13},{6,14},{7,15},{8,0},{9,1},... | collective-permute-start | bytes 884744 | tf_op jit(solution)/shard_map/ppermute | solution.py:520
  534.5 14.6 %collective-permute-start.23 = (f32[384,2304]{1,0:T(8,128)}, f32[384,2304]{1,0:T(8,128)S(1)}, u32[]{:S(2)}, u32[]{:S(2)}) collective-permute-start(f32[384,2304]{1,0:T(8,128)} %fusion.64), channel_id=1, source_target_pairs={{0,1},{1,0},{2,3},{3,2},{4,5},{5,4},{6,7},{7,6},{8,9},{9,8},{10,11... | collective-permute-start | bytes 10616840 | tf_op jit(solution)/shard_map/ppermute | solution.py:548
  553.4 29.5 %collective-permute-start.26 = (f32[2,2,2,24,1152]{4,3,2,1,0:T(8,128)}, f32[2,2,2,24,1152]{4,3,2,1,0:T(8,128)S(1)}, u32[]{:S(2)}, u32[]{:S(2)}) collective-permute-start(f32[2,2,2,24,1152]{4,3,2,1,0:T(8,128)} %dynamic-slice_bitcast_fusion.1), channel_id=1, source_target_pairs={{0,8},{1,9},{2,10},{3,11},{4,12},{5,13},{6,14},{7,15},{8,0},{9,1},... | collective-permute-start | bytes 2654216 | tf_op jit(solution)/shard_map/ppermute | solution.py:520
  555.1 34.8 %collective-permute-start.27 = (f32[2,2,2,24,1152]{4,3,2,1,0:T(8,128)}, f32[2,2,2,24,1152]{4,3,2,1,0:T(8,128)}, u32[]{:S(2)}, u32[]{:S(2)}) collective-permute-start(f32[2,2,2,24,1152]{4,3,2,1,0:T(8,128)} %dynamic-slice_bitcast_fusion), channel_id=1, source_target_pairs={{0,16},{1,17},{2,18},{3,19},{4,20},{5,21},{6,22},{7,23},{8,24},{9,... | collective-permute-start | bytes 2654216 | tf_op jit(solution)/shard_map/ppermute | solution.py:520
  555.4 8.6 %collective-permute-start.28 = (bf16[2,24,1536]{2,1,0:T(8,128)(2,1)S(1)}, bf16[2,24,1536]{2,1,0:T(8,128)(2,1)S(1)}, u32[]{:S(2)}, u32[]{:S(2)}) collective-permute-start(bf16[2,24,1536]{2,1,0:T(8,128)(2,1)S(1)} %fusion.89), channel_id=1, source_target_pairs={{0,2},{1,3},{2,0},{3,1},{4,6},{5,7},{6,4},{7,5},{8,10},{9,11},{10,... | collective-permute-start | bytes 442376 | tf_op jit(solution)/shard_map/ppermute | solution.py:520
  555.4 8.9 %collective-permute-start.29 = (bf16[2,24,1536]{2,1,0:T(8,128)(2,1)}, bf16[2,24,1536]{2,1,0:T(8,128)(2,1)S(1)}, u32[]{:S(2)}, u32[]{:S(2)}) collective-permute-start(bf16[2,24,1536]{2,1,0:T(8,128)(2,1)} %fusion.90), channel_id=1, source_target_pairs={{0,2},{1,3},{2,0},{3,1},{4,6},{5,7},{6,4},{7,5},{8,10},{9,11},{10,... | collective-permute-start | bytes 442376 | tf_op jit(solution)/shard_map/ppermute | solution.py:520
  561.1 55.1 %all-to-all-start.4 = ((bf16[32,24,1024]{2,1,0:T(8,128)(2,1)}), bf16[32,24,1024]{2,1,0:T(8,128)(2,1)S(1)}, u32[]{:S(2)}, u32[]{:S(2)}) async-start(bf16[32,24,1024]{2,1,0:T(8,128)(2,1)} %bitcast.281), calls=%async_computation.4 | async-start | bytes 3145728 | tf_op jit(solution)/shard_map/all_to_all | solution.py:808
  597.7 107.5 %collective-permute-start.30 = (f32[2,2,24,1152]{3,2,0,1:T(8,128)}, f32[2,2,24,1152]{3,2,0,1:T(8,128)}, u32[]{:S(2)}, u32[]{:S(2)}) collective-permute-start(f32[2,2,24,1152]{3,2,0,1:T(8,128)} %bitcast.266), channel_id=1, source_target_pairs={{0,16},{1,17},{2,18},{3,19},{4,20},{5,21},{6,22},{7,23},{8,24},{9,... | collective-permute-start | bytes 1327112 | tf_op jit(solution)/shard_map/ppermute | solution.py:520
  597.7 107.5 %collective-permute-start.31 = (f32[2,2,24,1152]{3,2,0,1:T(8,128)}, f32[2,2,24,1152]{3,2,0,1:T(8,128)}, u32[]{:S(2)}, u32[]{:S(2)}) collective-permute-start(f32[2,2,24,1152]{3,2,0,1:T(8,128)} %bitcast.265), channel_id=1, source_target_pairs={{0,8},{1,9},{2,10},{3,11},{4,12},{5,13},{6,14},{7,15},{8,0},{9,1},... | collective-permute-start | bytes 1327112 | tf_op jit(solution)/shard_map/ppermute | solution.py:520
  617.0 87.6 %all-to-all-start.5 = ((f32[32,1,336]{2,1,0:T(1,128)}), f32[32,1,336]{2,1,0:T(1,128)S(1)}, u32[]{:S(2)}, u32[]{:S(2)}) async-start(f32[32,1,336]{2,1,0:T(1,128)} %reshape.535), calls=%async_computation.7 | async-start | bytes 98304 | tf_op jit(solution)/shard_map/all_to_all | solution.py:826
  622.5 82.7 %collective-permute-start.32 = (bf16[24,1536]{1,0:T(8,128)(2,1)}, bf16[24,1536]{1,0:T(8,128)(2,1)S(1)}, u32[]{:S(2)}, u32[]{:S(2)}) collective-permute-start(bf16[24,1536]{1,0:T(8,128)(2,1)} %fusion.93), channel_id=1, source_target_pairs={{0,4},{1,5},{2,6},{3,7},{4,0},{5,1},{6,2},{7,3},{8,12},{9,13},{10,... | collective-permute-start | bytes 221192 | tf_op jit(solution)/shard_map/ppermute | solution.py:520
  625.2 80.0 %collective-permute-start.33 = (bf16[24,1536]{1,0:T(8,128)(2,1)}, bf16[24,1536]{1,0:T(8,128)(2,1)}, u32[]{:S(2)}, u32[]{:S(2)}) collective-permute-start(bf16[24,1536]{1,0:T(8,128)(2,1)} %fusion.94), channel_id=1, source_target_pairs={{0,4},{1,5},{2,6},{3,7},{4,0},{5,1},{6,2},{7,3},{8,12},{9,13},{10,... | collective-permute-start | bytes 221192 | tf_op jit(solution)/shard_map/ppermute | solution.py:520
  707.6 8.4 %collective-permute-start.34 = (f32[2,24,1152]{2,1,0:T(8,128)S(1)}, f32[2,24,1152]{2,1,0:T(8,128)S(1)}, u32[]{:S(2)}, u32[]{:S(2)}) collective-permute-start(f32[2,24,1152]{2,1,0:T(8,128)S(1)} %dynamic-slice_bitcast_fusion.3), channel_id=1, source_target_pairs={{0,2},{1,3},{2,0},{3,1},{4,6},{5,7},{6,4},{7,5},{8,10},{9,11},{10,... | collective-permute-start | bytes 663560 | tf_op jit(solution)/shard_map/ppermute | solution.py:520
  709.4 10.0 %collective-permute-start.35 = (f32[2,24,1152]{2,1,0:T(8,128)S(1)}, f32[2,24,1152]{2,1,0:T(8,128)S(1)}, u32[]{:S(2)}, u32[]{:S(2)}) collective-permute-start(f32[2,24,1152]{2,1,0:T(8,128)S(1)} %dynamic-slice_bitcast_fusion.2), channel_id=1, source_target_pairs={{0,2},{1,3},{2,0},{3,1},{4,6},{5,7},{6,4},{7,5},{8,10},{9,11},{10,... | collective-permute-start | bytes 663560 | tf_op jit(solution)/shard_map/ppermute | solution.py:520
  719.6 10.6 %collective-permute-start.36 = (f32[24,1152]{1,0:T(8,128)S(1)}, f32[24,1152]{1,0:T(8,128)S(1)}, u32[]{:S(2)}, u32[]{:S(2)}) collective-permute-start(f32[24,1152]{1,0:T(8,128)S(1)} %dynamic-slice_bitcast_fusion.5), channel_id=1, source_target_pairs={{0,4},{1,5},{2,6},{3,7},{4,0},{5,1},{6,2},{7,3},{8,12},{9,13},{10,... | collective-permute-start | bytes 331784 | tf_op jit(solution)/shard_map/ppermute | solution.py:520
  722.2 9.2 %collective-permute-start.37 = (f32[24,1152]{1,0:T(8,128)S(1)}, f32[24,1152]{1,0:T(8,128)S(1)}, u32[]{:S(2)}, u32[]{:S(2)}) collective-permute-start(f32[24,1152]{1,0:T(8,128)S(1)} %dynamic-slice_bitcast_fusion.4), channel_id=1, source_target_pairs={{0,4},{1,5},{2,6},{3,7},{4,0},{5,1},{6,2},{7,3},{8,12},{9,13},{10,... | collective-permute-start | bytes 331784 | tf_op jit(solution)/shard_map/ppermute | solution.py:520
  740.7 12.8 %all-to-all-start.6 = ((f32[32,1,2]{2,1,0:T(1,128)}), f32[32,1,2]{2,1,0:T(1,128)S(1)}, u32[]{:S(2)}, u32[]{:S(2)}) async-start(f32[32,1,2]{2,1,0:T(1,128)} %broadcast_in_dim.51), calls=%async_computation.8 | async-start | bytes 32768 | tf_op jit(solution)/shard_map/all_to_all | solution.py:625
  (98 other events, 2020.0 us)
Sparse Core Ops, SparseCore 0:
  11.6 90.5 all-gather.2
  105.9 69.3 all-gather.4
  397.6 135.9 reduce-scatter.2
  540.6 160.1 reduce-scatter.4

commit v3 on v2

--- a/solution.py
+++ b/solution.py
@@ -680,16 +680,18 @@
     flat_ids = jnp.transpose(token_ids, (1, 0, 2)).reshape(-1)
     ids_by_run = flat_ids.reshape(count, 1, tokens)
     columns = gather_features(embed_in, ids_by_run)
-    columns, vector_half = lax.optimization_barrier((columns, vector_params.astype(half_type)))
     arrived = lax.all_to_all(columns, AXES, split_axis=0, concat_axis=0, tiled=True)
     embedded = arrived.reshape(width, tokens).T.astype(full_type)
     places = scatter_places(ids_by_run, own_width, vocab)
 
-    both = jnp.concatenate([proj_in.astype(half_type), proj_up.astype(half_type)], 1)
+    small = vector_params.astype(half_type).reshape(own_width, -1)
+    each = small.shape[1]
+    small = jnp.pad(small, ((0, 0), (0, -each % LANES)))
+    both = jnp.concatenate([proj_in.astype(half_type), proj_up.astype(half_type), small], 1)
     both = lax.all_gather(both, AXES, axis=0, tiled=True)
-    weight_in, weight_up = both[:, : 3 * width], both[:, 3 * width :]
+    weight_in, weight_up = both[:, : 3 * width], both[:, 3 * width : 3 * width + hidden]
     weight_mix = lax.all_gather(proj_mix.astype(half_type), AXES, axis=0, tiled=True)
-    vector = shared_by_all(vector_half, count).reshape(-1).astype(full_type)
+    vector = both[:, 3 * width + hidden : 3 * width + hidden + each].reshape(-1).astype(full_type)
     pairing = pair_first(width, own_width, place)
     basis_paired = jnp.dot(basis_in, pairing, preferred_element_type=full_type).astype(half_type)
     (
@@ -775,37 +777,37 @@
     grad_residual = norm_back(grad_final * gain_last, normed_last, inv_last)
     grad_branch = grad_residual.astype(half_type)
     grad_mix = jnp.einsum("sa,sb->ab", joined, grad_branch, preferred_element_type=full_type)
+    grad_branch, grad_mix = lax.optimization_barrier((grad_branch, grad_mix))
     own_mix = lax.psum_scatter(grad_mix, AXES, scatter_dimension=0, tiled=True)
     grad_joined = jnp.einsum("sb,ab->sa", grad_branch, weight_mix, preferred_element_type=full_type)
-    grad_context = (
-        grad_joined[:, :width].astype(half_type)
-    )
-    grad_hidden = (grad_joined[:, width:] * gelu_slope(hidden_pre)).astype(half_type)
-    grad_up = jnp.einsum("sa,sb->ab", second_in, grad_hidden, preferred_element_type=full_type)
-    grad_second = jnp.einsum("sb,ab->sa", grad_hidden, weight_up, preferred_element_type=full_type)
-    own_up = lax.psum_scatter(grad_up, AXES, scatter_dimension=0, tiled=True)
-
-    rot_out = jnp.dot(grad_hidden, basis_out, preferred_element_type=full_type).astype(half_type)
-    scale_other, scale_own = document_squares(rot_in, rot_out, segments, total)
-    scale_step = FirstStep(scale_other, scale_own, own_width, half_type)
-    live = [scale_step]
-    grad_context = advance(grad_context, live)
+    grad_context = grad_joined[:, :width].astype(half_type)
     grad_parts = attention_backward(
         queries, keys_all, values_all, grad_context, logsum, tables, segments
     )
     grad_mixed = jnp.concatenate([grad_parts[0], grad_parts[1], grad_parts[2]], 1)
-    grad_mixed = advance(grad_mixed, live)
     in_other = jnp.dot(first_turned[: width // 2], grad_mixed, preferred_element_type=full_type)
     in_own = jnp.dot(first_turned[width // 2 :], grad_mixed, preferred_element_type=full_type)
     in_step = FirstStep(in_other, in_own, own_width, full_type)
-    live.append(in_step)
-    grad_mixed = advance(grad_mixed, live)
+    live = [in_step]
+    grad_joined = advance(grad_joined, live)
+    grad_hidden = (grad_joined[:, width:] * gelu_slope(hidden_pre)).astype(half_type)
+    grad_hidden = advance(grad_hidden, live)
+    grad_up = jnp.einsum("sa,sb->ab", second_in, grad_hidden, preferred_element_type=full_type)
+    grad_second = jnp.einsum("sb,ab->sa", grad_hidden, weight_up, preferred_element_type=full_type)
+    grad_up, grad_second, grad_mixed = advance((grad_up, grad_second, grad_mixed), live)
+    own_up = lax.psum_scatter(grad_up, AXES, scatter_dimension=0, tiled=True)
     grad_first = jnp.einsum("sb,ab->sa", grad_mixed, weight_in, preferred_element_type=full_type)
     grad_embedded = grad_residual + norm_back(
         grad_first * gain_first + grad_second * gain_second, normed, inv_std
     )
     sending = grad_embedded.astype(half_type).T.reshape(count, own_width, tokens)
+    sending, grad_hidden_late = advance((sending, grad_hidden), live)
     returned = lax.all_to_all(sending, AXES, split_axis=0, concat_axis=0, tiled=True)
+
+    rot_out = jnp.dot(grad_hidden_late, basis_out, preferred_element_type=full_type).astype(half_type)
+    scale_other, scale_own = document_squares(rot_in, rot_out, segments, total)
+    scale_step = FirstStep(scale_other, scale_own, own_width, half_type)
+    scale_live = [scale_step]
     vector_grad = jnp.concatenate(
         [
             jnp.sum(grad_mixed.astype(full_type), 0),
@@ -819,9 +821,8 @@
             jnp.sum(grad_final * normed_last, 0),
         ]
     )
-    vector_grad = advance(vector_grad, live)
-    vector_grad = advance(vector_grad, live)
-    returned, vector_grad = lax.optimization_barrier((returned, vector_grad))
+    returned, vector_grad = advance((returned, vector_grad), live)
+    returned, vector_grad = advance((returned, vector_grad), scale_live)
     own_vector = jnp.sum(
         lax.all_to_all(
             vector_grad.reshape(count, 1, -1), AXES, split_axis=0, concat_axis=0, tiled=True
@@ -831,11 +832,11 @@
     grad_in_table, in_squares = scatter_features(returned, places, vocab)
     in_squares = run_all(in_squares, live)
     own_in = in_step.finished()
-    eigen_scales = scale_step.finished() / float(micro_count * count * DOCS)
     grads = (grad_in_table, grad_out_table, own_in, own_up, own_mix, own_vector)
     squares = jnp.sum(in_squares) + out_squares
     squares = squares + sum((jnp.sum(gradient * gradient) for gradient in grads[2:]))
     both = jnp.sum(shared_by_all(jnp.stack([squares, loss_part])[None], count), (0, 1))
+    advance(jnp.zeros((), full_type), scale_live)
     grad_norm = jnp.sqrt(both[0])
     loss_value = both[1]
     factor = jnp.minimum(1.0, clip_limit / (grad_norm + 1e-06))
@@ -857,13 +858,15 @@
         proj_mix_second,
         vector_second,
     )
-    results = []
-    for weight, gradient, moment_one, moment_two, rate in zip(
-        weights, grads, firsts, seconds, step_rates
-    ):
-        results.extend(
-            adam_update(weight, gradient * factor, moment_one, moment_two, rate, step_value)
-        )
+    updates = []
+    for index, (weight, moment_one, moment_two, rate) in enumerate(zip(weights, firsts, seconds, step_rates)):
+        gradient = grads[index]
+        if index in (1, 2):
+            updates[-1], gradient = advance((updates[-1], gradient), scale_live)
+        updates.append(adam_update(weight, gradient * factor, moment_one, moment_two, rate, step_value))
+    run_all(loss_value, scale_live)
+    eigen_scales = scale_step.finished() / float(micro_count * count * DOCS)
+    results = [value for update in updates for value in update]
     return tuple(results) + (loss_value, grad_norm, eigen_scales)
 
 

time: 799 us -> 785 us (0.982)
  waiting for transfers between devices: 190 us -> 159 us
    ppermute x26, waiting for transfers between devices: 85.7 us -> 53 us  [send(): lax.ppermute(ready, AXES, partner_pairs(lax.axis_size(AXES), self.order.p...]
    all_to_all x1, waiting for transfers between devices: 18.5 us -> 0.01 us  [per_device(): lax.all_to_all(sending, AXES, split_axis=0, concat_axis=0, tiled=True)]
    all_to_all x1, waiting for transfers between devices: 40.3 us -> 54.2 us  [per_device(): lax.all_to_all(columns, AXES, split_axis=0, concat_axis=0, tiled=True)]
    reduce_sum x1, other arithmetic: 13 us -> 0.91 us  [per_device(): jnp.sum(grad_hidden.astype(full_type), 0)]
    all_gather x1, waiting for transfers between devices: 0.01 us -> 11.4 us  [per_device(): lax.all_gather(proj_mix.astype(half_type), AXES, axis=0, tiled=True)]
    convert_element_type x2 -> x4, other arithmetic: 0.82 us -> 11 us  [the longest x1 9.02 us: per_device(): (grad_joined[:, width:] * gelu_slope(hidden_pre)).astype(half_type)]
    all_to_all x3 -> x2, waiting for transfers between devices: 18.9 us -> 9.26 us  [shared_by_all(): lax.all_to_all(jnp.broadcast_to(own[None], (count,) + own.shape), AXES, s...]
    all_to_all x3 -> x2, starting transfers between devices: 15.7 us -> 6.23 us  [shared_by_all(): lax.all_to_all(jnp.broadcast_to(own[None], (count,) + own.shape), AXES, s...]
  transfers between devices with their start and end apart: 49 -> 48, of which waited for: 32 -> 29; matrix products, arithmetic and copies ran while one was open for 19% -> 27% of each run, Pallas kernels for 25% -> 25%
where the time goes in v3:
time: 785 us; the launch traced here: 775 us
  Pallas kernels  195 us (25%)
  waiting for transfers between devices  159 us (20%)
  matrix products  148 us (19%)
  other arithmetic  122 us (16%)
  starting transfers between devices  71 us (9%)
  local copies, waits for them, and re-layouts  55 us (7%)
  between operations  24.2 us (3%)
    pallas_call x1, Pallas kernels, scatter_features(): pl.pallas_call(scatter_kernel, out_shape=(jax.ShapeDtypeStruct((width, vo...  79.1 us
    all_to_all x1, waiting for transfers between devices, per_device(): lax.all_to_all(columns, AXES, split_axis=0, concat_axis=0, tiled=True)  54.2 us
    ppermute x26, waiting for transfers between devices, send(): lax.ppermute(ready, AXES, partner_pairs(lax.axis_size(AXES), self.order.p...  53 us
    pallas_call x1, Pallas kernels, gather_features(): pl.pallas_call(gather_kernel, out_shape=jax.ShapeDtypeStruct((count, widt...  40.5 us
    pallas_call x1, Pallas kernels, attention_backward(): pl.pallas_call(backward_kernel, out_shape=jax.ShapeDtypeStruct((3, tokens...  32.7 us
    ppermute x26, starting transfers between devices, send(): lax.ppermute(ready, AXES, partner_pairs(lax.axis_size(AXES), self.order.p...  28.9 us
    sub x6, other arithmetic, adam_update(): weight - rate * (update + weight_decay * weight)  28.5 us
    dot_general x1, matrix products, per_device(): jnp.dot(grad_hidden_late, basis_out, preferred_element_type=full_type)  25.8 us
  transfers between devices with their start and end apart: 48, of which 29 were waited for; matrix products, arithmetic and copies ran while one was open for 27% of the time, Pallas kernels for 25%

profile of v3, /device:TPU:0, one launch (start us, length us, event | category | flops | bytes accessed | tf_op | source)
XLA Modules:
  0.0 774.6 jit_solution(16110828328275887410)
XLA Ops:
  16.2 40.5 %shard_map.409 = bf16[32,24,1024]{2,1,0:T(8,128)(2,1)} custom-call(s32[32,1,1024]{2,1,0:T(1,128)S(1)} %reshape_reshape.3.ids_ref, f32[24,50304]{1,0:T(8,128)S(1)} %copy-done.2), custom_call_target="tpu_custom_call" | custom-call | tf_op jit(solution)/shard_map/pallas_call | solution.py:123
  56.8 7.4 all-to-all-start
  69.0 54.2 %all-to-all-done = bf16[32,24,1024]{2,1,0:T(8,128)(2,1)} async-done(((bf16[32,24,1024]{2,1,0:T(8,128)(2,1)}), bf16[32,24,1024]{2,1,0:T(8,128)(2,1)}, u32[]{:S(2)}, u32[]{:S(2)}) %all-to-all-start) | async-done | bytes 1572896 | tf_op jit(solution)/shard_map/all_to_all | solution.py:683
  130.3 9.5 %convolution_add_fusion.query_in.key_in.value_in = f32[1024,2304]{1,0:T(8,128)} fusion(bf16[1024,768]{0,1:T(8,128)(2,1)S(1)} %get-tuple-element.295, f32[2304]{0:T(1024)S(1)} %slice.186, bf16[768,5504]{1,0:T(8,128)(2,1)} %all-gather.3.cloned.1.call-done), kind=kOutput, calls=%fused_computation.23 | convolution fusion | flops 3626237952 | bytes 14558208 | tf_op jit(solution)/shard_map/dot_general | solution.py:716
  139.9 21.2 %shard_map.410 = (bf16[1024,768]{1,0:T(8,128)(2,1)S(1)}, bf16[1024,768]{1,0:T(8,128)(2,1)S(1)}, bf16[1024,768]{1,0:T(8,128)(2,1)S(1)}, bf16[1024,768]{1,0:T(8,128)(2,1)S(1)}, f32[2,6,2,512]{3,2,1,0:T(2,128)S(1)}) custom-call(f32[1024,2304]{1,0:T(8,128)} %convolution_add_fusion.query_in.key_in.value_in, ...), custom_call_target="tpu_custom_call" | custom-call | tf_op jit(solution)/shard_map/pallas_call | solution.py:329
  165.7 10.1 %multiply_convert_fusion = (bf16[1024,3072]{1,0:T(8,128)(2,1)}, f32[1024,3072]{1,0:T(8,128)}) fusion(f32[3072]{0:T(1024)S(1)} %slice.190, bf16[1024,768]{0,1:T(8,128)(2,1)S(1)} %get-tuple-element.143, bf16[768,5504]{1,0:T(8,128)(2,1)S(1)} %bitcast.319), kind=kOutput, calls=%fused_computation.17 | convolution fusion | flops 4850712576 | bytes 25178112 | tf_op jit(solution)/shard_map/dot_general | solution.py:719
  175.8 11.4 %all-gather.5.cloned.1.call-done = bf16[3840,768]{1,0:T(8,128)(2,1)} async-done(((bf16[120,768]{1,0:T(8,128)(2,1)}), bf16[3840,768]{1,0:T(8,128)(2,1)}) %all-gather.5.cloned.1.call-update) | async-done | bytes 5898256 | tf_op jit(solution)/shard_map/all_gather | solution.py:693
  187.2 10.9 %fusion.145 = (f32[1024]{0:T(1024)S(1)}, f32[1024,768]{0,1:T(8,128)S(1)}) fusion(f32[768]{0:T(1024)S(1)} %get-tuple-element.334, bf16[3840,768]{1,0:T(8,128)(2,1)} %all-gather.5.cloned.1.call-done, bf16[1024,3072]{1,0:T(8,128)(2,1)} %get-tuple-element.352, bf16[1024,768]{1,0:T(8,128)(2,1)} %copy-done.15, bf16[32,24,1024]{2,1,0:T(8,128)(2,1)} %all-to-all-done), kind=kOutput, calls=%fused_computation.371 | convolution fusion | flops 6058671104 | bytes 18488320 | tf_op jit(solution)/shard_map/dot_general | solution.py:722
  229.4 4.5 collective-permute-done.3
  239.1 8.2 %fusion.146 = (f32[2048]{0:T(1024)S(1)}, f32[2048,1572]{0,1:T(8,128)}) fusion(bf16[2048,768]{1,0:T(8,128)(2,1)S(1)} %bitcast.288, f32[1572,768]{1,0:T(8,128)S(1)} %bitcast.287), kind=kOutput, calls=%fused_computation.372 | convolution fusion | flops 4949509120 | bytes 20860928 | tf_op jit(solution)/shard_map/rd,vd->rv/dot_general | solution.py:737
  247.4 6.8 exponential_reduce_fusion
  255.9 4.6 all-to-all-start.1
  260.6 7.2 all-to-all-done.1
  272.2 6.9 all-to-all-done.2
  280.9 7.3 fusion.3
  288.2 9.0 %fusion.55 = f32[2048,768]{1,0:T(8,128)S(1)} fusion(bf16[2048,1572]{0,1:T(8,128)(2,1)S(1)} %fusion.3, f32[1572,768]{1,0:T(8,128)} %param.35), kind=kOutput, calls=%fused_computation.99 | convolution fusion | flops 4946291712 | bytes 17559552 | tf_op jit(solution)/shard_map/dot_general | solution.py:758
  301.2 8.1 %multiply_reduce_fusion = (f32[]{:T(128)}, f32[1572,768]{1,0:T(8,128)}) fusion(bf16[2048,1572]{0,1:T(8,128)(2,1)S(1)} %fusion.3, bf16[2048,768]{1,0:T(8,128)(2,1)S(1)} %bitcast.289), kind=kOutput, calls=%fused_computation.30 | convolution fusion | flops 4947499008 | bytes 14413828 | tf_op jit(solution)/shard_map/rv,rd->vd/dot_general | solution.py:765
  313.2 5.2 convolution_convert_fusion.2.in_ref
  318.4 13.1 %collective-permute-done.12 = f32[2,2,2,32,768]{4,3,2,1,0:T(8,128)} collective-permute-done((f32[2,2,2,32,768]{4,3,2,1,0:T(8,128)S(1)}, f32[2,2,2,32,768]{4,3,2,1,0:T(8,128)}, u32[]{:S(2)}, u32[]{:S(2)}) %collective-permute-start.12) | collective-permute-done | bytes 786464 | tf_op jit(solution)/shard_map/ppermute | solution.py:520
  337.0 7.7 collective-permute-done.14
  347.3 4.4 collective-permute-done.16
  356.8 4.7 collective-permute-done.18
  369.0 4.0 multiply_reduce_fusion.1
  377.8 9.7 %fusion.10 = f32[3840,768]{1,0:T(8,128)} fusion(bf16[1024,768]{0,1:T(8,128)(2,1)S(1)} %convert_element_type.209, bf16[1024,3072]{1,0:T(8,128)(2,1)S(1)} %bitcast.324, bf16[1024,768]{1,0:T(8,128)(2,1)S(1)} %copy-done.16), kind=kOutput, calls=%fused_computation.25 | convolution fusion | flops 6055526400 | bytes 21233664 | tf_op jit(solution)/shard_map/sa,sb->ab/dot_general | solution.py:779
  387.7 13.1 %fusion.147 = f32[1024,3840]{1,0:T(8,128)} fusion(bf16[1024,768]{0,1:T(8,128)(2,1)} %copy-done.34, bf16[3840,768]{1,0:T(8,128)(2,1)} %all-gather.5.cloned.1.call-done), kind=kOutput, calls=%fused_computation.373 | convolution fusion | flops 6039797760 | bytes 23199744 | tf_op jit(solution)/shard_map/sb,ab->sa/dot_general | solution.py:782
  404.0 32.7 %shard_map.411 = bf16[3,1024,768]{2,1,0:T(8,128)(2,1)S(1)} custom-call(bf16[1024,768]{1,0:T(8,128)(2,1)S(1)} %copy-done.6, bf16[1024,768]{1,0:T(8,128)(2,1)S(1)} %copy-done.8, bf16[1024,768]{1,0:T(8,128)(2,1)S(1)} %copy-done.10, bf16[1024,768]{1,0:T(8,128)(2,1)S(1)} %slice.228.grad_ref, f32[3,512,128]{2,1,0:T(8,128)S(1)} %pad_maximum_fusion.7.tables_ref, ...), custom_call_target="tpu_custom_call" | custom-call | tf_op jit(solution)/shard_map/pallas_call | solution.py:382
  438.4 4.6 fusion.64
  445.5 4.1 pad_maximum_fusion.3
  449.6 5.6 fusion.62
  455.3 9.0 %fusion.9 = bf16[1024,3072]{1,0:T(8,128)(2,1)S(1)} fusion(f32[1024,3840]{1,0:T(8,128)} %fusion.147, f32[1024,3072]{1,0:T(8,128)S(1)} %bitcast.274, f32[3072]{0:T(1024)S(1)} %slice.190), kind=kLoop, calls=%fused_computation.15 | loop fusion | flops 34603008 | bytes 31469568 | tf_op jit(solution)/shard_map/convert_element_type | solution.py:793
  464.3 4.9 add.565
  475.9 6.7 fusion.18
  482.6 7.6 fusion.148
  490.1 9.1 %collective-permute-done.21 = f32[2,2,2,24,1152]{4,3,2,1,0:T(8,128)S(1)} collective-permute-done((f32[2,2,2,24,1152]{4,3,2,1,0:T(8,128)}, f32[2,2,2,24,1152]{4,3,2,1,0:T(8,128)S(1)}, u32[]{:S(2)}, u32[]{:S(2)}) %collective-permute-start.21) | collective-permute-done | bytes 884768 | tf_op jit(solution)/shard_map/ppermute | solution.py:520
  505.1 3.6 copy.220
  511.0 11.2 %fusion.127 = (f32[1024]{0:T(1024)S(1)}, f32[1024]{0:T(1024)S(1)}, f32[768]{0:T(1024)S(1)}, f32[768]{0:T(1024)S(1)}, f32[768]{0:T(1024)S(1)}, /*index=5*/f32[1024,768]{0,1:T(8,128)}) fusion(f32[1024]{0:T(1024)S(1)} %copy-done.55, f32[1024]{0:T(1024)S(1)} %copy-done.53, bf16[32,24,1024]{2,1,0:T(8,128)(2,1)} %all-to-all-done, f32[1024,768]{0,1:T(8,128)} %copy.220, ...), kind=kOutput, calls=%fused_computation.359 | convolution fusion | flops 3634884352 | bytes 16153600 | tf_op jit(solution)/shard_map/sb,ab->sa/dot_general | solution.py:799
  523.1 5.5 fusion.38
  532.2 3.6 all-to-all-start.3
  538.0 25.8 %convolution_convert_fusion.out_ref = bf16[1024,3072]{1,0:T(8,128)(2,1)} fusion(bf16[1024,3072]{1,0:T(8,128)(2,1)} %copy-done.21, bf16[3072,3072]{1,0:T(8,128)(2,1)} %param.51), kind=kOutput, calls=%fused_computation.24 | convolution fusion | flops 19330498560 | bytes 31457280 | tf_op jit(solution)/shard_map/dot_general | solution.py:807
  563.8 21.3 %shard_map.412 = (f32[384,3072]{1,0:T(8,128)S(1)}, f32[384,3072]{1,0:T(8,128)S(1)}) custom-call(s32[2,5]{1,0:T(2,128)S(1)} %copy.225.starts_ref, f32[1]{0:T(128)} %bitcast.80.total_ref, bf16[1024,768]{1,0:T(8,128)(2,1)S(1)} %copy-done.4, bf16[1024,3072]{1,0:T(8,128)(2,1)} %convolution_convert_fusion.out_ref), custom_call_target="tpu_custom_call" | custom-call | tf_op jit(solution)/shard_map/pallas_call | solution.py:468
  590.4 8.0 %all-to-all-start.4 = ((f32[32,1,336]{2,1,0:T(1,128)}), f32[32,1,336]{2,1,0:T(1,128)S(1)}, u32[]{:S(2)}, u32[]{:S(2)}) async-start(f32[32,1,336]{2,1,0:T(1,128)} %reshape.529), calls=%async_computation.6 | async-start | bytes 98304 | tf_op jit(solution)/shard_map/all_to_all | solution.py:827
  603.8 79.1 %shard_map.413 = (f32[24,50304]{1,0:T(8,128)}, f32[8,128]{1,0:T(8,128)S(1)}) custom-call(s32[32,1,1024]{2,1,0:T(1,128)S(1)} %get-tuple-element.315.places_ref, s32[32,1,1024]{2,1,0:T(1,128)S(1)} %get-tuple-element.314.groups_ref, bf16[32,24,1024]{2,1,0:T(8,128)(2,1)S(1)} %all-to-all-done.3.grad_ref), custom_call_target="tpu_custom_call" | custom-call | tf_op jit(solution)/shard_map/pallas_call | solution.py:214
  686.9 4.5 add.596
  694.9 5.1 reduce-scatter.3.cloned.1.call-done
  705.0 3.7 all-to-all-start.5
  717.7 11.4 %add_subtract_fusion = (f32[24,50304]{1,0:T(8,128)}, f32[24,50304]{1,0:T(8,128)}, f32[24,50304]{1,0:T(8,128)}) fusion(f32[24,50304]{1,0:T(8,128)} %table_ref.1, f32[]{:T(128)} %bitcast.88, f32[]{:T(128)} %bitcast.87, f32[24,50304]{1,0:T(8,128)} %get-tuple-element.203, f32[]{:T(128)S(6)} %min.3, f32[24,50304]{1,0:T(8,128)} %param.34, f32[24,50304]{1,0:T(8,128)} %param.33), kind=kLoop, calls=%fused_computation.32 | loop fusion | flops 18109440 | bytes 33804300 | tf_op jit(solution)/shard_map/sub | solution.py:636
  733.1 13.3 %multiply_subtract_fusion = (f32[1572,768]{1,0:T(8,128)}, f32[1572,768]{1,0:T(8,128)}, f32[1572,768]{1,0:T(8,128)}) fusion(f32[1572,768]{1,0:T(8,128)} %param.35, f32[]{:T(128)} %bitcast.88, f32[]{:T(128)} %bitcast.87, f32[1572,768]{1,0:T(8,128)} %get-tuple-element.228, f32[]{:T(128)S(6)} %min.3, f32[1572,768]{1,0:T(8,128)} %param.37, f32[1572,768]{1,0:T(8,128)} %param.36), kind=kLoop, calls=%fused_computation.28 | loop fusion | flops 19316736 | bytes 33804300 | tf_op jit(solution)/shard_map/sub | solution.py:636
  751.6 4.1 collective-permute-done.34
  (501 shorter events, 176.1 us)
Async XLA Ops:
  7.2 119.6 %all-gather.3.cloned.1.call-start = ((), (), s32[]{:S(2)}) async-start(), calls=%async_computation.8 | async-start | bytes 8718336 | tf_op jit(solution)/shard_map/all_gather | solution.py:691
  10.8 176.4 %all-gather.5.cloned.1.call-start = ((), (), s32[]{:S(2)}) async-start(), calls=%async_computation.9 | async-start | bytes 6082560 | tf_op jit(solution)/shard_map/all_gather | solution.py:693
  56.8 66.5 %all-to-all-start = ((bf16[32,24,1024]{2,1,0:T(8,128)(2,1)}), bf16[32,24,1024]{2,1,0:T(8,128)(2,1)}, u32[]{:S(2)}, u32[]{:S(2)}) async-start(bf16[32,24,1024]{2,1,0:T(8,128)(2,1)} %shard_map.409), calls=%async_computation | async-start | bytes 3145728 | tf_op jit(solution)/shard_map/all_to_all | solution.py:683
  206.4 5.1 collective-permute-start
  208.8 6.3 collective-permute-start.5
  211.5 5.6 collective-permute-start.1
  215.1 4.7 collective-permute-start.6
  217.2 5.7 collective-permute-start.2
  219.8 7.9 %collective-permute-start.7 = (bf16[4,32,768]{2,1,0:T(8,128)(2,1)S(1)}, bf16[4,32,768]{2,1,0:T(8,128)(2,1)S(1)}, u32[]{:S(2)}, u32[]{:S(2)}) collective-permute-start(bf16[4,32,768]{2,1,0:T(8,128)(2,1)S(1)} %pad_maximum_fusion.12), channel_id=1, source_target_pairs={{0,8},{1,9},{2,10},{3,11},{4,12},{5,13},{6,14},{7,15},{8,0},{9,1},... | collective-permute-start | bytes 589832 | tf_op jit(solution)/shard_map/ppermute | solution.py:619
  222.9 10.9 %collective-permute-start.3 = (bf16[8,32,768]{2,1,0:T(8,128)(2,1)S(1)}, bf16[8,32,768]{2,1,0:T(8,128)(2,1)S(1)}, u32[]{:S(2)}, u32[]{:S(2)}) collective-permute-start(bf16[8,32,768]{2,1,0:T(8,128)(2,1)S(1)} %pad_maximum_fusion.8), channel_id=1, source_target_pairs={{0,8},{1,9},{2,10},{3,11},{4,12},{5,13},{6,14},{7,15},{8,0},{9,1},... | collective-permute-start | bytes 1179656 | tf_op jit(solution)/shard_map/ppermute | solution.py:619
  227.8 7.8 %collective-permute-start.8 = (bf16[8,32,768]{2,1,0:T(8,128)(2,1)S(1)}, bf16[8,32,768]{2,1,0:T(8,128)(2,1)S(1)}, u32[]{:S(2)}, u32[]{:S(2)}) collective-permute-start(bf16[8,32,768]{2,1,0:T(8,128)(2,1)S(1)} %pad_maximum_fusion.9), channel_id=1, source_target_pairs={{0,16},{1,17},{2,18},{3,19},{4,20},{5,21},{6,22},{7,23},{8,24},{9,... | collective-permute-start | bytes 1179656 | tf_op jit(solution)/shard_map/ppermute | solution.py:619
  233.9 2.4 collective-permute-start.4
  235.7 2.4 collective-permute-start.9
  255.9 11.9 %all-to-all-start.1 = ((f32[32,1,192]{2,1,0:T(1,128)}), f32[32,1,192]{2,1,0:T(1,128)S(1)}, u32[]{:S(2)}, u32[]{:S(2)}) async-start(f32[32,1,192]{2,1,0:T(1,128)} %reshape.550), calls=%async_computation.1 | async-start | bytes 65536 | tf_op jit(solution)/shard_map/all_to_all | solution.py:745
  269.5 9.6 %all-to-all-start.2 = ((f32[32,1,64]{2,1,0:T(1,128)}), f32[32,1,64]{2,1,0:T(1,128)S(1)}, u32[]{:S(2)}, u32[]{:S(2)}) async-start(f32[32,1,64]{2,1,0:T(1,128)} %broadcast_in_dim.45), calls=%async_computation.2 | async-start | bytes 32768 | tf_op jit(solution)/shard_map/all_to_all | solution.py:625
  272.1 421.2 %reduce-scatter.5.cloned.1.call-start = ((), (), s32[]{:S(2)}) async-start(), calls=%async_computation.11 | async-start | bytes 12165120 | tf_op jit(solution)/shard_map/reduce_scatter | solution.py:781
  297.8 11.5 %collective-permute-start.10 = (f32[2,2,2,2,32,768]{5,4,3,2,1,0:T(8,128)S(1)}, f32[2,2,2,2,32,768]{5,4,3,2,1,0:T(8,128)S(1)}, u32[]{:S(2)}, u32[]{:S(2)}) collective-permute-start(f32[2,2,2,2,32,768]{5,4,3,2,1,0:T(8,128)S(1)} %bitcast.293), channel_id=1, source_target_pairs={{0,1},{1,0},{2,3},{3,2},{4,5},{5,4},{6,7},{7,6},{8,9},{9,8},{10,11... | collective-permute-start | bytes 4718600 | tf_op jit(solution)/shard_map/ppermute | solution.py:520
  297.9 11.4 %collective-permute-start.11 = (f32[2,2,2,2,32,768]{5,4,3,2,1,0:T(8,128)S(1)}, f32[2,2,2,2,32,768]{5,4,3,2,1,0:T(8,128)S(1)}, u32[]{:S(2)}, u32[]{:S(2)}) collective-permute-start(f32[2,2,2,2,32,768]{5,4,3,2,1,0:T(8,128)S(1)} %bitcast.292), channel_id=1, source_target_pairs={{0,1},{1,0},{2,3},{3,2},{4,5},{5,4},{6,7},{7,6},{8,9},{9,8},{10,11... | collective-permute-start | bytes 4718600 | tf_op jit(solution)/shard_map/ppermute | solution.py:520
  312.0 19.4 %collective-permute-start.12 = (f32[2,2,2,32,768]{4,3,2,1,0:T(8,128)S(1)}, f32[2,2,2,32,768]{4,3,2,1,0:T(8,128)}, u32[]{:S(2)}, u32[]{:S(2)}) collective-permute-start(f32[2,2,2,32,768]{4,3,2,1,0:T(8,128)S(1)} %slice_bitcast_fusion.5), channel_id=1, source_target_pairs={{0,8},{1,9},{2,10},{3,11},{4,12},{5,13},{6,14},{7,15},{8,0},{9,1},... | collective-permute-start | bytes 2359304 | tf_op jit(solution)/shard_map/ppermute | solution.py:520
  312.6 19.3 %collective-permute-start.13 = (f32[2,2,2,32,768]{4,3,2,1,0:T(8,128)}, f32[2,2,2,32,768]{4,3,2,1,0:T(8,128)}, u32[]{:S(2)}, u32[]{:S(2)}) collective-permute-start(f32[2,2,2,32,768]{4,3,2,1,0:T(8,128)} %slice_bitcast_fusion.4), channel_id=1, source_target_pairs={{0,16},{1,17},{2,18},{3,19},{4,20},{5,21},{6,22},{7,23},{8,24},{9,... | collective-permute-start | bytes 2359304 | tf_op jit(solution)/shard_map/ppermute | solution.py:520
  334.9 9.8 %collective-permute-start.14 = (f32[2,2,32,768]{3,2,1,0:T(8,128)S(1)}, f32[2,2,32,768]{3,2,1,0:T(8,128)S(1)}, u32[]{:S(2)}, u32[]{:S(2)}) collective-permute-start(f32[2,2,32,768]{3,2,1,0:T(8,128)S(1)} %slice_bitcast_fusion.9), channel_id=1, source_target_pairs={{0,16},{1,17},{2,18},{3,19},{4,20},{5,21},{6,22},{7,23},{8,24},{9,... | collective-permute-start | bytes 1179656 | tf_op jit(solution)/shard_map/ppermute | solution.py:520
  335.6 9.4 %collective-permute-start.15 = (f32[2,2,32,768]{3,2,1,0:T(8,128)S(1)}, f32[2,2,32,768]{3,2,1,0:T(8,128)S(1)}, u32[]{:S(2)}, u32[]{:S(2)}) collective-permute-start(f32[2,2,32,768]{3,2,1,0:T(8,128)S(1)} %slice_bitcast_fusion.8), channel_id=1, source_target_pairs={{0,8},{1,9},{2,10},{3,11},{4,12},{5,13},{6,14},{7,15},{8,0},{9,1},... | collective-permute-start | bytes 1179656 | tf_op jit(solution)/shard_map/ppermute | solution.py:520
  345.2 6.4 collective-permute-start.16
  345.8 8.0 %collective-permute-start.17 = (f32[2,32,768]{2,1,0:T(8,128)S(1)}, f32[2,32,768]{2,1,0:T(8,128)S(1)}, u32[]{:S(2)}, u32[]{:S(2)}) collective-permute-start(f32[2,32,768]{2,1,0:T(8,128)S(1)} %slice_bitcast_fusion.12), channel_id=1, source_target_pairs={{0,2},{1,3},{2,0},{3,1},{4,6},{5,7},{6,4},{7,5},{8,10},{9,11},{10,... | collective-permute-start | bytes 589832 | tf_op jit(solution)/shard_map/ppermute | solution.py:520
  353.8 7.7 collective-permute-start.18
  354.4 8.1 %collective-permute-start.19 = (f32[32,768]{1,0:T(8,128)S(1)}, f32[32,768]{1,0:T(8,128)S(1)}, u32[]{:S(2)}, u32[]{:S(2)}) collective-permute-start(f32[32,768]{1,0:T(8,128)S(1)} %slice_bitcast_fusion.16), channel_id=1, source_target_pairs={{0,4},{1,5},{2,6},{3,7},{4,0},{5,1},{6,2},{7,3},{8,12},{9,13},{10,... | collective-permute-start | bytes 294920 | tf_op jit(solution)/shard_map/ppermute | solution.py:520
  387.6 312.4 %reduce-scatter.3.cloned.1.call-start = ((), (), s32[]{:S(2)}) async-start(), calls=%async_computation.10 | async-start | bytes 9732096 | tf_op jit(solution)/shard_map/reduce_scatter | solution.py:798
  443.0 21.3 %collective-permute-start.20 = (f32[384,2304]{1,0:T(8,128)}, f32[384,2304]{1,0:T(8,128)}, u32[]{:S(2)}, u32[]{:S(2)}) collective-permute-start(f32[384,2304]{1,0:T(8,128)} %fusion.64), channel_id=1, source_target_pairs={{0,1},{1,0},{2,3},{3,2},{4,5},{5,4},{6,7},{7,6},{8,9},{9,8},{10,11... | collective-permute-start | bytes 10616840 | tf_op jit(solution)/shard_map/ppermute | solution.py:548
  472.0 27.3 %collective-permute-start.21 = (f32[2,2,2,24,1152]{4,3,2,1,0:T(8,128)}, f32[2,2,2,24,1152]{4,3,2,1,0:T(8,128)S(1)}, u32[]{:S(2)}, u32[]{:S(2)}) collective-permute-start(f32[2,2,2,24,1152]{4,3,2,1,0:T(8,128)} %dynamic-slice_bitcast_fusion.1), channel_id=1, source_target_pairs={{0,8},{1,9},{2,10},{3,11},{4,12},{5,13},{6,14},{7,15},{8,0},{9,1},... | collective-permute-start | bytes 2654216 | tf_op jit(solution)/shard_map/ppermute | solution.py:520
  473.4 26.7 %collective-permute-start.22 = (f32[2,2,2,24,1152]{4,3,2,1,0:T(8,128)}, f32[2,2,2,24,1152]{4,3,2,1,0:T(8,128)}, u32[]{:S(2)}, u32[]{:S(2)}) collective-permute-start(f32[2,2,2,24,1152]{4,3,2,1,0:T(8,128)} %dynamic-slice_bitcast_fusion), channel_id=1, source_target_pairs={{0,16},{1,17},{2,18},{3,19},{4,20},{5,21},{6,22},{7,23},{8,24},{9,... | collective-permute-start | bytes 2654216 | tf_op jit(solution)/shard_map/ppermute | solution.py:520
  508.7 19.8 %collective-permute-start.23 = (f32[2,2,24,1152]{3,2,0,1:T(8,128)S(1)}, f32[2,2,24,1152]{3,2,0,1:T(8,128)S(1)}, u32[]{:S(2)}, u32[]{:S(2)}) collective-permute-start(f32[2,2,24,1152]{3,2,0,1:T(8,128)S(1)} %bitcast.295), channel_id=1, source_target_pairs={{0,16},{1,17},{2,18},{3,19},{4,20},{5,21},{6,22},{7,23},{8,24},{9,... | collective-permute-start | bytes 1327112 | tf_op jit(solution)/shard_map/ppermute | solution.py:520
  510.2 18.4 %collective-permute-start.24 = (f32[2,2,24,1152]{3,2,0,1:T(8,128)S(1)}, f32[2,2,24,1152]{3,2,0,1:T(8,128)}, u32[]{:S(2)}, u32[]{:S(2)}) collective-permute-start(f32[2,2,24,1152]{3,2,0,1:T(8,128)S(1)} %bitcast.294), channel_id=1, source_target_pairs={{0,8},{1,9},{2,10},{3,11},{4,12},{5,13},{6,14},{7,15},{8,0},{9,1},... | collective-permute-start | bytes 1327112 | tf_op jit(solution)/shard_map/ppermute | solution.py:520
  532.2 57.2 %all-to-all-start.3 = ((bf16[32,24,1024]{2,1,0:T(8,128)(2,1)}), bf16[32,24,1024]{2,1,0:T(8,128)(2,1)S(1)}, u32[]{:S(2)}, u32[]{:S(2)}) async-start(bf16[32,24,1024]{2,1,0:T(8,128)(2,1)} %bitcast.283), calls=%async_computation.3 | async-start | bytes 3145728 | tf_op jit(solution)/shard_map/all_to_all | solution.py:805
  535.9 53.6 %collective-permute-start.25 = (f32[2,24,1152]{2,1,0:T(8,128)}, f32[2,24,1152]{2,1,0:T(8,128)S(1)}, u32[]{:S(2)}, u32[]{:S(2)}) collective-permute-start(f32[2,24,1152]{2,1,0:T(8,128)} %dynamic-slice_bitcast_fusion.3), channel_id=1, source_target_pairs={{0,2},{1,3},{2,0},{3,1},{4,6},{5,7},{6,4},{7,5},{8,10},{9,11},{10,... | collective-permute-start | bytes 663560 | tf_op jit(solution)/shard_map/ppermute | solution.py:520
  537.8 51.7 %collective-permute-start.26 = (f32[2,24,1152]{2,1,0:T(8,128)S(1)}, f32[2,24,1152]{2,1,0:T(8,128)S(1)}, u32[]{:S(2)}, u32[]{:S(2)}) collective-permute-start(f32[2,24,1152]{2,1,0:T(8,128)S(1)} %dynamic-slice_bitcast_fusion.2), channel_id=1, source_target_pairs={{0,2},{1,3},{2,0},{3,1},{4,6},{5,7},{6,4},{7,5},{8,10},{9,11},{10,... | collective-permute-start | bytes 663560 | tf_op jit(solution)/shard_map/ppermute | solution.py:520
  589.6 97.3 %collective-permute-start.29 = (f32[384,3072]{1,0:T(8,128)}, f32[384,3072]{1,0:T(8,128)}, u32[]{:S(2)}, u32[]{:S(2)}) collective-permute-start(f32[384,3072]{1,0:T(8,128)} %copy-done.14), channel_id=1, source_target_pairs={{0,1},{1,0},{2,3},{3,2},{4,5},{5,4},{6,7},{7,6},{8,9},{9,8},{10,11... | collective-permute-start | bytes 14155784 | tf_op jit(solution)/shard_map/ppermute | solution.py:548
  590.4 92.5 %all-to-all-start.4 = ((f32[32,1,336]{2,1,0:T(1,128)}), f32[32,1,336]{2,1,0:T(1,128)S(1)}, u32[]{:S(2)}, u32[]{:S(2)}) async-start(f32[32,1,336]{2,1,0:T(1,128)} %reshape.529), calls=%async_computation.6 | async-start | bytes 98304 | tf_op jit(solution)/shard_map/all_to_all | solution.py:827
  600.8 82.8 %collective-permute-start.27 = (f32[24,1152]{1,0:T(8,128)S(1)}, f32[24,1152]{1,0:T(8,128)S(1)}, u32[]{:S(2)}, u32[]{:S(2)}) collective-permute-start(f32[24,1152]{1,0:T(8,128)S(1)} %dynamic-slice_bitcast_fusion.5), channel_id=1, source_target_pairs={{0,4},{1,5},{2,6},{3,7},{4,0},{5,1},{6,2},{7,3},{8,12},{9,13},{10,... | collective-permute-start | bytes 331784 | tf_op jit(solution)/shard_map/ppermute | solution.py:520
  603.7 79.9 %collective-permute-start.28 = (f32[24,1152]{1,0:T(8,128)S(1)}, f32[24,1152]{1,0:T(8,128)S(1)}, u32[]{:S(2)}, u32[]{:S(2)}) collective-permute-start(f32[24,1152]{1,0:T(8,128)S(1)} %dynamic-slice_bitcast_fusion.4), channel_id=1, source_target_pairs={{0,4},{1,5},{2,6},{3,7},{4,0},{5,1},{6,2},{7,3},{8,12},{9,13},{10,... | collective-permute-start | bytes 331784 | tf_op jit(solution)/shard_map/ppermute | solution.py:520
  705.0 10.6 %all-to-all-start.5 = ((f32[32,1,2]{2,1,0:T(1,128)}), f32[32,1,2]{2,1,0:T(1,128)}, u32[]{:S(2)}, u32[]{:S(2)}) async-start(f32[32,1,2]{2,1,0:T(1,128)} %broadcast_in_dim.84), calls=%async_computation.7 | async-start | bytes 32768 | tf_op jit(solution)/shard_map/all_to_all | solution.py:625
  710.0 19.1 %collective-permute-start.30 = (bf16[2,2,2,24,1536]{4,3,2,1,0:T(8,128)(2,1)S(1)}, bf16[2,2,2,24,1536]{4,3,2,1,0:T(8,128)(2,1)}, u32[]{:S(2)}, u32[]{:S(2)}) collective-permute-start(bf16[2,2,2,24,1536]{4,3,2,1,0:T(8,128)(2,1)S(1)} %fusion.70), channel_id=1, source_target_pairs={{0,8},{1,9},{2,10},{3,11},{4,12},{5,13},{6,14},{7,15},{8,0},{9,1},... | collective-permute-start | bytes 1769480 | tf_op jit(solution)/shard_map/ppermute | solution.py:520
  711.8 17.3 %collective-permute-start.31 = (bf16[2,2,2,24,1536]{4,3,1,2,0:T(8,128)(2,1)S(1)}, bf16[2,2,2,24,1536]{4,3,1,2,0:T(8,128)(2,1)}, u32[]{:S(2)}, u32[]{:S(2)}) collective-permute-start(bf16[2,2,2,24,1536]{4,3,1,2,0:T(8,128)(2,1)S(1)} %fusion.71), channel_id=1, source_target_pairs={{0,16},{1,17},{2,18},{3,19},{4,20},{5,21},{6,22},{7,23},{8,24},{9,... | collective-permute-start | bytes 1769480 | tf_op jit(solution)/shard_map/ppermute | solution.py:520
  731.7 17.0 %collective-permute-start.32 = (bf16[2,2,24,1536]{3,2,1,0:T(8,128)(2,1)S(1)}, bf16[2,2,24,1536]{3,2,1,0:T(8,128)(2,1)S(1)}, u32[]{:S(2)}, u32[]{:S(2)}) collective-permute-start(bf16[2,2,24,1536]{3,2,1,0:T(8,128)(2,1)S(1)} %fusion.77), channel_id=1, source_target_pairs={{0,16},{1,17},{2,18},{3,19},{4,20},{5,21},{6,22},{7,23},{8,24},{9,... | collective-permute-start | bytes 884744 | tf_op jit(solution)/shard_map/ppermute | solution.py:520
  732.4 16.3 %collective-permute-start.33 = (bf16[2,2,24,1536]{3,2,0,1:T(8,128)(2,1)S(1)}, bf16[2,2,24,1536]{3,2,0,1:T(8,128)(2,1)S(1)}, u32[]{:S(2)}, u32[]{:S(2)}) collective-permute-start(bf16[2,2,24,1536]{3,2,0,1:T(8,128)(2,1)S(1)} %fusion.78), channel_id=1, source_target_pairs={{0,8},{1,9},{2,10},{3,11},{4,12},{5,13},{6,14},{7,15},{8,0},{9,1},... | collective-permute-start | bytes 884744 | tf_op jit(solution)/shard_map/ppermute | solution.py:520
  748.9 6.8 collective-permute-start.34
  749.5 7.8 %collective-permute-start.35 = (bf16[2,24,1536]{2,1,0:T(8,128)(2,1)S(1)}, bf16[2,24,1536]{2,1,0:T(8,128)(2,1)S(1)}, u32[]{:S(2)}, u32[]{:S(2)}) collective-permute-start(bf16[2,24,1536]{2,1,0:T(8,128)(2,1)S(1)} %fusion.89), channel_id=1, source_target_pairs={{0,2},{1,3},{2,0},{3,1},{4,6},{5,7},{6,4},{7,5},{8,10},{9,11},{10,... | collective-permute-start | bytes 442376 | tf_op jit(solution)/shard_map/ppermute | solution.py:520
  757.4 7.5 collective-permute-start.36
  758.0 7.8 %collective-permute-start.37 = (bf16[24,1536]{1,0:T(8,128)(2,1)S(1)}, bf16[24,1536]{1,0:T(8,128)(2,1)S(1)}, u32[]{:S(2)}, u32[]{:S(2)}) collective-permute-start(bf16[24,1536]{1,0:T(8,128)(2,1)S(1)} %fusion.93), channel_id=1, source_target_pairs={{0,4},{1,5},{2,6},{3,7},{4,0},{5,1},{6,2},{7,3},{8,12},{9,13},{10,... | collective-permute-start | bytes 221192 | tf_op jit(solution)/shard_map/ppermute | solution.py:520
  (81 other events, 1084.4 us)
Sparse Core Ops, SparseCore 0:
  11.5 104.8 all-gather.2
  119.9 67.1 all-gather.4
  387.7 158.4 reduce-scatter.4
  553.0 147.0 reduce-scatter.2

commit v4 on v3

--- a/solution.py
+++ b/solution.py
@@ -78,7 +78,7 @@
     @pl.when(pl.program_id(0) == 0)
     def _():
         chunks = vocab // LANES
-        many = 8
+        many = 16
         filler = jnp.zeros((pad - width, LANES), full_type)
 
         def build(start):
@@ -800,14 +800,6 @@
     grad_embedded = grad_residual + norm_back(
         grad_first * gain_first + grad_second * gain_second, normed, inv_std
     )
-    sending = grad_embedded.astype(half_type).T.reshape(count, own_width, tokens)
-    sending, grad_hidden_late = advance((sending, grad_hidden), live)
-    returned = lax.all_to_all(sending, AXES, split_axis=0, concat_axis=0, tiled=True)
-
-    rot_out = jnp.dot(grad_hidden_late, basis_out, preferred_element_type=full_type).astype(half_type)
-    scale_other, scale_own = document_squares(rot_in, rot_out, segments, total)
-    scale_step = FirstStep(scale_other, scale_own, own_width, half_type)
-    scale_live = [scale_step]
     vector_grad = jnp.concatenate(
         [
             jnp.sum(grad_mixed.astype(full_type), 0),
@@ -821,22 +813,30 @@
             jnp.sum(grad_final * normed_last, 0),
         ]
     )
-    returned, vector_grad = advance((returned, vector_grad), live)
-    returned, vector_grad = advance((returned, vector_grad), scale_live)
-    own_vector = jnp.sum(
-        lax.all_to_all(
-            vector_grad.reshape(count, 1, -1), AXES, split_axis=0, concat_axis=0, tiled=True
-        ),
-        (0, 1),
-    )
+    sending = grad_embedded.astype(half_type).T.reshape(count, own_width, tokens)
+    sending, grad_hidden_late, vector_grad = advance((sending, grad_hidden, vector_grad), live)
+    returned = lax.all_to_all(sending, AXES, split_axis=0, concat_axis=0, tiled=True)
+    rot_out = jnp.dot(grad_hidden_late, basis_out, preferred_element_type=full_type).astype(half_type)
+    rot_out, vector_grad = lax.optimization_barrier((rot_out, vector_grad))
+    vector_parts = lax.all_to_all(
+        vector_grad.reshape(count, 1, -1), AXES, split_axis=0, concat_axis=0, tiled=True
+    )
+    scale_other, scale_own = document_squares(rot_in, rot_out, segments, total)
+    scale_step = FirstStep(scale_other, scale_own, own_width, half_type)
+    scale_live = [scale_step]
+    returned, vector_parts = advance((returned, vector_parts), live)
+    returned = advance(returned, scale_live)
+    own_vector = jnp.sum(vector_parts, (0, 1))
     grad_in_table, in_squares = scatter_features(returned, places, vocab)
     in_squares = run_all(in_squares, live)
     own_in = in_step.finished()
     grads = (grad_in_table, grad_out_table, own_in, own_up, own_mix, own_vector)
     squares = jnp.sum(in_squares) + out_squares
     squares = squares + sum((jnp.sum(gradient * gradient) for gradient in grads[2:]))
-    both = jnp.sum(shared_by_all(jnp.stack([squares, loss_part])[None], count), (0, 1))
-    advance(jnp.zeros((), full_type), scale_live)
+    norm_parts = jnp.stack([squares, loss_part])
+    both = jnp.sum(shared_by_all(norm_parts[None], count), (0, 1))
+    advance(norm_parts, scale_live)
+    both = advance(both, scale_live)
     grad_norm = jnp.sqrt(both[0])
     loss_value = both[1]
     factor = jnp.minimum(1.0, clip_limit / (grad_norm + 1e-06))

time: 785 us -> 804 us (1.024)
  waiting for transfers between devices: 159 us -> 170 us
  blocking collectives: 0 us -> 10.5 us
    all_to_all x0 -> x1, blocking collectives: none -> 10.5 us  [per_device(): lax.all_to_all(vector_grad.reshape(count, 1, -1), AXES, split_axis=0, con...]
    unnamed x179 -> x195, local copies, waits for them, and re-layouts: 23.5 us -> 26.5 us
  transfers between devices with their start and end apart: 48 -> 47, of which waited for: 29 -> 28; matrix products, arithmetic and copies ran while one was open for 27% -> 26% of each run, Pallas kernels for 25% -> 25%
where the time goes in v4:
time: 804 us; the launch traced here: 793 us
  Pallas kernels  196 us (24%)
  waiting for transfers between devices  170 us (21%)
  matrix products  146 us (18%)
  other arithmetic  126 us (16%)
  starting transfers between devices  63.5 us (8%)
  local copies, waits for them, and re-layouts  56.9 us (7%)
  between operations  24.3 us (3%)
  blocking collectives  10.5 us (1%)
    pallas_call x1, Pallas kernels, scatter_features(): pl.pallas_call(scatter_kernel, out_shape=(jax.ShapeDtypeStruct((width, vo...  79.1 us
    ppermute x26, waiting for transfers between devices, send(): lax.ppermute(ready, AXES, partner_pairs(lax.axis_size(AXES), self.order.p...  60.7 us
    all_to_all x1, waiting for transfers between devices, per_device(): lax.all_to_all(columns, AXES, split_axis=0, concat_axis=0, tiled=True)  55.9 us
    pallas_call x1, Pallas kernels, gather_features(): pl.pallas_call(gather_kernel, out_shape=jax.ShapeDtypeStruct((count, widt...  38.9 us
    pallas_call x1, Pallas kernels, attention_backward(): pl.pallas_call(backward_kernel, out_shape=jax.ShapeDtypeStruct((3, tokens...  32.7 us
    ppermute x26, starting transfers between devices, send(): lax.ppermute(ready, AXES, partner_pairs(lax.axis_size(AXES), self.order.p...  28.5 us
    sub x6, other arithmetic, adam_update(): weight - rate * (update + weight_decay * weight)  27.8 us
    unnamed x195, local copies, waits for them, and re-layouts  26.5 us
  transfers between devices with their start and end apart: 47, of which 28 were waited for; matrix products, arithmetic and copies ran while one was open for 26% of the time, Pallas kernels for 25%

profile of v4, /device:TPU:0, one launch (start us, length us, event | category | flops | bytes accessed | tf_op | source)
XLA Modules:
  0.0 792.7 jit_solution(1911191580198960976)
XLA Ops:
  16.2 38.9 %shard_map.409 = bf16[32,24,1024]{2,1,0:T(8,128)(2,1)} custom-call(s32[32,1,1024]{2,1,0:T(1,128)S(1)} %reshape_reshape.3.ids_ref, f32[24,50304]{1,0:T(8,128)S(1)} %copy-done.2), custom_call_target="tpu_custom_call" | custom-call | tf_op jit(solution)/shard_map/pallas_call | solution.py:123
  55.1 7.4 all-to-all-start
  67.3 55.9 %all-to-all-done = bf16[32,24,1024]{2,1,0:T(8,128)(2,1)} async-done(((bf16[32,24,1024]{2,1,0:T(8,128)(2,1)}), bf16[32,24,1024]{2,1,0:T(8,128)(2,1)}, u32[]{:S(2)}, u32[]{:S(2)}) %all-to-all-start) | async-done | bytes 1572896 | tf_op jit(solution)/shard_map/all_to_all | solution.py:683
  130.4 9.5 %convolution_add_fusion.query_in.key_in.value_in = f32[1024,2304]{1,0:T(8,128)} fusion(bf16[1024,768]{0,1:T(8,128)(2,1)S(1)} %get-tuple-element.301, f32[2304]{0:T(1024)S(1)} %slice.186, bf16[768,5504]{1,0:T(8,128)(2,1)} %all-gather.3.cloned.1.call-done), kind=kOutput, calls=%fused_computation.23 | convolution fusion | flops 3626237952 | bytes 14558208 | tf_op jit(solution)/shard_map/dot_general | solution.py:716
  139.9 21.2 %shard_map.410 = (bf16[1024,768]{1,0:T(8,128)(2,1)S(1)}, bf16[1024,768]{1,0:T(8,128)(2,1)S(1)}, bf16[1024,768]{1,0:T(8,128)(2,1)S(1)}, bf16[1024,768]{1,0:T(8,128)(2,1)S(1)}, f32[2,6,2,512]{3,2,1,0:T(2,128)S(1)}) custom-call(f32[1024,2304]{1,0:T(8,128)} %convolution_add_fusion.query_in.key_in.value_in, ...), custom_call_target="tpu_custom_call" | custom-call | tf_op jit(solution)/shard_map/pallas_call | solution.py:329
  165.7 10.1 %multiply_convert_fusion = (bf16[1024,3072]{1,0:T(8,128)(2,1)}, f32[1024,3072]{1,0:T(8,128)}) fusion(f32[3072]{0:T(1024)S(1)} %slice.190, bf16[1024,768]{0,1:T(8,128)(2,1)S(1)} %get-tuple-element.146, bf16[768,5504]{1,0:T(8,128)(2,1)S(1)} %bitcast.329), kind=kOutput, calls=%fused_computation.17 | convolution fusion | flops 4850712576 | bytes 25178112 | tf_op jit(solution)/shard_map/dot_general | solution.py:719
  175.8 12.4 %all-gather.5.cloned.1.call-done = bf16[3840,768]{1,0:T(8,128)(2,1)} async-done(((bf16[120,768]{1,0:T(8,128)(2,1)}), bf16[3840,768]{1,0:T(8,128)(2,1)}) %all-gather.5.cloned.1.call-update) | async-done | bytes 5898256 | tf_op jit(solution)/shard_map/all_gather | solution.py:693
  188.1 10.9 %fusion.145 = (f32[1024]{0:T(1024)S(1)}, f32[1024,768]{0,1:T(8,128)S(1)}) fusion(f32[768]{0:T(1024)S(1)} %get-tuple-element.340, bf16[3840,768]{1,0:T(8,128)(2,1)} %all-gather.5.cloned.1.call-done, bf16[1024,3072]{1,0:T(8,128)(2,1)} %get-tuple-element.358, bf16[1024,768]{1,0:T(8,128)(2,1)} %copy-done.15, bf16[32,24,1024]{2,1,0:T(8,128)(2,1)} %all-to-all-done), kind=kOutput, calls=%fused_computation.371 | convolution fusion | flops 6058671104 | bytes 18488320 | tf_op jit(solution)/shard_map/dot_general | solution.py:722
  230.4 4.5 collective-permute-done.3
  240.3 8.2 %fusion.146 = (f32[2048]{0:T(1024)S(1)}, f32[2048,1572]{0,1:T(8,128)}) fusion(bf16[2048,768]{1,0:T(8,128)(2,1)S(1)} %bitcast.298, f32[1572,768]{1,0:T(8,128)S(1)} %bitcast.289), kind=kOutput, calls=%fused_computation.372 | convolution fusion | flops 4949509120 | bytes 20860928 | tf_op jit(solution)/shard_map/rd,vd->rv/dot_general | solution.py:737
  248.6 6.8 exponential_reduce_fusion
  257.1 4.4 all-to-all-start.1
  261.5 7.2 all-to-all-done.1
  273.2 6.9 all-to-all-done.2
  281.8 7.3 fusion.3
  289.1 9.0 %fusion.55 = f32[2048,768]{1,0:T(8,128)S(1)} fusion(bf16[2048,1572]{0,1:T(8,128)(2,1)S(1)} %fusion.3, f32[1572,768]{1,0:T(8,128)} %param.35), kind=kOutput, calls=%fused_computation.99 | convolution fusion | flops 4946291712 | bytes 17559552 | tf_op jit(solution)/shard_map/dot_general | solution.py:758
  302.2 8.1 %multiply_reduce_fusion = (f32[]{:T(128)}, f32[1572,768]{1,0:T(8,128)}) fusion(bf16[2048,1572]{0,1:T(8,128)(2,1)S(1)} %fusion.3, bf16[2048,768]{1,0:T(8,128)(2,1)S(1)} %bitcast.299), kind=kOutput, calls=%fused_computation.30 | convolution fusion | flops 4947499008 | bytes 14413828 | tf_op jit(solution)/shard_map/rv,rd->vd/dot_general | solution.py:765
  314.2 5.2 convolution_convert_fusion.2.in_ref
  319.3 13.1 %collective-permute-done.12 = f32[2,2,2,32,768]{4,3,2,1,0:T(8,128)} collective-permute-done((f32[2,2,2,32,768]{4,3,2,1,0:T(8,128)S(1)}, f32[2,2,2,32,768]{4,3,2,1,0:T(8,128)}, u32[]{:S(2)}, u32[]{:S(2)}) %collective-permute-start.12) | collective-permute-done | bytes 786464 | tf_op jit(solution)/shard_map/ppermute | solution.py:520
  338.0 7.6 collective-permute-done.14
  348.2 4.3 collective-permute-done.16
  357.7 4.7 collective-permute-done.18
  366.4 3.5 copy.216
  369.9 4.0 multiply_reduce_fusion.1
  378.8 9.7 %fusion.10 = f32[3840,768]{1,0:T(8,128)} fusion(bf16[1024,768]{0,1:T(8,128)(2,1)S(1)} %convert_element_type.209, bf16[1024,3072]{1,0:T(8,128)(2,1)S(1)} %bitcast.334, bf16[1024,768]{1,0:T(8,128)(2,1)S(1)} %copy-done.16), kind=kOutput, calls=%fused_computation.25 | convolution fusion | flops 6055526400 | bytes 21233664 | tf_op jit(solution)/shard_map/sa,sb->ab/dot_general | solution.py:779
  388.6 12.9 %fusion.147 = f32[1024,3840]{1,0:T(8,128)} fusion(bf16[1024,768]{0,1:T(8,128)(2,1)} %copy-done.36, bf16[3840,768]{1,0:T(8,128)(2,1)} %all-gather.5.cloned.1.call-done), kind=kOutput, calls=%fused_computation.373 | convolution fusion | flops 6039797760 | bytes 23199744 | tf_op jit(solution)/shard_map/sb,ab->sa/dot_general | solution.py:782
  404.7 32.7 %shard_map.411 = bf16[3,1024,768]{2,1,0:T(8,128)(2,1)S(1)} custom-call(bf16[1024,768]{1,0:T(8,128)(2,1)S(1)} %copy-done.6, bf16[1024,768]{1,0:T(8,128)(2,1)S(1)} %copy-done.8, bf16[1024,768]{1,0:T(8,128)(2,1)S(1)} %copy-done.10, bf16[1024,768]{1,0:T(8,128)(2,1)S(1)} %slice.228.grad_ref, f32[3,512,128]{2,1,0:T(8,128)S(1)} %pad_maximum_fusion.7.tables_ref, ...), custom_call_target="tpu_custom_call" | custom-call | tf_op jit(solution)/shard_map/pallas_call | solution.py:382
  439.2 4.6 fusion.64
  446.0 4.1 pad_maximum_fusion.3
  450.1 5.6 fusion.62
  455.7 9.3 %fusion.9 = bf16[1024,3072]{1,0:T(8,128)(2,1)S(1)} fusion(f32[1024,3840]{1,0:T(8,128)} %fusion.147, f32[1024,3072]{1,0:T(8,128)S(1)} %bitcast.276, f32[3072]{0:T(1024)S(1)} %slice.190), kind=kLoop, calls=%fused_computation.15 | loop fusion | flops 34603008 | bytes 31469568 | tf_op jit(solution)/shard_map/convert_element_type | solution.py:793
  465.0 4.9 add.565
  476.6 6.7 fusion.18
  483.3 7.5 fusion.148
  490.8 9.3 %collective-permute-done.21 = f32[2,2,2,24,1152]{4,3,2,1,0:T(8,128)S(1)} collective-permute-done((f32[2,2,2,24,1152]{4,3,2,1,0:T(8,128)}, f32[2,2,2,24,1152]{4,3,2,1,0:T(8,128)S(1)}, u32[]{:S(2)}, u32[]{:S(2)}) %collective-permute-start.21) | collective-permute-done | bytes 884768 | tf_op jit(solution)/shard_map/ppermute | solution.py:520
  505.9 3.8 copy.220
  512.0 11.2 %fusion.127 = (f32[1024]{0:T(1024)S(1)}, f32[1024]{0:T(1024)S(1)}, f32[768]{0:T(1024)S(1)}, f32[768]{0:T(1024)S(1)}, f32[768]{0:T(1024)S(1)}, /*index=5*/f32[1024,768]{0,1:T(8,128)}) fusion(f32[1024]{0:T(1024)S(1)} %copy-done.53, f32[1024]{0:T(1024)S(1)} %copy-done.51, bf16[32,24,1024]{2,1,0:T(8,128)(2,1)} %all-to-all-done, f32[1024,768]{0,1:T(8,128)} %copy.220, ...), kind=kOutput, calls=%fused_computation.359 | convolution fusion | flops 3634884352 | bytes 16153600 | tf_op jit(solution)/shard_map/sb,ab->sa/dot_general | solution.py:799
  524.2 5.6 fusion.38
  533.5 23.8 %convolution_convert_fusion.out_ref = bf16[1024,3072]{1,0:T(8,128)(2,1)} fusion(bf16[1024,3072]{1,0:T(8,128)(2,1)S(1)} %bitcast.270, bf16[3072,3072]{1,0:T(8,128)(2,1)} %param.51), kind=kOutput, calls=%fused_computation.24 | convolution fusion | flops 19330498560 | bytes 31457280 | tf_op jit(solution)/shard_map/dot_general | solution.py:819
  557.5 10.5 %all_to_all.30 = f32[32,1,336]{2,1,0:T(1,128)S(1)} all-to-all(f32[32,1,336]{2,1,0:T(1,128)S(1)} %reshape.528), channel_id=1, replica_groups=mesh['dp'=4,'fsdp'=8] {'dp','fsdp'}, dimensions={0} | all-to-all | bytes 86016 | tf_op jit(solution)/shard_map/all_to_all | solution.py:821
  574.7 24.1 %shard_map.412 = (f32[384,3072]{1,0:T(8,128)S(1)}, f32[384,3072]{1,0:T(8,128)S(1)}) custom-call(s32[2,5]{1,0:T(2,128)S(1)} %copy.225.starts_ref, f32[1]{0:T(128)} %bitcast.80.total_ref, bf16[1024,768]{1,0:T(8,128)(2,1)S(1)} %copy-done.4, bf16[1024,3072]{1,0:T(8,128)(2,1)} %convolution_convert_fusion.out_ref), custom_call_target="tpu_custom_call" | custom-call | tf_op jit(solution)/shard_map/pallas_call | solution.py:468
  603.3 14.0 %collective-permute-done.26 = f32[2,24,1152]{2,1,0:T(8,128)S(1)} collective-permute-done((f32[2,24,1152]{2,1,0:T(8,128)S(1)}, f32[2,24,1152]{2,1,0:T(8,128)S(1)}, u32[]{:S(2)}, u32[]{:S(2)}) %collective-permute-start.26) | collective-permute-done | bytes 221216 | tf_op jit(solution)/shard_map/ppermute | solution.py:520
  622.2 79.1 %shard_map.413 = (f32[24,50304]{1,0:T(8,128)}, f32[8,128]{1,0:T(8,128)S(1)}) custom-call(s32[32,1,1024]{2,1,0:T(1,128)S(1)} %get-tuple-element.321.places_ref, s32[32,1,1024]{2,1,0:T(1,128)S(1)} %get-tuple-element.320.groups_ref, bf16[32,24,1024]{2,1,0:T(8,128)(2,1)S(1)} %all-to-all-done.3.grad_ref), custom_call_target="tpu_custom_call" | custom-call | tf_op jit(solution)/shard_map/pallas_call | solution.py:214
  711.2 4.5 add.590
  719.8 3.5 all-to-all-start.5
  724.0 9.8 %all-to-all-done.5 = f32[32,1,2]{2,1,0:T(1,128)} async-done(((f32[32,1,2]{2,1,0:T(1,128)}), f32[32,1,2]{2,1,0:T(1,128)}, u32[]{:S(2)}, u32[]{:S(2)}) %all-to-all-start.5) | async-done | bytes 288 | tf_op jit(solution)/shard_map/all_to_all | solution.py:625
  742.7 12.8 %add_subtract_fusion = (f32[24,50304]{1,0:T(8,128)}, f32[24,50304]{1,0:T(8,128)}, f32[24,50304]{1,0:T(8,128)}) fusion(f32[24,50304]{1,0:T(8,128)} %table_ref.1, f32[]{:T(128)} %bitcast.97, f32[]{:T(128)} %bitcast.96, f32[24,50304]{1,0:T(8,128)} %get-tuple-element.207, f32[]{:T(128)S(6)} %min.3, f32[24,50304]{1,0:T(8,128)} %param.34, f32[24,50304]{1,0:T(8,128)} %param.33), kind=kLoop, calls=%fused_computation.32 | loop fusion | flops 18109440 | bytes 33804300 | tf_op jit(solution)/shard_map/sub | solution.py:636
  767.8 6.4 multiply_subtract_fusion
  (521 shorter events, 180.8 us)
Async XLA Ops:
  7.2 307.0 %copy-start = (bf16[768,768]{1,0:T(8,128)(2,1)S(1)}, bf16[768,768]{1,0:T(8,128)(2,1)}, u32[]{:S(2)}) copy-start(bf16[768,768]{1,0:T(8,128)(2,1)} %param.50) | copy-start | bytes 3538948
  7.2 119.6 %all-gather.3.cloned.1.call-start = ((), (), s32[]{:S(2)}) async-start(), calls=%async_computation.8 | async-start | bytes 8718336 | tf_op jit(solution)/shard_map/all_gather | solution.py:691
  10.8 177.3 %all-gather.5.cloned.1.call-start = ((), (), s32[]{:S(2)}) async-start(), calls=%async_computation.9 | async-start | bytes 6082560 | tf_op jit(solution)/shard_map/all_gather | solution.py:693
  55.1 68.2 %all-to-all-start = ((bf16[32,24,1024]{2,1,0:T(8,128)(2,1)}), bf16[32,24,1024]{2,1,0:T(8,128)(2,1)}, u32[]{:S(2)}, u32[]{:S(2)}) async-start(bf16[32,24,1024]{2,1,0:T(8,128)(2,1)} %shard_map.409), calls=%async_computation | async-start | bytes 3145728 | tf_op jit(solution)/shard_map/all_to_all | solution.py:683
  207.4 5.1 collective-permute-start
  209.8 6.3 collective-permute-start.5
  212.5 5.6 collective-permute-start.1
  216.1 4.7 collective-permute-start.6
  218.1 5.7 collective-permute-start.2
  220.8 8.1 %collective-permute-start.7 = (bf16[4,32,768]{2,1,0:T(8,128)(2,1)S(1)}, bf16[4,32,768]{2,1,0:T(8,128)(2,1)S(1)}, u32[]{:S(2)}, u32[]{:S(2)}) collective-permute-start(bf16[4,32,768]{2,1,0:T(8,128)(2,1)S(1)} %pad_maximum_fusion.12), channel_id=1, source_target_pairs={{0,8},{1,9},{2,10},{3,11},{4,12},{5,13},{6,14},{7,15},{8,0},{9,1},... | collective-permute-start | bytes 589832 | tf_op jit(solution)/shard_map/ppermute | solution.py:619
  223.9 10.9 %collective-permute-start.3 = (bf16[8,32,768]{2,1,0:T(8,128)(2,1)S(1)}, bf16[8,32,768]{2,1,0:T(8,128)(2,1)S(1)}, u32[]{:S(2)}, u32[]{:S(2)}) collective-permute-start(bf16[8,32,768]{2,1,0:T(8,128)(2,1)S(1)} %pad_maximum_fusion.8), channel_id=1, source_target_pairs={{0,8},{1,9},{2,10},{3,11},{4,12},{5,13},{6,14},{7,15},{8,0},{9,1},... | collective-permute-start | bytes 1179656 | tf_op jit(solution)/shard_map/ppermute | solution.py:619
  229.0 7.8 collective-permute-start.8
  234.9 2.4 collective-permute-start.4
  236.9 2.4 collective-permute-start.9
  257.1 11.6 %all-to-all-start.1 = ((f32[32,1,192]{2,1,0:T(1,128)}), f32[32,1,192]{2,1,0:T(1,128)S(1)}, u32[]{:S(2)}, u32[]{:S(2)}) async-start(f32[32,1,192]{2,1,0:T(1,128)} %reshape.550), calls=%async_computation.1 | async-start | bytes 65536 | tf_op jit(solution)/shard_map/all_to_all | solution.py:745
  270.5 9.6 %all-to-all-start.2 = ((f32[32,1,64]{2,1,0:T(1,128)}), f32[32,1,64]{2,1,0:T(1,128)S(1)}, u32[]{:S(2)}, u32[]{:S(2)}) async-start(f32[32,1,64]{2,1,0:T(1,128)} %broadcast_in_dim.45), calls=%async_computation.2 | async-start | bytes 32768 | tf_op jit(solution)/shard_map/all_to_all | solution.py:625
  273.0 432.2 %reduce-scatter.5.cloned.1.call-start = ((), (), s32[]{:S(2)}) async-start(), calls=%async_computation.11 | async-start | bytes 12165120 | tf_op jit(solution)/shard_map/reduce_scatter | solution.py:781
  298.7 11.5 %collective-permute-start.10 = (f32[2,2,2,2,32,768]{5,4,3,2,1,0:T(8,128)S(1)}, f32[2,2,2,2,32,768]{5,4,3,2,1,0:T(8,128)S(1)}, u32[]{:S(2)}, u32[]{:S(2)}) collective-permute-start(f32[2,2,2,2,32,768]{5,4,3,2,1,0:T(8,128)S(1)} %bitcast.303), channel_id=1, source_target_pairs={{0,1},{1,0},{2,3},{3,2},{4,5},{5,4},{6,7},{7,6},{8,9},{9,8},{10,11... | collective-permute-start | bytes 4718600 | tf_op jit(solution)/shard_map/ppermute | solution.py:520
  298.8 11.4 %collective-permute-start.11 = (f32[2,2,2,2,32,768]{5,4,3,2,1,0:T(8,128)S(1)}, f32[2,2,2,2,32,768]{5,4,3,2,1,0:T(8,128)S(1)}, u32[]{:S(2)}, u32[]{:S(2)}) collective-permute-start(f32[2,2,2,2,32,768]{5,4,3,2,1,0:T(8,128)S(1)} %bitcast.302), channel_id=1, source_target_pairs={{0,1},{1,0},{2,3},{3,2},{4,5},{5,4},{6,7},{7,6},{8,9},{9,8},{10,11... | collective-permute-start | bytes 4718600 | tf_op jit(solution)/shard_map/ppermute | solution.py:520
  313.0 19.4 %collective-permute-start.12 = (f32[2,2,2,32,768]{4,3,2,1,0:T(8,128)S(1)}, f32[2,2,2,32,768]{4,3,2,1,0:T(8,128)}, u32[]{:S(2)}, u32[]{:S(2)}) collective-permute-start(f32[2,2,2,32,768]{4,3,2,1,0:T(8,128)S(1)} %slice_bitcast_fusion.5), channel_id=1, source_target_pairs={{0,8},{1,9},{2,10},{3,11},{4,12},{5,13},{6,14},{7,15},{8,0},{9,1},... | collective-permute-start | bytes 2359304 | tf_op jit(solution)/shard_map/ppermute | solution.py:520
  313.6 19.3 %collective-permute-start.13 = (f32[2,2,2,32,768]{4,3,2,1,0:T(8,128)}, f32[2,2,2,32,768]{4,3,2,1,0:T(8,128)}, u32[]{:S(2)}, u32[]{:S(2)}) collective-permute-start(f32[2,2,2,32,768]{4,3,2,1,0:T(8,128)} %slice_bitcast_fusion.4), channel_id=1, source_target_pairs={{0,16},{1,17},{2,18},{3,19},{4,20},{5,21},{6,22},{7,23},{8,24},{9,... | collective-permute-start | bytes 2359304 | tf_op jit(solution)/shard_map/ppermute | solution.py:520
  335.9 9.7 %collective-permute-start.14 = (f32[2,2,32,768]{3,2,1,0:T(8,128)S(1)}, f32[2,2,32,768]{3,2,1,0:T(8,128)S(1)}, u32[]{:S(2)}, u32[]{:S(2)}) collective-permute-start(f32[2,2,32,768]{3,2,1,0:T(8,128)S(1)} %slice_bitcast_fusion.9), channel_id=1, source_target_pairs={{0,16},{1,17},{2,18},{3,19},{4,20},{5,21},{6,22},{7,23},{8,24},{9,... | collective-permute-start | bytes 1179656 | tf_op jit(solution)/shard_map/ppermute | solution.py:520
  336.6 9.4 %collective-permute-start.15 = (f32[2,2,32,768]{3,2,1,0:T(8,128)S(1)}, f32[2,2,32,768]{3,2,1,0:T(8,128)S(1)}, u32[]{:S(2)}, u32[]{:S(2)}) collective-permute-start(f32[2,2,32,768]{3,2,1,0:T(8,128)S(1)} %slice_bitcast_fusion.8), channel_id=1, source_target_pairs={{0,8},{1,9},{2,10},{3,11},{4,12},{5,13},{6,14},{7,15},{8,0},{9,1},... | collective-permute-start | bytes 1179656 | tf_op jit(solution)/shard_map/ppermute | solution.py:520
  346.1 6.4 collective-permute-start.16
  346.7 8.0 %collective-permute-start.17 = (f32[2,32,768]{2,1,0:T(8,128)S(1)}, f32[2,32,768]{2,1,0:T(8,128)S(1)}, u32[]{:S(2)}, u32[]{:S(2)}) collective-permute-start(f32[2,32,768]{2,1,0:T(8,128)S(1)} %slice_bitcast_fusion.12), channel_id=1, source_target_pairs={{0,2},{1,3},{2,0},{3,1},{4,6},{5,7},{6,4},{7,5},{8,10},{9,11},{10,... | collective-permute-start | bytes 589832 | tf_op jit(solution)/shard_map/ppermute | solution.py:520
  354.8 7.7 collective-permute-start.18
  355.4 8.1 %collective-permute-start.19 = (f32[32,768]{1,0:T(8,128)S(1)}, f32[32,768]{1,0:T(8,128)S(1)}, u32[]{:S(2)}, u32[]{:S(2)}) collective-permute-start(f32[32,768]{1,0:T(8,128)S(1)} %slice_bitcast_fusion.16), channel_id=1, source_target_pairs={{0,4},{1,5},{2,6},{3,7},{4,0},{5,1},{6,2},{7,3},{8,12},{9,13},{10,... | collective-permute-start | bytes 294920 | tf_op jit(solution)/shard_map/ppermute | solution.py:520
  388.5 318.4 %reduce-scatter.3.cloned.1.call-start = ((), (), s32[]{:S(2)}) async-start(), calls=%async_computation.10 | async-start | bytes 9732096 | tf_op jit(solution)/shard_map/reduce_scatter | solution.py:798
  443.8 21.2 %collective-permute-start.20 = (f32[384,2304]{1,0:T(8,128)}, f32[384,2304]{1,0:T(8,128)}, u32[]{:S(2)}, u32[]{:S(2)}) collective-permute-start(f32[384,2304]{1,0:T(8,128)} %fusion.64), channel_id=1, source_target_pairs={{0,1},{1,0},{2,3},{3,2},{4,5},{5,4},{6,7},{7,6},{8,9},{9,8},{10,11... | collective-permute-start | bytes 10616840 | tf_op jit(solution)/shard_map/ppermute | solution.py:548
  472.7 27.5 %collective-permute-start.21 = (f32[2,2,2,24,1152]{4,3,2,1,0:T(8,128)}, f32[2,2,2,24,1152]{4,3,2,1,0:T(8,128)S(1)}, u32[]{:S(2)}, u32[]{:S(2)}) collective-permute-start(f32[2,2,2,24,1152]{4,3,2,1,0:T(8,128)} %dynamic-slice_bitcast_fusion.1), channel_id=1, source_target_pairs={{0,8},{1,9},{2,10},{3,11},{4,12},{5,13},{6,14},{7,15},{8,0},{9,1},... | collective-permute-start | bytes 2654216 | tf_op jit(solution)/shard_map/ppermute | solution.py:520
  474.2 26.9 %collective-permute-start.22 = (f32[2,2,2,24,1152]{4,3,2,1,0:T(8,128)}, f32[2,2,2,24,1152]{4,3,2,1,0:T(8,128)}, u32[]{:S(2)}, u32[]{:S(2)}) collective-permute-start(f32[2,2,2,24,1152]{4,3,2,1,0:T(8,128)} %dynamic-slice_bitcast_fusion), channel_id=1, source_target_pairs={{0,16},{1,17},{2,18},{3,19},{4,20},{5,21},{6,22},{7,23},{8,24},{9,... | collective-permute-start | bytes 2654216 | tf_op jit(solution)/shard_map/ppermute | solution.py:520
  509.7 20.1 %collective-permute-start.23 = (f32[2,2,24,1152]{3,2,0,1:T(8,128)S(1)}, f32[2,2,24,1152]{3,2,0,1:T(8,128)S(1)}, u32[]{:S(2)}, u32[]{:S(2)}) collective-permute-start(f32[2,2,24,1152]{3,2,0,1:T(8,128)S(1)} %bitcast.305), channel_id=1, source_target_pairs={{0,16},{1,17},{2,18},{3,19},{4,20},{5,21},{6,22},{7,23},{8,24},{9,... | collective-permute-start | bytes 1327112 | tf_op jit(solution)/shard_map/ppermute | solution.py:520
  511.3 18.5 %collective-permute-start.24 = (f32[2,2,24,1152]{3,2,0,1:T(8,128)S(1)}, f32[2,2,24,1152]{3,2,0,1:T(8,128)}, u32[]{:S(2)}, u32[]{:S(2)}) collective-permute-start(f32[2,2,24,1152]{3,2,0,1:T(8,128)S(1)} %bitcast.304), channel_id=1, source_target_pairs={{0,8},{1,9},{2,10},{3,11},{4,12},{5,13},{6,14},{7,15},{8,0},{9,1},... | collective-permute-start | bytes 1327112 | tf_op jit(solution)/shard_map/ppermute | solution.py:520
  567.9 49.4 %all-to-all-start.3 = ((bf16[32,24,1024]{2,1,0:T(8,128)(2,1)}), bf16[32,24,1024]{2,1,0:T(8,128)(2,1)S(1)}, u32[]{:S(2)}, u32[]{:S(2)}) async-start(bf16[32,24,1024]{2,1,0:T(8,128)(2,1)} %bitcast.285), calls=%async_computation.3 | async-start | bytes 3145728 | tf_op jit(solution)/shard_map/all_to_all | solution.py:818
  570.8 32.5 %collective-permute-start.25 = (f32[2,24,1152]{2,1,0:T(8,128)}, f32[2,24,1152]{2,1,0:T(8,128)S(1)}, u32[]{:S(2)}, u32[]{:S(2)}) collective-permute-start(f32[2,24,1152]{2,1,0:T(8,128)} %dynamic-slice_bitcast_fusion.3), channel_id=1, source_target_pairs={{0,2},{1,3},{2,0},{3,1},{4,6},{5,7},{6,4},{7,5},{8,10},{9,11},{10,... | collective-permute-start | bytes 663560 | tf_op jit(solution)/shard_map/ppermute | solution.py:520
  572.7 44.6 %collective-permute-start.26 = (f32[2,24,1152]{2,1,0:T(8,128)S(1)}, f32[2,24,1152]{2,1,0:T(8,128)S(1)}, u32[]{:S(2)}, u32[]{:S(2)}) collective-permute-start(f32[2,24,1152]{2,1,0:T(8,128)S(1)} %dynamic-slice_bitcast_fusion.2), channel_id=1, source_target_pairs={{0,2},{1,3},{2,0},{3,1},{4,6},{5,7},{6,4},{7,5},{8,10},{9,11},{10,... | collective-permute-start | bytes 663560 | tf_op jit(solution)/shard_map/ppermute | solution.py:520
  617.4 93.8 %collective-permute-start.29 = (f32[384,3072]{1,0:T(8,128)}, f32[384,3072]{1,0:T(8,128)}, u32[]{:S(2)}, u32[]{:S(2)}) collective-permute-start(f32[384,3072]{1,0:T(8,128)} %copy-done.14), channel_id=1, source_target_pairs={{0,1},{1,0},{2,3},{3,2},{4,5},{5,4},{6,7},{7,6},{8,9},{9,8},{10,11... | collective-permute-start | bytes 14155784 | tf_op jit(solution)/shard_map/ppermute | solution.py:548
  619.2 82.7 %collective-permute-start.27 = (f32[24,1152]{1,0:T(8,128)S(1)}, f32[24,1152]{1,0:T(8,128)S(1)}, u32[]{:S(2)}, u32[]{:S(2)}) collective-permute-start(f32[24,1152]{1,0:T(8,128)S(1)} %dynamic-slice_bitcast_fusion.5), channel_id=1, source_target_pairs={{0,4},{1,5},{2,6},{3,7},{4,0},{5,1},{6,2},{7,3},{8,12},{9,13},{10,... | collective-permute-start | bytes 331784 | tf_op jit(solution)/shard_map/ppermute | solution.py:520
  619.3 82.6 %collective-permute-start.28 = (f32[24,1152]{1,0:T(8,128)S(1)}, f32[24,1152]{1,0:T(8,128)S(1)}, u32[]{:S(2)}, u32[]{:S(2)}) collective-permute-start(f32[24,1152]{1,0:T(8,128)S(1)} %dynamic-slice_bitcast_fusion.4), channel_id=1, source_target_pairs={{0,4},{1,5},{2,6},{3,7},{4,0},{5,1},{6,2},{7,3},{8,12},{9,13},{10,... | collective-permute-start | bytes 331784 | tf_op jit(solution)/shard_map/ppermute | solution.py:520
  717.5 17.1 %collective-permute-start.30 = (bf16[2,2,2,24,1536]{4,3,2,1,0:T(8,128)(2,1)S(1)}, bf16[2,2,2,24,1536]{4,3,2,1,0:T(8,128)(2,1)}, u32[]{:S(2)}, u32[]{:S(2)}) collective-permute-start(bf16[2,2,2,24,1536]{4,3,2,1,0:T(8,128)(2,1)S(1)} %fusion.70), channel_id=1, source_target_pairs={{0,8},{1,9},{2,10},{3,11},{4,12},{5,13},{6,14},{7,15},{8,0},{9,1},... | collective-permute-start | bytes 1769480 | tf_op jit(solution)/shard_map/ppermute | solution.py:520
  717.6 17.0 %collective-permute-start.31 = (bf16[2,2,2,24,1536]{4,3,1,2,0:T(8,128)(2,1)S(1)}, bf16[2,2,2,24,1536]{4,3,1,2,0:T(8,128)(2,1)}, u32[]{:S(2)}, u32[]{:S(2)}) collective-permute-start(bf16[2,2,2,24,1536]{4,3,1,2,0:T(8,128)(2,1)S(1)} %fusion.71), channel_id=1, source_target_pairs={{0,16},{1,17},{2,18},{3,19},{4,20},{5,21},{6,22},{7,23},{8,24},{9,... | collective-permute-start | bytes 1769480 | tf_op jit(solution)/shard_map/ppermute | solution.py:520
  719.8 14.0 %all-to-all-start.5 = ((f32[32,1,2]{2,1,0:T(1,128)}), f32[32,1,2]{2,1,0:T(1,128)}, u32[]{:S(2)}, u32[]{:S(2)}) async-start(f32[32,1,2]{2,1,0:T(1,128)} %broadcast_in_dim.84), calls=%async_computation.7 | async-start | bytes 32768 | tf_op jit(solution)/shard_map/all_to_all | solution.py:625
  740.0 22.3 %collective-permute-start.32 = (bf16[2,2,24,1536]{3,2,1,0:T(8,128)(2,1)}, bf16[2,2,24,1536]{3,2,1,0:T(8,128)(2,1)}, u32[]{:S(2)}, u32[]{:S(2)}) collective-permute-start(bf16[2,2,24,1536]{3,2,1,0:T(8,128)(2,1)} %fusion.77), channel_id=1, source_target_pairs={{0,16},{1,17},{2,18},{3,19},{4,20},{5,21},{6,22},{7,23},{8,24},{9,... | collective-permute-start | bytes 884744 | tf_op jit(solution)/shard_map/ppermute | solution.py:520
  740.9 21.3 %collective-permute-start.33 = (bf16[2,2,24,1536]{3,2,0,1:T(8,128)(2,1)S(1)}, bf16[2,2,24,1536]{3,2,0,1:T(8,128)(2,1)}, u32[]{:S(2)}, u32[]{:S(2)}) collective-permute-start(bf16[2,2,24,1536]{3,2,0,1:T(8,128)(2,1)S(1)} %fusion.78), channel_id=1, source_target_pairs={{0,8},{1,9},{2,10},{3,11},{4,12},{5,13},{6,14},{7,15},{8,0},{9,1},... | collective-permute-start | bytes 884744 | tf_op jit(solution)/shard_map/ppermute | solution.py:520
  765.7 8.6 %collective-permute-start.34 = (bf16[2,24,1536]{2,1,0:T(8,128)(2,1)}, bf16[2,24,1536]{2,1,0:T(8,128)(2,1)S(1)}, u32[]{:S(2)}, u32[]{:S(2)}) collective-permute-start(bf16[2,24,1536]{2,1,0:T(8,128)(2,1)} %fusion.88), channel_id=1, source_target_pairs={{0,2},{1,3},{2,0},{3,1},{4,6},{5,7},{6,4},{7,5},{8,10},{9,11},{10,... | collective-permute-start | bytes 442376 | tf_op jit(solution)/shard_map/ppermute | solution.py:520
  765.7 8.7 %collective-permute-start.35 = (bf16[2,24,1536]{2,1,0:T(8,128)(2,1)}, bf16[2,24,1536]{2,1,0:T(8,128)(2,1)}, u32[]{:S(2)}, u32[]{:S(2)}) collective-permute-start(bf16[2,24,1536]{2,1,0:T(8,128)(2,1)} %fusion.89), channel_id=1, source_target_pairs={{0,2},{1,3},{2,0},{3,1},{4,6},{5,7},{6,4},{7,5},{8,10},{9,11},{10,... | collective-permute-start | bytes 442376 | tf_op jit(solution)/shard_map/ppermute | solution.py:520
  775.4 7.5 collective-permute-start.36
  775.8 8.0 %collective-permute-start.37 = (bf16[24,1536]{1,0:T(8,128)(2,1)S(1)}, bf16[24,1536]{1,0:T(8,128)(2,1)S(1)}, u32[]{:S(2)}, u32[]{:S(2)}) collective-permute-start(bf16[24,1536]{1,0:T(8,128)(2,1)S(1)} %fusion.93), channel_id=1, source_target_pairs={{0,4},{1,5},{2,6},{3,7},{4,0},{5,1},{6,2},{7,3},{8,12},{9,13},{10,... | collective-permute-start | bytes 221192 | tf_op jit(solution)/shard_map/ppermute | solution.py:520
  (88 other events, 959.3 us)
Sparse Core Ops, SparseCore 0:
  11.5 105.7 all-gather.2
  120.9 67.2 all-gather.4
  388.6 156.1 reduce-scatter.4
  551.6 147.3 reduce-scatter.2

commit v5 on v4

--- a/solution.py
+++ b/solution.py
@@ -816,15 +816,16 @@
     sending = grad_embedded.astype(half_type).T.reshape(count, own_width, tokens)
     sending, grad_hidden_late, vector_grad = advance((sending, grad_hidden, vector_grad), live)
     returned = lax.all_to_all(sending, AXES, split_axis=0, concat_axis=0, tiled=True)
-    rot_out = jnp.dot(grad_hidden_late, basis_out, preferred_element_type=full_type).astype(half_type)
-    rot_out, vector_grad = lax.optimization_barrier((rot_out, vector_grad))
     vector_parts = lax.all_to_all(
         vector_grad.reshape(count, 1, -1), AXES, split_axis=0, concat_axis=0, tiled=True
     )
+
+    rot_out = jnp.dot(grad_hidden_late, basis_out, preferred_element_type=full_type).astype(half_type)
+    rot_out, vector_parts = lax.optimization_barrier((rot_out, vector_parts))
     scale_other, scale_own = document_squares(rot_in, rot_out, segments, total)
     scale_step = FirstStep(scale_other, scale_own, own_width, half_type)
     scale_live = [scale_step]
-    returned, vector_parts = advance((returned, vector_parts), live)
+    returned = advance(returned, live)
     returned = advance(returned, scale_live)
     own_vector = jnp.sum(vector_parts, (0, 1))
     grad_in_table, in_squares = scatter_features(returned, places, vocab)
@@ -833,9 +834,8 @@
     grads = (grad_in_table, grad_out_table, own_in, own_up, own_mix, own_vector)
     squares = jnp.sum(in_squares) + out_squares
     squares = squares + sum((jnp.sum(gradient * gradient) for gradient in grads[2:]))
-    norm_parts = jnp.stack([squares, loss_part])
-    both = jnp.sum(shared_by_all(norm_parts[None], count), (0, 1))
-    advance(norm_parts, scale_live)
+    both = jnp.sum(shared_by_all(jnp.stack([squares, loss_part])[None], count), (0, 1))
+    advance(jnp.zeros((), full_type), scale_live)
     both = advance(both, scale_live)
     grad_norm = jnp.sqrt(both[0])
     loss_value = both[1]

time: 804 us -> 782 us (0.973)
  blocking collectives: 10.5 us -> 0 us
  waiting for transfers between devices: 170 us -> 161 us
    ppermute x26, waiting for transfers between devices: 60.7 us -> 46.7 us  [send(): lax.ppermute(ready, AXES, partner_pairs(lax.axis_size(AXES), self.order.p...]
    all_to_all x1 -> x0, blocking collectives: 10.5 us -> none  [per_device(): lax.all_to_all(vector_grad.reshape(count, 1, -1), AXES, split_axis=0, con...]
    unnamed x195 -> x193, local copies, waits for them, and re-layouts: 26.5 us -> 23.9 us
  transfers between devices with their start and end apart: 47 -> 48, of which waited for: 28 -> 28; matrix products, arithmetic and copies ran while one was open for 26% -> 27% of each run, Pallas kernels for 25% -> 25%
where the time goes in v5:
time: 782 us; the launch traced here: 772 us
  Pallas kernels  194 us (25%)
  waiting for transfers between devices  161 us (21%)
  matrix products  146 us (19%)
  other arithmetic  123 us (16%)
  starting transfers between devices  68.8 us (9%)
  local copies, waits for them, and re-layouts  55.9 us (7%)
  between operations  24.3 us (3%)
    pallas_call x1, Pallas kernels, scatter_features(): pl.pallas_call(scatter_kernel, out_shape=(jax.ShapeDtypeStruct((width, vo...  79.3 us
    all_to_all x1, waiting for transfers between devices, per_device(): lax.all_to_all(columns, AXES, split_axis=0, concat_axis=0, tiled=True)  55.9 us
    ppermute x26, waiting for transfers between devices, send(): lax.ppermute(ready, AXES, partner_pairs(lax.axis_size(AXES), self.order.p...  46.7 us
    pallas_call x1, Pallas kernels, gather_features(): pl.pallas_call(gather_kernel, out_shape=jax.ShapeDtypeStruct((count, widt...  38.9 us
    pallas_call x1, Pallas kernels, attention_backward(): pl.pallas_call(backward_kernel, out_shape=jax.ShapeDtypeStruct((3, tokens...  32.9 us
    ppermute x26, starting transfers between devices, send(): lax.ppermute(ready, AXES, partner_pairs(lax.axis_size(AXES), self.order.p...  31.9 us
    sub x6, other arithmetic, adam_update(): weight - rate * (update + weight_decay * weight)  27.8 us
    dot_general x1, matrix products, per_device(): jnp.dot(grad_hidden_late, basis_out, preferred_element_type=full_type)  25.9 us
  transfers between devices with their start and end apart: 48, of which 28 were waited for; matrix products, arithmetic and copies ran while one was open for 27% of the time, Pallas kernels for 25%

profile of v5, /device:TPU:0, one launch (start us, length us, event | category | flops | bytes accessed | tf_op | source)
XLA Modules:
  0.0 772.2 jit_solution(6136175052166240656)
XLA Ops:
  16.2 38.9 %shard_map.409 = bf16[32,24,1024]{2,1,0:T(8,128)(2,1)} custom-call(s32[32,1,1024]{2,1,0:T(1,128)S(1)} %reshape_reshape.3.ids_ref, f32[24,50304]{1,0:T(8,128)S(1)} %copy-done.2), custom_call_target="tpu_custom_call" | custom-call | tf_op jit(solution)/shard_map/pallas_call | solution.py:123
  55.1 7.4 all-to-all-start
  67.3 55.9 %all-to-all-done = bf16[32,24,1024]{2,1,0:T(8,128)(2,1)} async-done(((bf16[32,24,1024]{2,1,0:T(8,128)(2,1)}), bf16[32,24,1024]{2,1,0:T(8,128)(2,1)}, u32[]{:S(2)}, u32[]{:S(2)}) %all-to-all-start) | async-done | bytes 1572896 | tf_op jit(solution)/shard_map/all_to_all | solution.py:683
  130.4 9.5 %convolution_add_fusion.query_in.key_in.value_in = f32[1024,2304]{1,0:T(8,128)} fusion(bf16[1024,768]{0,1:T(8,128)(2,1)S(1)} %get-tuple-element.297, f32[2304]{0:T(1024)S(1)} %slice.186, bf16[768,5504]{1,0:T(8,128)(2,1)} %all-gather.3.cloned.1.call-done), kind=kOutput, calls=%fused_computation.23 | convolution fusion | flops 3626237952 | bytes 14558208 | tf_op jit(solution)/shard_map/dot_general | solution.py:716
  139.9 21.2 %shard_map.410 = (bf16[1024,768]{1,0:T(8,128)(2,1)S(1)}, bf16[1024,768]{1,0:T(8,128)(2,1)S(1)}, bf16[1024,768]{1,0:T(8,128)(2,1)S(1)}, bf16[1024,768]{1,0:T(8,128)(2,1)S(1)}, f32[2,6,2,512]{3,2,1,0:T(2,128)S(1)}) custom-call(f32[1024,2304]{1,0:T(8,128)} %convolution_add_fusion.query_in.key_in.value_in, ...), custom_call_target="tpu_custom_call" | custom-call | tf_op jit(solution)/shard_map/pallas_call | solution.py:329
  165.7 10.1 %multiply_convert_fusion = (bf16[1024,3072]{1,0:T(8,128)(2,1)}, f32[1024,3072]{1,0:T(8,128)}) fusion(f32[3072]{0:T(1024)S(1)} %slice.190, bf16[1024,768]{0,1:T(8,128)(2,1)S(1)} %get-tuple-element.144, bf16[768,5504]{1,0:T(8,128)(2,1)S(1)} %bitcast.325), kind=kOutput, calls=%fused_computation.17 | convolution fusion | flops 4850712576 | bytes 25178112 | tf_op jit(solution)/shard_map/dot_general | solution.py:719
  175.9 12.3 %all-gather.5.cloned.1.call-done = bf16[3840,768]{1,0:T(8,128)(2,1)} async-done(((bf16[120,768]{1,0:T(8,128)(2,1)}), bf16[3840,768]{1,0:T(8,128)(2,1)}) %all-gather.5.cloned.1.call-update) | async-done | bytes 5898256 | tf_op jit(solution)/shard_map/all_gather | solution.py:693
  188.1 10.9 %fusion.145 = (f32[1024]{0:T(1024)S(1)}, f32[1024,768]{0,1:T(8,128)S(1)}) fusion(f32[768]{0:T(1024)S(1)} %get-tuple-element.336, bf16[3840,768]{1,0:T(8,128)(2,1)} %all-gather.5.cloned.1.call-done, bf16[1024,3072]{1,0:T(8,128)(2,1)} %get-tuple-element.354, bf16[1024,768]{1,0:T(8,128)(2,1)} %copy-done.15, bf16[32,24,1024]{2,1,0:T(8,128)(2,1)} %all-to-all-done), kind=kOutput, calls=%fused_computation.371 | convolution fusion | flops 6058671104 | bytes 18488320 | tf_op jit(solution)/shard_map/dot_general | solution.py:722
  230.4 4.5 collective-permute-done.3
  240.1 8.3 %fusion.146 = (f32[2048]{0:T(1024)S(1)}, f32[2048,1572]{0,1:T(8,128)}) fusion(bf16[2048,768]{1,0:T(8,128)(2,1)S(1)} %bitcast.294, f32[1572,768]{1,0:T(8,128)S(1)} %bitcast.285), kind=kOutput, calls=%fused_computation.372 | convolution fusion | flops 4949509120 | bytes 20860928 | tf_op jit(solution)/shard_map/rd,vd->rv/dot_general | solution.py:737
  248.5 6.8 exponential_reduce_fusion
  256.9 4.6 all-to-all-start.1
  261.6 7.2 all-to-all-done.1
  273.2 6.9 all-to-all-done.2
  281.9 7.3 fusion.3
  289.2 9.0 %fusion.55 = f32[2048,768]{1,0:T(8,128)S(1)} fusion(bf16[2048,1572]{0,1:T(8,128)(2,1)S(1)} %fusion.3, f32[1572,768]{1,0:T(8,128)} %param.35), kind=kOutput, calls=%fused_computation.99 | convolution fusion | flops 4946291712 | bytes 17559552 | tf_op jit(solution)/shard_map/dot_general | solution.py:758
  302.2 8.1 %multiply_reduce_fusion = (f32[]{:T(128)}, f32[1572,768]{1,0:T(8,128)}) fusion(bf16[2048,1572]{0,1:T(8,128)(2,1)S(1)} %fusion.3, bf16[2048,768]{1,0:T(8,128)(2,1)S(1)} %bitcast.295), kind=kOutput, calls=%fused_computation.30 | convolution fusion | flops 4947499008 | bytes 14413828 | tf_op jit(solution)/shard_map/rv,rd->vd/dot_general | solution.py:765
  314.2 5.2 convolution_convert_fusion.2.in_ref
  319.4 13.1 %collective-permute-done.12 = f32[2,2,2,32,768]{4,3,2,1,0:T(8,128)} collective-permute-done((f32[2,2,2,32,768]{4,3,2,1,0:T(8,128)S(1)}, f32[2,2,2,32,768]{4,3,2,1,0:T(8,128)}, u32[]{:S(2)}, u32[]{:S(2)}) %collective-permute-start.12) | collective-permute-done | bytes 786464 | tf_op jit(solution)/shard_map/ppermute | solution.py:520
  338.1 7.6 collective-permute-done.14
  348.3 4.4 collective-permute-done.16
  357.8 4.7 collective-permute-done.18
  366.4 3.5 copy.216
  370.0 4.0 multiply_reduce_fusion.1
  378.8 9.7 %fusion.10 = f32[3840,768]{1,0:T(8,128)} fusion(bf16[1024,768]{0,1:T(8,128)(2,1)S(1)} %convert_element_type.209, bf16[1024,3072]{1,0:T(8,128)(2,1)S(1)} %bitcast.330, bf16[1024,768]{1,0:T(8,128)(2,1)S(1)} %copy-done.16), kind=kOutput, calls=%fused_computation.25 | convolution fusion | flops 6055526400 | bytes 21233664 | tf_op jit(solution)/shard_map/sa,sb->ab/dot_general | solution.py:779
  388.6 12.7 %fusion.147 = f32[1024,3840]{1,0:T(8,128)} fusion(bf16[1024,768]{0,1:T(8,128)(2,1)} %copy-done.38, bf16[3840,768]{1,0:T(8,128)(2,1)} %all-gather.5.cloned.1.call-done), kind=kOutput, calls=%fused_computation.373 | convolution fusion | flops 6039797760 | bytes 23199744 | tf_op jit(solution)/shard_map/sb,ab->sa/dot_general | solution.py:782
  404.5 32.9 %shard_map.411 = bf16[3,1024,768]{2,1,0:T(8,128)(2,1)S(1)} custom-call(bf16[1024,768]{1,0:T(8,128)(2,1)S(1)} %copy-done.6, bf16[1024,768]{1,0:T(8,128)(2,1)S(1)} %copy-done.8, bf16[1024,768]{1,0:T(8,128)(2,1)S(1)} %copy-done.10, bf16[1024,768]{1,0:T(8,128)(2,1)S(1)} %slice.228.grad_ref, f32[3,512,128]{2,1,0:T(8,128)S(1)} %pad_maximum_fusion.7.tables_ref, ...), custom_call_target="tpu_custom_call" | custom-call | tf_op jit(solution)/shard_map/pallas_call | solution.py:382
  439.2 4.6 fusion.64
  446.0 4.1 pad_maximum_fusion.3
  450.1 5.6 fusion.62
  455.7 9.3 %fusion.9 = bf16[1024,3072]{1,0:T(8,128)(2,1)S(1)} fusion(f32[1024,3840]{1,0:T(8,128)} %fusion.147, f32[1024,3072]{1,0:T(8,128)S(1)} %bitcast.272, f32[3072]{0:T(1024)S(1)} %slice.190), kind=kLoop, calls=%fused_computation.15 | loop fusion | flops 34603008 | bytes 31469568 | tf_op jit(solution)/shard_map/convert_element_type | solution.py:793
  465.0 4.9 add.565
  476.6 6.7 fusion.18
  483.3 7.6 fusion.148
  490.9 9.3 %collective-permute-done.21 = f32[2,2,2,24,1152]{4,3,2,1,0:T(8,128)S(1)} collective-permute-done((f32[2,2,2,24,1152]{4,3,2,1,0:T(8,128)}, f32[2,2,2,24,1152]{4,3,2,1,0:T(8,128)S(1)}, u32[]{:S(2)}, u32[]{:S(2)}) %collective-permute-start.21) | collective-permute-done | bytes 884768 | tf_op jit(solution)/shard_map/ppermute | solution.py:520
  505.9 3.8 copy.220
  515.2 9.0 %fusion.127 = (f32[1024]{0:T(1024)S(1)}, f32[1024]{0:T(1024)S(1)}, f32[768]{0:T(1024)S(1)}, f32[768]{0:T(1024)S(1)}, f32[768]{0:T(1024)S(1)}, /*index=5*/f32[1024,768]{0,1:T(8,128)S(1)}) fusion(f32[1024]{0:T(1024)S(1)} %copy-done.56, f32[1024]{0:T(1024)S(1)} %copy-done.54, bf16[32,24,1024]{2,1,0:T(8,128)(2,1)} %all-to-all-done, ...), kind=kOutput, calls=%fused_computation.359 | convolution fusion | flops 3634884352 | bytes 16153600 | tf_op jit(solution)/shard_map/sb,ab->sa/dot_general | solution.py:799
  524.3 3.6 fusion.38
  529.5 3.7 all-to-all-start.4
  535.9 5.2 all-to-all-done.4
  544.0 25.9 %convolution_convert_fusion.out_ref = bf16[1024,3072]{1,0:T(8,128)(2,1)} fusion(bf16[1024,3072]{1,0:T(8,128)(2,1)} %copy-done.22, bf16[3072,3072]{1,0:T(8,128)(2,1)} %param.51), kind=kOutput, calls=%fused_computation.24 | convolution fusion | flops 19330498560 | bytes 31457280 | tf_op jit(solution)/shard_map/dot_general | solution.py:823
  569.9 21.3 %shard_map.412 = (f32[384,3072]{1,0:T(8,128)S(1)}, f32[384,3072]{1,0:T(8,128)S(1)}) custom-call(s32[2,5]{1,0:T(2,128)S(1)} %copy.225.starts_ref, f32[1]{0:T(128)} %bitcast.80.total_ref, bf16[1024,768]{1,0:T(8,128)(2,1)S(1)} %copy-done.4, bf16[1024,3072]{1,0:T(8,128)(2,1)} %convolution_convert_fusion.out_ref), custom_call_target="tpu_custom_call" | custom-call | tf_op jit(solution)/shard_map/pallas_call | solution.py:468
  601.8 79.3 %shard_map.413 = (f32[24,50304]{1,0:T(8,128)}, f32[8,128]{1,0:T(8,128)S(1)}) custom-call(s32[32,1,1024]{2,1,0:T(1,128)S(1)} %get-tuple-element.317.places_ref, s32[32,1,1024]{2,1,0:T(1,128)S(1)} %get-tuple-element.316.groups_ref, bf16[32,24,1024]{2,1,0:T(8,128)(2,1)S(1)} %all-to-all-done.3.grad_ref), custom_call_target="tpu_custom_call" | custom-call | tf_op jit(solution)/shard_map/pallas_call | solution.py:214
  681.2 4.5 add.590
  687.8 4.8 collective-permute-start.30
  709.1 6.3 all-to-all-done.5
  722.3 12.8 %add_subtract_fusion = (f32[24,50304]{1,0:T(8,128)}, f32[24,50304]{1,0:T(8,128)}, f32[24,50304]{1,0:T(8,128)}) fusion(f32[24,50304]{1,0:T(8,128)} %table_ref.1, f32[]{:T(128)} %bitcast.97, f32[]{:T(128)} %bitcast.96, f32[24,50304]{1,0:T(8,128)} %get-tuple-element.203, f32[]{:T(128)S(6)} %min.3, f32[24,50304]{1,0:T(8,128)} %param.34, f32[24,50304]{1,0:T(8,128)} %param.33), kind=kLoop, calls=%fused_computation.32 | loop fusion | flops 18109440 | bytes 33804300 | tf_op jit(solution)/shard_map/sub | solution.py:636
  747.3 6.4 multiply_subtract_fusion
  (518 shorter events, 182.3 us)
Async XLA Ops:
  7.2 119.6 %all-gather.3.cloned.1.call-start = ((), (), s32[]{:S(2)}) async-start(), calls=%async_computation.8 | async-start | bytes 8718336 | tf_op jit(solution)/shard_map/all_gather | solution.py:691
  10.8 177.3 %all-gather.5.cloned.1.call-start = ((), (), s32[]{:S(2)}) async-start(), calls=%async_computation.9 | async-start | bytes 6082560 | tf_op jit(solution)/shard_map/all_gather | solution.py:693
  55.1 68.2 %all-to-all-start = ((bf16[32,24,1024]{2,1,0:T(8,128)(2,1)}), bf16[32,24,1024]{2,1,0:T(8,128)(2,1)}, u32[]{:S(2)}, u32[]{:S(2)}) async-start(bf16[32,24,1024]{2,1,0:T(8,128)(2,1)} %shard_map.409), calls=%async_computation | async-start | bytes 3145728 | tf_op jit(solution)/shard_map/all_to_all | solution.py:683
  207.4 5.1 collective-permute-start
  209.8 6.3 collective-permute-start.5
  212.4 5.6 collective-permute-start.1
  216.1 4.7 collective-permute-start.6
  218.1 5.7 collective-permute-start.2
  220.8 7.9 %collective-permute-start.7 = (bf16[4,32,768]{2,1,0:T(8,128)(2,1)S(1)}, bf16[4,32,768]{2,1,0:T(8,128)(2,1)S(1)}, u32[]{:S(2)}, u32[]{:S(2)}) collective-permute-start(bf16[4,32,768]{2,1,0:T(8,128)(2,1)S(1)} %pad_maximum_fusion.12), channel_id=1, source_target_pairs={{0,8},{1,9},{2,10},{3,11},{4,12},{5,13},{6,14},{7,15},{8,0},{9,1},... | collective-permute-start | bytes 589832 | tf_op jit(solution)/shard_map/ppermute | solution.py:619
  223.9 10.9 %collective-permute-start.3 = (bf16[8,32,768]{2,1,0:T(8,128)(2,1)S(1)}, bf16[8,32,768]{2,1,0:T(8,128)(2,1)S(1)}, u32[]{:S(2)}, u32[]{:S(2)}) collective-permute-start(bf16[8,32,768]{2,1,0:T(8,128)(2,1)S(1)} %pad_maximum_fusion.8), channel_id=1, source_target_pairs={{0,8},{1,9},{2,10},{3,11},{4,12},{5,13},{6,14},{7,15},{8,0},{9,1},... | collective-permute-start | bytes 1179656 | tf_op jit(solution)/shard_map/ppermute | solution.py:619
  228.7 7.8 %collective-permute-start.8 = (bf16[8,32,768]{2,1,0:T(8,128)(2,1)S(1)}, bf16[8,32,768]{2,1,0:T(8,128)(2,1)S(1)}, u32[]{:S(2)}, u32[]{:S(2)}) collective-permute-start(bf16[8,32,768]{2,1,0:T(8,128)(2,1)S(1)} %pad_maximum_fusion.9), channel_id=1, source_target_pairs={{0,16},{1,17},{2,18},{3,19},{4,20},{5,21},{6,22},{7,23},{8,24},{9,... | collective-permute-start | bytes 1179656 | tf_op jit(solution)/shard_map/ppermute | solution.py:619
  234.9 2.4 collective-permute-start.4
  236.6 2.4 collective-permute-start.9
  256.9 11.9 %all-to-all-start.1 = ((f32[32,1,192]{2,1,0:T(1,128)}), f32[32,1,192]{2,1,0:T(1,128)S(1)}, u32[]{:S(2)}, u32[]{:S(2)}) async-start(f32[32,1,192]{2,1,0:T(1,128)} %reshape.550), calls=%async_computation.1 | async-start | bytes 65536 | tf_op jit(solution)/shard_map/all_to_all | solution.py:745
  270.5 9.6 %all-to-all-start.2 = ((f32[32,1,64]{2,1,0:T(1,128)}), f32[32,1,64]{2,1,0:T(1,128)S(1)}, u32[]{:S(2)}, u32[]{:S(2)}) async-start(f32[32,1,64]{2,1,0:T(1,128)} %broadcast_in_dim.45), calls=%async_computation.2 | async-start | bytes 32768 | tf_op jit(solution)/shard_map/all_to_all | solution.py:625
  273.1 424.2 %reduce-scatter.5.cloned.1.call-start = ((), (), s32[]{:S(2)}) async-start(), calls=%async_computation.11 | async-start | bytes 12165120 | tf_op jit(solution)/shard_map/reduce_scatter | solution.py:781
  298.8 11.5 %collective-permute-start.10 = (f32[2,2,2,2,32,768]{5,4,3,2,1,0:T(8,128)S(1)}, f32[2,2,2,2,32,768]{5,4,3,2,1,0:T(8,128)S(1)}, u32[]{:S(2)}, u32[]{:S(2)}) collective-permute-start(f32[2,2,2,2,32,768]{5,4,3,2,1,0:T(8,128)S(1)} %bitcast.299), channel_id=1, source_target_pairs={{0,1},{1,0},{2,3},{3,2},{4,5},{5,4},{6,7},{7,6},{8,9},{9,8},{10,11... | collective-permute-start | bytes 4718600 | tf_op jit(solution)/shard_map/ppermute | solution.py:520
  298.9 11.4 %collective-permute-start.11 = (f32[2,2,2,2,32,768]{5,4,3,2,1,0:T(8,128)S(1)}, f32[2,2,2,2,32,768]{5,4,3,2,1,0:T(8,128)S(1)}, u32[]{:S(2)}, u32[]{:S(2)}) collective-permute-start(f32[2,2,2,2,32,768]{5,4,3,2,1,0:T(8,128)S(1)} %bitcast.298), channel_id=1, source_target_pairs={{0,1},{1,0},{2,3},{3,2},{4,5},{5,4},{6,7},{7,6},{8,9},{9,8},{10,11... | collective-permute-start | bytes 4718600 | tf_op jit(solution)/shard_map/ppermute | solution.py:520
  313.0 19.4 %collective-permute-start.12 = (f32[2,2,2,32,768]{4,3,2,1,0:T(8,128)S(1)}, f32[2,2,2,32,768]{4,3,2,1,0:T(8,128)}, u32[]{:S(2)}, u32[]{:S(2)}) collective-permute-start(f32[2,2,2,32,768]{4,3,2,1,0:T(8,128)S(1)} %slice_bitcast_fusion.5), channel_id=1, source_target_pairs={{0,8},{1,9},{2,10},{3,11},{4,12},{5,13},{6,14},{7,15},{8,0},{9,1},... | collective-permute-start | bytes 2359304 | tf_op jit(solution)/shard_map/ppermute | solution.py:520
  313.6 19.3 %collective-permute-start.13 = (f32[2,2,2,32,768]{4,3,2,1,0:T(8,128)}, f32[2,2,2,32,768]{4,3,2,1,0:T(8,128)}, u32[]{:S(2)}, u32[]{:S(2)}) collective-permute-start(f32[2,2,2,32,768]{4,3,2,1,0:T(8,128)} %slice_bitcast_fusion.4), channel_id=1, source_target_pairs={{0,16},{1,17},{2,18},{3,19},{4,20},{5,21},{6,22},{7,23},{8,24},{9,... | collective-permute-start | bytes 2359304 | tf_op jit(solution)/shard_map/ppermute | solution.py:520
  336.0 9.7 %collective-permute-start.14 = (f32[2,2,32,768]{3,2,1,0:T(8,128)S(1)}, f32[2,2,32,768]{3,2,1,0:T(8,128)S(1)}, u32[]{:S(2)}, u32[]{:S(2)}) collective-permute-start(f32[2,2,32,768]{3,2,1,0:T(8,128)S(1)} %slice_bitcast_fusion.9), channel_id=1, source_target_pairs={{0,16},{1,17},{2,18},{3,19},{4,20},{5,21},{6,22},{7,23},{8,24},{9,... | collective-permute-start | bytes 1179656 | tf_op jit(solution)/shard_map/ppermute | solution.py:520
  336.6 9.4 %collective-permute-start.15 = (f32[2,2,32,768]{3,2,1,0:T(8,128)S(1)}, f32[2,2,32,768]{3,2,1,0:T(8,128)S(1)}, u32[]{:S(2)}, u32[]{:S(2)}) collective-permute-start(f32[2,2,32,768]{3,2,1,0:T(8,128)S(1)} %slice_bitcast_fusion.8), channel_id=1, source_target_pairs={{0,8},{1,9},{2,10},{3,11},{4,12},{5,13},{6,14},{7,15},{8,0},{9,1},... | collective-permute-start | bytes 1179656 | tf_op jit(solution)/shard_map/ppermute | solution.py:520
  346.2 6.4 collective-permute-start.16
  346.8 8.0 %collective-permute-start.17 = (f32[2,32,768]{2,1,0:T(8,128)S(1)}, f32[2,32,768]{2,1,0:T(8,128)S(1)}, u32[]{:S(2)}, u32[]{:S(2)}) collective-permute-start(f32[2,32,768]{2,1,0:T(8,128)S(1)} %slice_bitcast_fusion.12), channel_id=1, source_target_pairs={{0,2},{1,3},{2,0},{3,1},{4,6},{5,7},{6,4},{7,5},{8,10},{9,11},{10,... | collective-permute-start | bytes 589832 | tf_op jit(solution)/shard_map/ppermute | solution.py:520
  354.8 7.7 collective-permute-start.18
  355.5 8.1 %collective-permute-start.19 = (f32[32,768]{1,0:T(8,128)S(1)}, f32[32,768]{1,0:T(8,128)S(1)}, u32[]{:S(2)}, u32[]{:S(2)}) collective-permute-start(f32[32,768]{1,0:T(8,128)S(1)} %slice_bitcast_fusion.16), channel_id=1, source_target_pairs={{0,4},{1,5},{2,6},{3,7},{4,0},{5,1},{6,2},{7,3},{8,12},{9,13},{10,... | collective-permute-start | bytes 294920 | tf_op jit(solution)/shard_map/ppermute | solution.py:520
  443.8 21.2 %collective-permute-start.20 = (f32[384,2304]{1,0:T(8,128)}, f32[384,2304]{1,0:T(8,128)}, u32[]{:S(2)}, u32[]{:S(2)}) collective-permute-start(f32[384,2304]{1,0:T(8,128)} %fusion.64), channel_id=1, source_target_pairs={{0,1},{1,0},{2,3},{3,2},{4,5},{5,4},{6,7},{7,6},{8,9},{9,8},{10,11... | collective-permute-start | bytes 10616840 | tf_op jit(solution)/shard_map/ppermute | solution.py:548
  472.7 27.5 %collective-permute-start.21 = (f32[2,2,2,24,1152]{4,3,2,1,0:T(8,128)}, f32[2,2,2,24,1152]{4,3,2,1,0:T(8,128)S(1)}, u32[]{:S(2)}, u32[]{:S(2)}) collective-permute-start(f32[2,2,2,24,1152]{4,3,2,1,0:T(8,128)} %dynamic-slice_bitcast_fusion.1), channel_id=1, source_target_pairs={{0,8},{1,9},{2,10},{3,11},{4,12},{5,13},{6,14},{7,15},{8,0},{9,1},... | collective-permute-start | bytes 2654216 | tf_op jit(solution)/shard_map/ppermute | solution.py:520
  474.2 26.9 %collective-permute-start.22 = (f32[2,2,2,24,1152]{4,3,2,1,0:T(8,128)}, f32[2,2,2,24,1152]{4,3,2,1,0:T(8,128)}, u32[]{:S(2)}, u32[]{:S(2)}) collective-permute-start(f32[2,2,2,24,1152]{4,3,2,1,0:T(8,128)} %dynamic-slice_bitcast_fusion), channel_id=1, source_target_pairs={{0,16},{1,17},{2,18},{3,19},{4,20},{5,21},{6,22},{7,23},{8,24},{9,... | collective-permute-start | bytes 2654216 | tf_op jit(solution)/shard_map/ppermute | solution.py:520
  509.7 18.2 %collective-permute-start.23 = (f32[2,2,24,1152]{3,2,0,1:T(8,128)S(1)}, f32[2,2,24,1152]{3,2,0,1:T(8,128)S(1)}, u32[]{:S(2)}, u32[]{:S(2)}) collective-permute-start(f32[2,2,24,1152]{3,2,0,1:T(8,128)S(1)} %bitcast.301), channel_id=1, source_target_pairs={{0,16},{1,17},{2,18},{3,19},{4,20},{5,21},{6,22},{7,23},{8,24},{9,... | collective-permute-start | bytes 1327112 | tf_op jit(solution)/shard_map/ppermute | solution.py:520
  511.3 16.6 %collective-permute-start.24 = (f32[2,2,24,1152]{3,2,0,1:T(8,128)S(1)}, f32[2,2,24,1152]{3,2,0,1:T(8,128)S(1)}, u32[]{:S(2)}, u32[]{:S(2)}) collective-permute-start(f32[2,2,24,1152]{3,2,0,1:T(8,128)S(1)} %bitcast.300), channel_id=1, source_target_pairs={{0,8},{1,9},{2,10},{3,11},{4,12},{5,13},{6,14},{7,15},{8,0},{9,1},... | collective-permute-start | bytes 1327112 | tf_op jit(solution)/shard_map/ppermute | solution.py:520
  529.5 11.6 %all-to-all-start.4 = ((f32[32,1,336]{2,1,0:T(1,128)}), f32[32,1,336]{2,1,0:T(1,128)S(1)}, u32[]{:S(2)}, u32[]{:S(2)}) async-start(f32[32,1,336]{2,1,0:T(1,128)} %reshape.529), calls=%async_computation.4 | async-start | bytes 98304 | tf_op jit(solution)/shard_map/all_to_all | solution.py:819
  533.2 166.7 %reduce-scatter.3.cloned.1.call-start = ((), (), s32[]{:S(2)}) async-start(), calls=%async_computation.10 | async-start | bytes 9732096 | tf_op jit(solution)/shard_map/reduce_scatter | solution.py:798
  533.8 61.9 %collective-permute-start.25 = (f32[2,24,1152]{2,1,0:T(8,128)}, f32[2,24,1152]{2,1,0:T(8,128)S(1)}, u32[]{:S(2)}, u32[]{:S(2)}) collective-permute-start(f32[2,24,1152]{2,1,0:T(8,128)} %dynamic-slice_bitcast_fusion.3), channel_id=1, source_target_pairs={{0,2},{1,3},{2,0},{3,1},{4,6},{5,7},{6,4},{7,5},{8,10},{9,11},{10,... | collective-permute-start | bytes 663560 | tf_op jit(solution)/shard_map/ppermute | solution.py:520
  535.6 60.0 %collective-permute-start.26 = (f32[2,24,1152]{2,1,0:T(8,128)S(1)}, f32[2,24,1152]{2,1,0:T(8,128)S(1)}, u32[]{:S(2)}, u32[]{:S(2)}) collective-permute-start(f32[2,24,1152]{2,1,0:T(8,128)S(1)} %dynamic-slice_bitcast_fusion.2), channel_id=1, source_target_pairs={{0,2},{1,3},{2,0},{3,1},{4,6},{5,7},{6,4},{7,5},{8,10},{9,11},{10,... | collective-permute-start | bytes 663560 | tf_op jit(solution)/shard_map/ppermute | solution.py:520
  541.1 54.5 %all-to-all-start.3 = ((bf16[32,24,1024]{2,1,0:T(8,128)(2,1)}), bf16[32,24,1024]{2,1,0:T(8,128)(2,1)S(1)}, u32[]{:S(2)}, u32[]{:S(2)}) async-start(bf16[32,24,1024]{2,1,0:T(8,128)(2,1)} %bitcast.281), calls=%async_computation.3 | async-start | bytes 3145728 | tf_op jit(solution)/shard_map/all_to_all | solution.py:818
  596.4 84.8 %collective-permute-start.29 = (f32[384,3072]{1,0:T(8,128)}, f32[384,3072]{1,0:T(8,128)}, u32[]{:S(2)}, u32[]{:S(2)}) collective-permute-start(f32[384,3072]{1,0:T(8,128)} %copy-done.14), channel_id=1, source_target_pairs={{0,1},{1,0},{2,3},{3,2},{4,5},{5,4},{6,7},{7,6},{8,9},{9,8},{10,11... | collective-permute-start | bytes 14155784 | tf_op jit(solution)/shard_map/ppermute | solution.py:548
  598.2 82.9 %collective-permute-start.27 = (f32[24,1152]{1,0:T(8,128)S(1)}, f32[24,1152]{1,0:T(8,128)S(1)}, u32[]{:S(2)}, u32[]{:S(2)}) collective-permute-start(f32[24,1152]{1,0:T(8,128)S(1)} %dynamic-slice_bitcast_fusion.5), channel_id=1, source_target_pairs={{0,4},{1,5},{2,6},{3,7},{4,0},{5,1},{6,2},{7,3},{8,12},{9,13},{10,... | collective-permute-start | bytes 331784 | tf_op jit(solution)/shard_map/ppermute | solution.py:520
  601.1 80.0 %collective-permute-start.28 = (f32[24,1152]{1,0:T(8,128)S(1)}, f32[24,1152]{1,0:T(8,128)S(1)}, u32[]{:S(2)}, u32[]{:S(2)}) collective-permute-start(f32[24,1152]{1,0:T(8,128)S(1)} %dynamic-slice_bitcast_fusion.4), channel_id=1, source_target_pairs={{0,4},{1,5},{2,6},{3,7},{4,0},{5,1},{6,2},{7,3},{8,12},{9,13},{10,... | collective-permute-start | bytes 331784 | tf_op jit(solution)/shard_map/ppermute | solution.py:520
  687.8 27.8 %collective-permute-start.30 = (bf16[2,2,2,24,1536]{4,3,2,1,0:T(8,128)(2,1)}, bf16[2,2,2,24,1536]{4,3,2,1,0:T(8,128)(2,1)}, u32[]{:S(2)}, u32[]{:S(2)}) collective-permute-start(bf16[2,2,2,24,1536]{4,3,2,1,0:T(8,128)(2,1)} %fusion.70), channel_id=1, source_target_pairs={{0,8},{1,9},{2,10},{3,11},{4,12},{5,13},{6,14},{7,15},{8,0},{9,1},... | collective-permute-start | bytes 1769480 | tf_op jit(solution)/shard_map/ppermute | solution.py:520
  692.5 23.0 %collective-permute-start.31 = (bf16[2,2,2,24,1536]{4,3,1,2,0:T(8,128)(2,1)S(1)}, bf16[2,2,2,24,1536]{4,3,1,2,0:T(8,128)(2,1)}, u32[]{:S(2)}, u32[]{:S(2)}) collective-permute-start(bf16[2,2,2,24,1536]{4,3,1,2,0:T(8,128)(2,1)S(1)} %fusion.71), channel_id=1, source_target_pairs={{0,16},{1,17},{2,18},{3,19},{4,20},{5,21},{6,22},{7,23},{8,24},{9,... | collective-permute-start | bytes 1769480 | tf_op jit(solution)/shard_map/ppermute | solution.py:520
  704.9 10.6 %all-to-all-start.5 = ((f32[32,1,2]{2,1,0:T(1,128)}), f32[32,1,2]{2,1,0:T(1,128)S(1)}, u32[]{:S(2)}, u32[]{:S(2)}) async-start(f32[32,1,2]{2,1,0:T(1,128)} %broadcast_in_dim.84), calls=%async_computation.7 | async-start | bytes 32768 | tf_op jit(solution)/shard_map/all_to_all | solution.py:625
  720.9 20.9 %collective-permute-start.32 = (bf16[2,2,24,1536]{3,2,1,0:T(8,128)(2,1)}, bf16[2,2,24,1536]{3,2,1,0:T(8,128)(2,1)}, u32[]{:S(2)}, u32[]{:S(2)}) collective-permute-start(bf16[2,2,24,1536]{3,2,1,0:T(8,128)(2,1)} %fusion.77), channel_id=1, source_target_pairs={{0,16},{1,17},{2,18},{3,19},{4,20},{5,21},{6,22},{7,23},{8,24},{9,... | collective-permute-start | bytes 884744 | tf_op jit(solution)/shard_map/ppermute | solution.py:520
  721.5 20.2 %collective-permute-start.33 = (bf16[2,2,24,1536]{3,2,0,1:T(8,128)(2,1)S(1)}, bf16[2,2,24,1536]{3,2,0,1:T(8,128)(2,1)}, u32[]{:S(2)}, u32[]{:S(2)}) collective-permute-start(bf16[2,2,24,1536]{3,2,0,1:T(8,128)(2,1)S(1)} %fusion.78), channel_id=1, source_target_pairs={{0,8},{1,9},{2,10},{3,11},{4,12},{5,13},{6,14},{7,15},{8,0},{9,1},... | collective-permute-start | bytes 884744 | tf_op jit(solution)/shard_map/ppermute | solution.py:520
  745.2 8.6 %collective-permute-start.34 = (bf16[2,24,1536]{2,1,0:T(8,128)(2,1)}, bf16[2,24,1536]{2,1,0:T(8,128)(2,1)S(1)}, u32[]{:S(2)}, u32[]{:S(2)}) collective-permute-start(bf16[2,24,1536]{2,1,0:T(8,128)(2,1)} %fusion.88), channel_id=1, source_target_pairs={{0,2},{1,3},{2,0},{3,1},{4,6},{5,7},{6,4},{7,5},{8,10},{9,11},{10,... | collective-permute-start | bytes 442376 | tf_op jit(solution)/shard_map/ppermute | solution.py:520
  745.7 8.0 %collective-permute-start.35 = (bf16[2,24,1536]{2,1,0:T(8,128)(2,1)}, bf16[2,24,1536]{2,1,0:T(8,128)(2,1)}, u32[]{:S(2)}, u32[]{:S(2)}) collective-permute-start(bf16[2,24,1536]{2,1,0:T(8,128)(2,1)} %fusion.89), channel_id=1, source_target_pairs={{0,2},{1,3},{2,0},{3,1},{4,6},{5,7},{6,4},{7,5},{8,10},{9,11},{10,... | collective-permute-start | bytes 442376 | tf_op jit(solution)/shard_map/ppermute | solution.py:520
  754.8 7.7 %collective-permute-start.36 = (bf16[24,1536]{1,0:T(8,128)(2,1)S(1)}, bf16[24,1536]{1,0:T(8,128)(2,1)S(1)}, u32[]{:S(2)}, u32[]{:S(2)}) collective-permute-start(bf16[24,1536]{1,0:T(8,128)(2,1)S(1)} %fusion.92), channel_id=1, source_target_pairs={{0,4},{1,5},{2,6},{3,7},{4,0},{5,1},{6,2},{7,3},{8,12},{9,13},{10,... | collective-permute-start | bytes 221192 | tf_op jit(solution)/shard_map/ppermute | solution.py:520
  755.4 8.0 %collective-permute-start.37 = (bf16[24,1536]{1,0:T(8,128)(2,1)S(1)}, bf16[24,1536]{1,0:T(8,128)(2,1)S(1)}, u32[]{:S(2)}, u32[]{:S(2)}) collective-permute-start(bf16[24,1536]{1,0:T(8,128)(2,1)S(1)} %fusion.93), channel_id=1, source_target_pairs={{0,4},{1,5},{2,6},{3,7},{4,0},{5,1},{6,2},{7,3},{8,12},{9,13},{10,... | collective-permute-start | bytes 221192 | tf_op jit(solution)/shard_map/ppermute | solution.py:520
  (88 other events, 1244.1 us)
Sparse Core Ops, SparseCore 0:
  11.5 105.7 all-gather.2
  120.9 67.1 all-gather.4
  388.7 158.5 reduce-scatter.4
  554.0 145.8 reduce-scatter.2
